TPU v7x, 32 devices: a whole 2x2x4 slice. The times are simulated.
32 devices in a mesh: groups: 2 (over x), seq: 16 (over z, y, core).
Axes of the slice: x: 2, y: 2, z: 4, core: 2. Of those that a mesh axis runs over, the one named last changes fastest.
Arguments:
- features: bfloat16 [4096, 2048], P(('groups', 'seq')), parts along dimension 0, may hold values from -40 to 40
- state_write: bfloat16 [4096, 64], P(('groups', 'seq')), parts along dimension 0, may hold values from -0.75 to 0.75
- state_read: bfloat16 [4096, 64], P(('groups', 'seq')), parts along dimension 0, may hold values from -0.75 to 0.75
- log_decay: float32 [4096, 32], P(('groups', 'seq')), parts along dimension 0, may hold values from -2 to 0
- skip_gain: float32 [32], replicated, may hold values from 1 to 4
- post_gain: float32 [2048], replicated, may hold values from 0.5 to 2
- start_index: int32 [4096], P(('groups', 'seq')), parts along dimension 0, may hold values from 0 to 2047, as said below
- step_noise: bfloat16 [3, 4096, 1024], P(None, ('groups', 'seq')), parts along dimension 1, may hold values from -4 to 4
- act_weight: bfloat16 [2048, 128], replicated, may hold values from -0.125 to 0.125
- dyn_weight: bfloat16 [2048, 1024], replicated, may hold values from -0.125 to 0.125
- act_in_weight: bfloat16 [128, 1024], replicated, may hold values from -0.5 to 0.5
- out_weight: bfloat16 [1024, 2048], replicated, may hold values from -0.1875 to 0.1875
- value_weight: bfloat16 [1024], replicated, may hold values from -0.1875 to 0.1875
Outputs:
- posterior: bfloat16 [4096, 2048], P(('groups', 'seq')), parts along dimension 0
- values: float32 [3, 4096], P(None, ('groups', 'seq')), parts along dimension 1
- final_latent: bfloat16 [4096, 2048], P(('groups', 'seq')), parts along dimension 0
There are 2 independent parts, one for each index of `groups`. A program takes and returns all parts, laid end to end along the dimension named above; an argument that names none is the same for every part. Nothing has to cross between parts.
Inputs may be any that keep to these rules, and one draw needn't show every extreme that they name: `start_index`: each aligned block of 128 starts (the starts of one device) names exactly 8 time steps in every aligned range of 128 time steps.
All inputs are finite; a program needn't handle non-finite values.
Results may differ from a plain program's by a relative error of at most 0.01.
Values may be sent and summed in bfloat16 or wider, within the bound.
No kernel may reach another device: no remote copies, remote signals or barrier semaphores. Data moves between devices by JAX's collectives and lax.ppermute only.
A program may use at most 192 MiB of HBM per device.

v0:
```python
import jax
import jax.numpy as jnp
from jax import lax
from jax.sharding import PartitionSpec as P


def entering(shard, axis, combine, identity):
    count, mine = (lax.axis_size(axis), lax.axis_index(axis))
    everything = jax.tree.map(lambda part: lax.all_gather(part, axis), shard)
    start = jax.tree.map(
        lambda part, zero: jnp.broadcast_to(jnp.asarray(zero, part.dtype), part.shape),
        shard,
        identity,
    )

    def lap(k, before):
        reached = k < mine
        new = combine(before, jax.tree.map(lambda part: part[k], everything))
        return jax.tree.map(lambda a, b: jnp.where(reached, a, b), new, before)

    return lax.fori_loop(0, count, lap, start)


def lower_ones(count):
    positions = jnp.arange(count, dtype=jnp.int32)
    return (positions[:, None] >= positions[None, :]).astype(jnp.float32)


def local_pass(wide_in, write_in, read_in, decay_in):
    row_count, width = wide_in.shape
    head_count = decay_in.shape[1]
    head_width = width // head_count
    block = min(256, row_count)
    block_count = row_count // block
    positions = jnp.arange(block, dtype=jnp.int32)
    lower_mask = positions[:, None] >= positions[None, :]
    lower_table = lower_mask.astype(jnp.float32)

    def advance(state_now, inputs):
        x_block, write_block, read_block, decay_block = inputs
        running = jnp.dot(lower_table, decay_block, precision=lax.Precision.HIGHEST)
        running_t = running.T
        spread = running_t[:, :, None] - running_t[:, None, :]
        weight = jnp.exp(jnp.where(lower_mask[None], spread, -jnp.inf))
        gram = jnp.dot(read_block, write_block.T, preferred_element_type=jnp.float32)
        inner_part = jnp.einsum(
            "hts,shp->thp",
            weight * gram[None],
            x_block.reshape(block, head_count, head_width),
            precision=lax.Precision.HIGHEST,
        ).reshape(block, width)
        read_wide = read_block.astype(jnp.float32)
        carried = jnp.dot(read_wide, state_now, precision=lax.Precision.HIGHEST) * jnp.repeat(
            jnp.exp(running), head_width, axis=1
        )
        tail = jnp.repeat(jnp.exp(running[-1:] - running), head_width, axis=1)
        whole_decay = jnp.repeat(jnp.exp(running[-1]), head_width)
        added = jnp.einsum(
            "sn,sd->nd",
            write_block.astype(jnp.float32),
            x_block * tail,
            precision=lax.Precision.HIGHEST,
        )
        state_next = state_now * whole_decay[None, :] + added
        return (state_next, inner_part + carried)

    zero_state = jnp.zeros((write_in.shape[1], width), jnp.float32)
    inputs = (
        wide_in.reshape(block_count, block, width),
        write_in.reshape(block_count, block, write_in.shape[1]),
        read_in.reshape(block_count, block, read_in.shape[1]),
        decay_in.reshape(block_count, block, head_count),
    )
    end_state, outputs = lax.scan(advance, zero_state, inputs)
    return (end_state, outputs.reshape(row_count, width))


def join_states(earlier, later):
    grow = jnp.repeat(later[0], earlier[1].shape[1] // later[0].shape[0])
    return (earlier[0] * later[0], earlier[1] * grow[None, :] + later[1])


def regroup_rows(posterior, start_index):
    row_count = posterior.shape[0]
    peer_count = lax.axis_size("seq")
    start_count = start_index.shape[0]
    slot_cap = start_count // peer_count
    owners = start_index // row_count
    offset = start_index % row_count
    owner_hits = (owners[:, None] == jnp.arange(peer_count, dtype=jnp.int32)[None, :]).astype(
        jnp.float32
    )
    running_hits = jnp.dot(lower_ones(start_count), owner_hits, precision=lax.Precision.HIGHEST)
    slot_rank = jnp.sum(running_hits * owner_hits, axis=1).astype(jnp.int32) - 1
    slot_index = owners * slot_cap + slot_rank
    wanted = (
        jnp.zeros((peer_count * slot_cap,), jnp.int32)
        .at[slot_index]
        .set(offset)
        .reshape(peer_count, slot_cap)
    )
    picked = jnp.take(
        posterior, lax.all_to_all(wanted, "seq", split_axis=0, concat_axis=0, tiled=True), axis=0
    )
    landed = lax.all_to_all(picked, "seq", split_axis=0, concat_axis=0, tiled=True)
    return jnp.take(landed.reshape(peer_count * slot_cap, posterior.shape[1]), slot_index, axis=0)


def imagine(latent, step_noise, act_weight, dyn_weight, act_in_weight, out_weight, value_weight):
    value_list = []
    for step_idx in range(step_noise.shape[0]):
        wide = latent.astype(jnp.float32)
        normed = (wide * lax.rsqrt(jnp.mean(wide * wide, axis=-1, keepdims=True) + 1e-06)).astype(
            jnp.bfloat16
        )
        action = jnp.tanh(jnp.dot(normed, act_weight, preferred_element_type=jnp.float32)).astype(
            jnp.bfloat16
        )
        inner = jnp.dot(normed, dyn_weight, preferred_element_type=jnp.float32) + jnp.dot(
            action, act_in_weight, preferred_element_type=jnp.float32
        )
        hidden = (jax.nn.silu(inner) + step_noise[step_idx].astype(jnp.float32)).astype(
            jnp.bfloat16
        )
        value_list.append(jnp.dot(hidden, value_weight, preferred_element_type=jnp.float32))
        latent = (wide + jnp.dot(hidden, out_weight, preferred_element_type=jnp.float32)).astype(
            jnp.bfloat16
        )
    return (jnp.stack(value_list), latent)


def per_device(
    features,
    state_write,
    state_read,
    log_decay,
    skip_gain,
    post_gain,
    start_index,
    step_noise,
    act_weight,
    dyn_weight,
    act_in_weight,
    out_weight,
    value_weight,
):
    row_count, width = features.shape
    head_count = log_decay.shape[1]
    head_width = width // head_count
    wide_in = features.astype(jnp.float32)
    end_state, local_out = local_pass(wide_in, state_write, state_read, log_decay)
    shard_decay = jnp.exp(jnp.sum(log_decay, axis=0))
    identity = (jnp.ones((head_count,), jnp.float32), jnp.zeros_like(end_state))
    _, carry_in = entering((shard_decay, end_state), "seq", join_states, identity)
    entered = jnp.exp(jnp.dot(lower_ones(row_count), log_decay, precision=lax.Precision.HIGHEST))
    from_before = jnp.dot(
        state_read.astype(jnp.float32), carry_in, precision=lax.Precision.HIGHEST
    ) * jnp.repeat(entered, head_width, axis=1)
    mixed = local_out + from_before + jnp.repeat(skip_gain, head_width)[None, :] * wide_in
    head_table = (
        jnp.arange(width, dtype=jnp.int32)[:, None] // head_width
        == jnp.arange(head_count, dtype=jnp.int32)[None, :]
    ).astype(jnp.float32)
    square_mean = jnp.dot(mixed * mixed, head_table, precision=lax.Precision.HIGHEST) / head_width
    scale = jnp.repeat(lax.rsqrt(square_mean + 1e-05), head_width, axis=1)
    posterior = (mixed * scale * post_gain[None, :]).astype(jnp.bfloat16)
    latent = regroup_rows(posterior, start_index)
    values, final_latent = imagine(
        latent, step_noise, act_weight, dyn_weight, act_in_weight, out_weight, value_weight
    )
    return (posterior, values, final_latent)


def solution(mesh):
    placed = (
        P(("groups", "seq"), None),
        P(("groups", "seq"), None),
        P(("groups", "seq"), None),
        P(("groups", "seq"), None),
        P(),
        P(),
        P(("groups", "seq")),
        P(None, ("groups", "seq"), None),
        P(),
        P(),
        P(),
        P(),
        P(),
    )
    return jax.shard_map(
        per_device,
        mesh=mesh,
        in_specs=placed,
        out_specs=(
            P(("groups", "seq"), None),
            P(None, ("groups", "seq")),
            P(("groups", "seq"), None),
        ),
        check_vma=False,
    )
```

profile of v0, /device:TPU:0, one launch (start us, length us, event | category | flops | bytes accessed | tf_op | source)
XLA Modules:
  0.0 165.3 jit_solution(9370423981715717801)
XLA Ops:
  8.7 1.3 copy.32
  10.1 2.3 %fusion.11 = f32[64,2048]{1,0:T(8,128)} fusion(bf16[128,64]{0,1:T(8,128)(2,1)} %param.16, f32[128,2048]{0,1:T(8,128)S(1)} %bitcast.98, bf16[128,2048]{0,1:T(8,128)(2,1)S(1)} %copy.32, f32[2048]{0:T(1024)S(1)} %mul.144), kind=kOutput, calls=%fused_computation.22 | convolution fusion | flops 201981952 | bytes 2121728 | tf_op jit(solution)/shard_map/while/body/eval_jaxpr/sn,sd->nd/dot_general | solution.py:58
  14.3 7.4 %all-to-all-start = ((s32[16,1,8]{2,1,0:T(1,128)}), s32[16,1,8]{2,1,0:T(1,128)S(1)}, u32[]{:S(2)}, u32[]{:S(2)}) async-start(s32[16,1,8]{2,1,0:T(1,128)} %bitcast.12), calls=%async_computation | async-start | bytes 16384 | tf_op jit(solution)/shard_map/all_to_all | solution.py:103
  23.5 2.5 %fusion.12 = f32[32,128,64]{1,2,0:T(8,128)S(1)} fusion(bf16[128,32,64]{0,2,1:T(8,128)(2,1)S(1)} %bitcast.97, f32[128,128]{1,0:T(8,128)S(1)} %fusion.53, f32[32,128]{1,0:T(8,128)S(1)} %bitcast.101, pred[128,128]{1,0:T(8,128)(4,1)S(1)} %iota_compare_fusion.2), kind=kOutput, calls=%fused_computation.23 | convolution fusion | flops 404226048 | bytes 1671168 | tf_op jit(solution)/shard_map/while/body/eval_jaxpr/hts,shp->thp/dot_general | solution.py:46
  26.0 1.6 fusion.5
  27.7 35.1 %all-reduce = f32[512]{0:T(512)S(1)} all-reduce(f32[512]{0:T(512)S(1)} %exponential_dynamic-update-slice_fusion), channel_id=2, replica_groups=mesh['groups'=2,'seq'=16] {'seq'}, use_global_device_ids=true, to_apply=%add | all-reduce | flops 512 | bytes 4096
  63.4 26.4 %all-gather.4.cloned.1.call-done = f32[1024,2048]{1,0:T(8,128)} async-done(((f32[64,2048]{1,0:T(8,128)}), f32[1024,2048]{1,0:T(8,128)}) %all-gather.4.cloned.1.call-update) | async-done | bytes 8388624 | tf_op jit(solution)/shard_map/all_gather | solution.py:9
  89.8 26.5 %while.9 = (s32[]{:T(128)}, f32[64,2048]{1,0:T(8,128)S(1)}, s32[]{:T(128)}, f32[16,32]{1,0:T(8,128)S(1)}, f32[16,64,2048]{2,1,0:T(8,128)}, /*index=5*/s32[]{:T(128)}, s32[]{:T(128)}) while((s32[]{:T(128)}, f32[64,2048]{1,0:T(8,128)S(1)}, s32[]{:T(128)}, f32[16,32]{1,0:T(8,128)S(1)}, f32[16,64,2048]{2,1,0:T(8,128)}, ...), condition=%wide.region_2.3_spmd.clone, body=%wide.region_1.2_spmd.clone.sunk | while | flops 524292 | bytes 1606121 | solution.py:21
  89.9 1.5 fusion.87
  91.6 1.5 fusion.87
  93.2 1.5 fusion.87
  94.9 1.5 fusion.87
  96.5 1.5 fusion.87
  98.2 1.5 fusion.87
  99.9 1.5 fusion.87
  101.5 1.5 fusion.87
  103.2 1.5 fusion.87
  104.8 1.5 fusion.87
  106.5 1.5 fusion.87
  108.1 1.5 fusion.87
  109.8 1.5 fusion.87
  111.5 1.5 fusion.87
  113.1 1.5 fusion.87
  114.8 1.5 fusion.87
  116.3 2.5 %fusion.3 = f32[128,2048]{0,1:T(8,128)S(1)} fusion(f32[128,2048]{0,1:T(8,128)} %fusion.5, f32[128,2048]{0,1:T(8,128)S(1)} %bitcast.96, f32[64,2048]{1,0:T(8,128)S(1)} %get-tuple-element.124, bf16[128,64]{0,1:T(8,128)(2,1)S(1)} %copy-done.8, bf16[128,2048]{0,1:T(8,128)(2,1)S(1)} %copy.32, f32[2048]{0:T(1024)S(1)} %mul.148), kind=kOutput, calls=%fused_computation.12 | convolution fusion | flops 202637312 | bytes 4218880 | tf_op jit(solution)/shard_map/dot_general | solution.py:156
  118.8 1.3 fusion.24
  122.6 3.8 %all-to-all-start.1 = ((bf16[16,8,2048]{2,1,0:T(8,128)(2,1)}), bf16[16,8,2048]{2,1,0:T(8,128)(2,1)S(1)}, u32[]{:S(2)}, u32[]{:S(2)}) async-start(bf16[16,8,2048]{2,1,0:T(8,128)(2,1)} %bitcast_select_fusion), calls=%async_computation.1 | async-start | bytes 1048576 | tf_op jit(solution)/shard_map/all_to_all | solution.py:105
  126.4 14.0 %all-to-all-done.1 = bf16[16,8,2048]{2,1,0:T(8,128)(2,1)S(1)} async-done(((bf16[16,8,2048]{2,1,0:T(8,128)(2,1)}), bf16[16,8,2048]{2,1,0:T(8,128)(2,1)S(1)}, u32[]{:S(2)}, u32[]{:S(2)}) %all-to-all-start.1) | async-done | bytes 524320 | tf_op jit(solution)/shard_map/all_to_all | solution.py:105
  142.2 3.3 %fusion.38 = bf16[128,1024]{1,0:T(8,128)(2,1)S(1)} fusion(f32[128,1024]{1,0:T(8,128)S(1)} %fusion.22, bf16[2048,1024]{1,0:T(8,128)(2,1)} %param.24, bf16[3,128,1024]{2,1,0:T(8,128)(2,1)} %param.22, f32[128]{0:T(128)S(1)} %add_rsqrt_fusion.2, bf16[128,2048]{1,0:T(8,128)(2,1)S(1)} %gather_fusion.1, pred[128]{0:T(512)(128)(4,1)S(1)} %get-tuple-element.162), kind=kOutput, calls=%fused_computation.70 | convolution fusion | flops 538968064 | bytes 5767808 | tf_op jit(solution)/shard_map/dot_general | solution.py:119
  147.2 3.3 %fusion.37 = bf16[128,1024]{1,0:T(8,128)(2,1)S(1)} fusion(f32[128,1024]{1,0:T(8,128)S(1)} %fusion.21, bf16[2048,1024]{1,0:T(8,128)(2,1)} %param.24, bf16[3,128,1024]{2,1,0:T(8,128)(2,1)} %param.22, f32[128,2048]{1,0:T(8,128)S(1)} %get-tuple-element.169, f32[128]{0:T(128)S(1)} %add_rsqrt_fusion.1), kind=kOutput, calls=%fused_computation.68 | convolution fusion | flops 538443776 | bytes 6291968 | tf_op jit(solution)/shard_map/dot_general | solution.py:119
  152.2 3.3 %fusion.36 = bf16[128,1024]{1,0:T(8,128)(2,1)S(1)} fusion(f32[128,1024]{1,0:T(8,128)S(1)} %fusion.20, bf16[2048,1024]{1,0:T(8,128)(2,1)} %param.24, bf16[3,128,1024]{2,1,0:T(8,128)(2,1)} %param.22, f32[128,2048]{1,0:T(8,128)S(1)} %get-tuple-element.171, f32[128]{0:T(128)S(1)} %add_rsqrt_fusion), kind=kOutput, calls=%fused_computation.66 | convolution fusion | flops 538443776 | bytes 6291968 | tf_op jit(solution)/shard_map/dot_general | solution.py:119
  155.8 1.6 fusion.10
  (134 shorter events, 16.4 us)
Async XLA Ops:
  7.2 134.5 %copy-start = (bf16[2048,128]{1,0:T(8,128)(2,1)S(1)}, bf16[2048,128]{1,0:T(8,128)(2,1)}, u32[]{:S(2)}) copy-start(bf16[2048,128]{1,0:T(8,128)(2,1)} %param.23) | copy-start | bytes 1572868
  7.2 14.7 %copy-start.15 = (u32[32]{0:T(128)S(1)}, u32[32]{0:T(128)}, u32[]{:S(2)}) copy-start(u32[32]{0:T(128)} %constant.141) | copy-start | bytes 388
  7.2 14.5 %copy-start.10 = (f32[128,32]{0,1:T(8,128)S(1)}, f32[128,32]{0,1:T(8,128)}, u32[]{:S(2)}) copy-start(f32[128,32]{0,1:T(8,128)} %param.18) | copy-start | bytes 49156
  7.2 16.1 %copy-start.9 = (bf16[128,64]{0,1:T(8,128)(2,1)S(1)}, bf16[128,64]{0,1:T(8,128)(2,1)}, u32[]{:S(2)}) copy-start(bf16[128,64]{0,1:T(8,128)(2,1)} %param.16) | copy-start | bytes 49156
  7.2 5.2 %copy-start.14 = (s32[128]{0:T(128)S(1)}, s32[128]{0:T(128)}, u32[]{:S(2)}) copy-start(s32[128]{0:T(128)} %param.21) | copy-start | bytes 1540
  7.2 16.0 %copy-start.8 = (bf16[128,64]{0,1:T(8,128)(2,1)S(1)}, bf16[128,64]{0,1:T(8,128)(2,1)}, u32[]{:S(2)}) copy-start(bf16[128,64]{0,1:T(8,128)(2,1)} %param.17) | copy-start | bytes 49156
  7.2 82.5 %all-gather.4.cloned.1.call-start = ((), (), s32[]{:S(2)}) async-start(), calls=%async_computation.2 | async-start | bytes 8912896 | tf_op jit(solution)/shard_map/all_gather | solution.py:9
  12.4 50.5 %copy-start.13 = (f32[32]{0:T(128)S(1)}, f32[32]{0:T(128)}, u32[]{:S(2)}) copy-start(f32[32]{0:T(128)} %param.19) | copy-start | bytes 388
  14.3 48.7 %all-to-all-start = ((s32[16,1,8]{2,1,0:T(1,128)}), s32[16,1,8]{2,1,0:T(1,128)S(1)}, u32[]{:S(2)}, u32[]{:S(2)}) async-start(s32[16,1,8]{2,1,0:T(1,128)} %bitcast.12), calls=%async_computation | async-start | bytes 16384 | tf_op jit(solution)/shard_map/all_to_all | solution.py:103
  116.3 3.8 %copy-start.11 = (f32[2048]{0:T(1024)S(1)}, f32[2048]{0:T(1024)}, u32[]{:S(2)}) copy-start(f32[2048]{0:T(1024)} %param.20) | copy-start | bytes 24580
  120.5 5.9 %copy-start.12 = (bf16[1024]{0:T(1024)(128)(2,1)S(1)}, bf16[1024]{0:T(1024)(128)(2,1)}, u32[]{:S(2)}) copy-start(bf16[1024]{0:T(1024)(128)(2,1)} %param.27) | copy-start | bytes 6148
  120.7 20.6 %copy-start.1 = (bf16[128,2048]{1,0:T(8,128)(2,1)}, bf16[128,2048]{1,0:T(8,128)(2,1)S(1)}, u32[]{:S(2)}) copy-start(bf16[128,2048]{1,0:T(8,128)(2,1)S(1)} %copy.40) | copy-start | bytes 1572868
  121.6 20.0 %copy-start.5 = (bf16[128,1024]{1,0:T(8,128)(2,1)S(1)}, bf16[128,1024]{1,0:T(8,128)(2,1)}, u32[]{:S(2)}) copy-start(bf16[128,1024]{1,0:T(8,128)(2,1)} %param.25) | copy-start | bytes 786436
  122.6 17.8 %all-to-all-start.1 = ((bf16[16,8,2048]{2,1,0:T(8,128)(2,1)}), bf16[16,8,2048]{2,1,0:T(8,128)(2,1)S(1)}, u32[]{:S(2)}, u32[]{:S(2)}) async-start(bf16[16,8,2048]{2,1,0:T(8,128)(2,1)} %bitcast_select_fusion), calls=%async_computation.1 | async-start | bytes 1048576 | tf_op jit(solution)/shard_map/all_to_all | solution.py:105
  142.2 3.5 %copy-start.2 = (bf16[1024,2048]{1,0:T(8,128)(2,1)S(1)}, bf16[1024,2048]{1,0:T(8,128)(2,1)}, u32[]{:S(2)}) copy-start(bf16[1024,2048]{1,0:T(8,128)(2,1)} %param.26) | copy-start | bytes 12582916
  147.2 3.5 %copy-start.3 = (bf16[1024,2048]{1,0:T(8,128)(2,1)S(1)}, bf16[1024,2048]{1,0:T(8,128)(2,1)}, u32[]{:S(2)}) copy-start(bf16[1024,2048]{1,0:T(8,128)(2,1)} %param.26) | copy-start | bytes 12582916
  150.8 0.9 copy-start.6
  152.2 3.5 %copy-start.4 = (bf16[1024,2048]{1,0:T(8,128)(2,1)S(1)}, bf16[1024,2048]{1,0:T(8,128)(2,1)}, u32[]{:S(2)}) copy-start(bf16[1024,2048]{1,0:T(8,128)(2,1)} %param.26) | copy-start | bytes 12582916
  155.8 1.7 %copy-start.7 = (bf16[128,1024]{1,0:T(8,128)(2,1)S(1)}, bf16[128,1024]{1,0:T(8,128)(2,1)}, u32[]{:S(2)}) copy-start(bf16[128,1024]{1,0:T(8,128)(2,1)} %copy-done.6) | copy-start | bytes 786436
Sparse Core Ops, SparseCore 0:
  12.5 77.1 all-gather.3
where the time goes:
time: 167 us; the launch traced here: 165 us
  waiting for transfers between devices  40.4 us (24%)
  blocking collectives  35.1 us (21%)
  matrix products  27 us (16%)
  other arithmetic  26.2 us (16%)
  between operations  15.1 us (9%)
  starting transfers between devices  11.2 us (7%)
  local copies, waits for them, and re-layouts  9.99 us (6%)
    unnamed x1, blocking collectives  35.1 us
    all_gather x1, waiting for transfers between devices, entering(): everything = jax.tree.map(lambda part: lax.all_gather(part, axis), shard)  26.4 us
    select_n x16, other arithmetic, lap(): return jax.tree.map(lambda a, b: jnp.where(reached, a, b), new, before)  23.7 us
    all_to_all x1, waiting for transfers between devices, regroup_rows(): lax.all_to_all(picked, 'seq', split_axis=0, concat_axis=0, tiled=True)  14 us
    dot_general x3, matrix products, imagine(): jnp.dot(normed, dyn_weight, preferred_element_type=jnp.float32)  9.93 us
    all_to_all x1, starting transfers between devices, regroup_rows(): lax.all_to_all(wanted, 'seq', split_axis=0, concat_axis=0, tiled=True)  7.41 us
    all_to_all x1, starting transfers between devices, regroup_rows(): lax.all_to_all(picked, 'seq', split_axis=0, concat_axis=0, tiled=True)  3.75 us
    dot_general x3, matrix products, imagine(): jnp.dot(hidden, out_weight, preferred_element_type=jnp.float32)  3.44 us
  transfers between devices with their start and end apart: 3, of which 2 were waited for; matrix products, arithmetic and copies ran while one was open for 4% of the time, Pallas kernels for 0%

commit v1 on v0

v1 whole, which is shorter than its diff:
```python
import functools
import jax
import jax.numpy as jnp
from jax import lax
from jax.experimental import pallas as pl
from jax.experimental.pallas import tpu as pltpu
from jax.sharding import PartitionSpec as P

F32 = jnp.float32
BF16 = jnp.bfloat16
LANES = 128
VMEM = pl.BlockSpec(memory_space=pltpu.VMEM)
SMEM = pl.BlockSpec(memory_space=pltpu.SMEM)


def iota(shape, dim):
    return lax.broadcasted_iota(jnp.int32, shape, dim)


def two_heads(cols, pair, head_width, shape):
    first = jnp.broadcast_to(cols[:, 2 * pair : 2 * pair + 1], shape)
    second = jnp.broadcast_to(cols[:, 2 * pair + 1 : 2 * pair + 2], shape)
    return jnp.where(iota(shape, 1) < head_width, first, second)


def before_kernel(peer_count, x_ref, write_ref, decay_ref, start_ref, send_ref, run_ref, run_t_ref, perm_ref, total_ref):
    rows, width = x_ref.shape
    head_count = decay_ref.shape[1]
    head_width = width // head_count
    state_size = write_ref.shape[1]
    half = width // 2
    lower = (iota((rows, rows), 0) >= iota((rows, rows), 1)).astype(F32)
    running = jnp.dot(lower, decay_ref[...], precision=lax.Precision.HIGHEST, preferred_element_type=F32)
    run_ref[...] = running
    run_t_ref[...] = running.T
    last = running[rows - 1 : rows, :]
    total = jnp.exp(last)
    total_ref[...] = total
    tail = jnp.exp(last - running)
    write_t = write_ref[...].T
    for pair in range(head_count // 2):
        lanes = slice(pair * LANES, (pair + 1) * LANES)
        scaled = (x_ref[:, lanes].astype(F32) * two_heads(tail, pair, head_width, (rows, LANES))).astype(BF16)
        ends = jnp.dot(write_t, scaled, preferred_element_type=F32)
        side, at = divmod(pair * LANES, half)
        send_ref[side, :, at : at + LANES] = ends
    starts = start_ref.shape[1]
    cap = starts // peer_count
    index = jnp.broadcast_to(start_ref[...].astype(F32), (starts, starts))
    index_t = index.T
    owner = jnp.floor(index * (1.0 / rows))
    owner_t = jnp.floor(index_t * (1.0 / rows))
    earlier = (iota((starts, starts), 1) < iota((starts, starts), 0)) & (owner == owner_t)
    rank = jnp.sum(earlier.astype(F32), axis=1, keepdims=True)
    slot = owner_t * cap + rank
    perm = (slot == iota((starts, starts), 1).astype(F32)).astype(F32)
    perm_ref[...] = perm.astype(BF16)
    offset = index_t - owner_t * rows
    wanted = jnp.sum(perm * offset, axis=0, keepdims=True)
    high = total.astype(BF16).astype(F32)
    meta = jnp.zeros((state_size, LANES), F32)
    row_at = iota((state_size, LANES), 0)
    pad = jnp.zeros((1, LANES - head_count), F32)
    meta = jnp.where(row_at == 0, jnp.concatenate([high, pad], axis=1), meta)
    meta = jnp.where(row_at == 1, jnp.concatenate([total - high, pad], axis=1), meta)
    meta = jnp.where(row_at == 2, wanted, meta)
    send_ref[0, :, half : half + LANES] = meta
    send_ref[1, :, half : half + LANES] = meta


def local_kernel(x_ref, write_ref, read_ref, run_ref, run_t_ref, skip_ref, out_ref):
    rows, width = x_ref.shape
    head_count = run_ref.shape[1]
    head_width = width // head_count
    gram = lax.dot_general(
        read_ref[...], write_ref[...], (((1,), (1,)), ((), ())), preferred_element_type=F32
    )
    square = (rows, rows)
    mask = iota(square, 0) >= iota(square, 1)
    lane = iota((rows, LANES), 1)
    for pair in range(head_count // 2):
        lanes = slice(pair * LANES, (pair + 1) * LANES)
        weights = []
        for head in (2 * pair, 2 * pair + 1):
            spread = run_ref[:, head : head + 1] - run_t_ref[head : head + 1, :]
            weights.append((jnp.exp(jnp.where(mask, spread, -jnp.inf)) * gram).astype(BF16))
        x = x_ref[:, lanes]
        zero = jnp.zeros_like(x)
        split = jnp.concatenate([jnp.where(lane < head_width, x, zero), jnp.where(lane < head_width, zero, x)], axis=0)
        inner = jnp.dot(jnp.concatenate(weights, axis=1), split, preferred_element_type=F32)
        out_ref[:, lanes] = inner + skip_ref[:, lanes] * x.astype(F32)


def after_kernel(core_ref, local_ref, read_ref, run_ref, keep_ref, got_ref, gain_ref, pick_ref, post_ref, sent_ref):
    rows, width = local_ref.shape
    head_count = run_ref.shape[1]
    head_width = width // head_count
    half = width // 2
    entered = jnp.exp(run_ref[...])
    read = read_ref[...]
    pick = pick_ref[...]
    mine_first = core_ref[0] == 0
    square = (LANES, LANES)
    same_head = (iota(square, 0) // head_width == iota(square, 1) // head_width).astype(BF16)
    for pair in range(head_count // 2):
        lanes = slice(pair * LANES, (pair + 1) * LANES)
        side, at = divmod(pair * LANES, half)
        keep, got = keep_ref[:, at : at + LANES], got_ref[:, at : at + LANES]
        carry = jnp.where(mine_first, keep, got) if side == 0 else jnp.where(mine_first, got, keep)
        carried = jnp.dot(read, carry, preferred_element_type=F32)
        mixed = local_ref[:, lanes] + carried * two_heads(entered, pair, head_width, (rows, LANES))
        squares = mixed * mixed
        high = squares.astype(BF16)
        low = (squares - high.astype(F32)).astype(BF16)
        total = jnp.dot(high, same_head, preferred_element_type=F32) + jnp.dot(
            low, same_head, preferred_element_type=F32
        )
        scale = lax.rsqrt(total * (1.0 / head_width) + 1e-05)
        posterior = (mixed * scale * gain_ref[:, lanes]).astype(BF16)
        post_ref[:, lanes] = posterior
        sent_ref[:, lanes] = jnp.dot(pick, posterior, preferred_element_type=F32).astype(BF16)


def imagine_kernel(landed_ref, perm_ref, noise_ref, act_ref, dyn_ref, act_in_ref, out_ref, value_ref, values_ref, final_ref):
    horizon = noise_ref.shape[0]
    latent = jnp.dot(perm_ref[...], landed_ref[...], preferred_element_type=F32)
    rows = []
    for step in range(horizon):
        scale = lax.rsqrt(jnp.mean(latent * latent, axis=1, keepdims=True) + 1e-06)
        normed = (latent * scale).astype(BF16)
        action = jnp.tanh(jnp.dot(normed, act_ref[...], preferred_element_type=F32)).astype(BF16)
        inner = jnp.dot(normed, dyn_ref[...], preferred_element_type=F32) + jnp.dot(
            action, act_in_ref[...], preferred_element_type=F32
        )
        hidden = (inner / (1.0 + jnp.exp(-inner)) + noise_ref[step].astype(F32)).astype(BF16)
        value = lax.dot_general(
            value_ref[...], hidden, (((1,), (1,)), ((), ())), preferred_element_type=F32
        )
        rows.append(value[0:1, :])
        moved = latent + jnp.dot(hidden, out_ref[...], preferred_element_type=F32)
        latent = moved.astype(BF16).astype(F32)
    final_ref[...] = latent.astype(BF16)
    values_ref[...] = jnp.concatenate(rows, axis=0)


def shape_of(shape, dtype):
    return jax.ShapeDtypeStruct(shape, dtype)


def cost(flops, read):
    return pl.CostEstimate(flops=flops, bytes_accessed=read, transcendentals=0)


def per_device(
    peer_count,
    features,
    state_write,
    state_read,
    log_decay,
    skip_gain,
    post_gain,
    start_index,
    step_noise,
    act_weight,
    dyn_weight,
    act_in_weight,
    out_weight,
    value_weight,
):
    rows, width = features.shape
    head_count = log_decay.shape[1]
    head_width = width // head_count
    state_size = state_write.shape[1]
    half = width // 2
    starts = start_index.shape[0]
    cap = starts // peer_count
    mine = lax.axis_index("seq")
    core = mine % 2
    params = pltpu.CompilerParams(vmem_limit_bytes=24 << 20)

    sides, running, running_t, perm, total = pl.pallas_call(
        functools.partial(before_kernel, peer_count),
        out_shape=(
            shape_of((2, state_size, half + LANES), F32),
            shape_of((rows, head_count), F32),
            shape_of((head_count, rows), F32),
            shape_of((starts, starts), BF16),
            shape_of((1, head_count), F32),
        ),
        in_specs=[VMEM] * 4,
        out_specs=(VMEM,) * 5,
        compiler_params=params,
    )(features, state_write, log_decay, start_index.reshape(1, starts))

    def spread_heads(per_head):
        own = lax.dynamic_slice(per_head, (core * (head_count // 2),), (head_count // 2,))
        return jnp.broadcast_to(own[:, None], (head_count // 2, head_width)).reshape(1, half)

    def swap(array, bit):
        return lax.ppermute(array, "seq", [(i, i ^ (1 << bit)) for i in range(peer_count)])

    def tagged(state, decay, wanted):
        high = decay.astype(BF16).astype(F32)
        pad = LANES - head_count
        meta = jnp.concatenate(
            [jnp.pad(high[None], ((0, 0), (0, pad))), jnp.pad((decay - high)[None], ((0, 0), (0, pad))), wanted], axis=0
        )
        blocks = -(-meta.shape[0] // state_size)
        meta = jnp.pad(meta, ((0, blocks * state_size - meta.shape[0]), (0, 0)))
        meta = [meta[k * state_size : (k + 1) * state_size] for k in range(blocks)]
        return jnp.concatenate([state] + meta, axis=1).astype(BF16)

    def untagged(array, count):
        array = array.astype(F32)
        blocks = (array.shape[1] - half) // LANES
        meta = jnp.concatenate([array[:, half + k * LANES : half + (k + 1) * LANES] for k in range(blocks)], axis=0)
        return array[:, :half], meta[0, :head_count] + meta[1, :head_count], meta[2 : 2 + count]

    upper = core == 1
    got = swap(lax.dynamic_index_in_dim(sides, 1 - core, 0, False).astype(BF16), 0)
    got_state, got_decay, got_wanted = untagged(got, 1)
    own_full = lax.dynamic_index_in_dim(sides, core, 0, False)
    own_state = own_full[:, :half]
    own_wanted = own_full[2:3, half:]
    own_decay = total[0]
    first_state = jnp.where(upper, got_state, own_state)
    first_decay = jnp.where(upper, got_decay, own_decay)
    second_state = jnp.where(upper, own_state, got_state)
    second_decay = jnp.where(upper, own_decay, got_decay)
    group_state = first_state * spread_heads(second_decay) + second_state
    group_decay = first_decay * second_decay
    wanted = jnp.where(
        upper, jnp.concatenate([got_wanted, own_wanted]), jnp.concatenate([own_wanted, got_wanted])
    )
    prefix = jnp.zeros_like(group_state)
    prefix_decay = jnp.ones_like(group_decay)

    local_out = None
    bits = peer_count.bit_length() - 1
    for bit in range(1, bits):
        later = (mine >> bit) % 2 == 1
        arrived = swap(tagged(group_state, group_decay, wanted), bit)
        if bit == 1:
            local_out = pl.pallas_call(
                local_kernel,
                out_shape=shape_of((rows, width), F32),
                in_specs=[VMEM] * 6,
                out_specs=VMEM,
                compiler_params=params,
                cost_estimate=cost(4 * rows * rows * width, 2 * rows * width),
            )(
                features,
                state_write,
                state_read,
                running,
                running_t,
                jnp.broadcast_to(skip_gain[:, None], (head_count, head_width)).reshape(1, width),
            )
        new_state, new_decay, new_wanted = untagged(arrived, wanted.shape[0])
        prefix = jnp.where(later, prefix + spread_heads(prefix_decay) * new_state, prefix)
        prefix_decay = jnp.where(later, prefix_decay * new_decay, prefix_decay)
        group_state = jnp.where(
            later,
            new_state * spread_heads(group_decay) + group_state,
            group_state * spread_heads(new_decay) + new_state,
        )
        group_decay = group_decay * new_decay
        wanted = jnp.where(
            later, jnp.concatenate([new_wanted, wanted]), jnp.concatenate([wanted, new_wanted])
        )

    second_entry = prefix * spread_heads(first_decay) + first_state
    keep = jnp.where(upper, second_entry, prefix).astype(BF16)
    back = swap(jnp.where(upper, prefix, second_entry).astype(BF16), 0)

    asked = lax.dynamic_slice(wanted, (0, mine * cap), (peer_count, cap)).reshape(starts, 1)
    pick = (asked == jnp.arange(rows, dtype=jnp.int32)[None, :].astype(F32)).astype(BF16)

    posterior, picked = pl.pallas_call(
        after_kernel,
        out_shape=(shape_of((rows, width), BF16), shape_of((starts, width), BF16)),
        in_specs=[SMEM] + [VMEM] * 7,
        out_specs=(VMEM, VMEM),
        compiler_params=params,
    )(core.reshape(1), local_out, state_read, running, keep, back, post_gain[None, :], pick)

    landed = lax.all_to_all(
        picked.reshape(peer_count, cap, width), "seq", split_axis=0, concat_axis=0, tiled=True
    ).reshape(starts, width)

    horizon = step_noise.shape[0]
    values, final_latent = pl.pallas_call(
        imagine_kernel,
        out_shape=(shape_of((horizon, starts), F32), shape_of((starts, width), BF16)),
        in_specs=[VMEM] * 8,
        out_specs=(VMEM, VMEM),
        compiler_params=pltpu.CompilerParams(vmem_limit_bytes=40 << 20),
    )(
        landed,
        perm,
        step_noise,
        act_weight,
        dyn_weight,
        act_in_weight,
        out_weight,
        jnp.broadcast_to(value_weight[None, :], (16, value_weight.shape[0])),
    )
    return (posterior, values, final_latent)


def solution(mesh):
    whole = P()
    by_row = P(("groups", "seq"), None)
    placed = (
        by_row,
        by_row,
        by_row,
        by_row,
        whole,
        whole,
        P(("groups", "seq")),
        P(None, ("groups", "seq"), None),
        whole,
        whole,
        whole,
        whole,
        whole,
    )
    return jax.shard_map(
        functools.partial(per_device, mesh.shape["seq"]),
        mesh=mesh,
        in_specs=placed,
        out_specs=(by_row, P(None, ("groups", "seq")), by_row),
        check_vma=False,
    )
```

time: 167 us -> 68.4 us (0.41)
  waiting for transfers between devices: 40.4 us -> 12.7 us
  matrix products: 27 us -> 0 us
  other arithmetic: 26.2 us -> 3.8 us
  blocking collectives: 35.1 us -> 19.4 us
  Pallas kernels: 0 us -> 14.6 us
  between operations: 15.1 us -> 1.01 us
  starting transfers between devices: 11.2 us -> 8.06 us
    unnamed x1 -> x0, blocking collectives: 35.1 us -> none
    dot_general x20 -> x0, matrix products: 27 us -> none  [the longest x3 9.93 us: imagine(): jnp.dot(normed, dyn_weight, preferred_element_type=jnp.float32)]
    all_gather x1 -> x0, waiting for transfers between devices: 26.4 us -> none  [entering(): everything = jax.tree.map(lambda part: lax.all_gather(part, axis), shard)]
    select_n x20 -> x2, other arithmetic: 24.6 us -> 0.08 us  [the longest x1 0.07 us: per_device(): jnp.where(later, jnp.concatenate([new_wanted, wanted]), jnp.concatenate([...]
    all_to_all x0 -> x1, blocking collectives: none -> 19.4 us  [per_device(): lax.all_to_all(picked.reshape(peer_count, cap, width), 'seq', split_axis=...]
    pallas_call x0 -> x4, Pallas kernels: none -> 14.6 us  [the longest x1 6.96 us: per_device(): pl.pallas_call(imagine_kernel, out_shape=(shape_of((horizon, starts), F32...]
    all_to_all x2 -> x0, waiting for transfers between devices: 14 us -> none  [the longest x1 14 us: regroup_rows(): lax.all_to_all(picked, 'seq', split_axis=0, concat_axis=0, tiled=True)]
    ppermute x0 -> x5, waiting for transfers between devices: none -> 12.7 us  [swap(): lax.ppermute(array, 'seq', [(i, i ^ 1 << bit) for i in range(peer_count)])]
  transfers between devices with their start and end apart: 3 -> 5, of which waited for: 2 -> 5; matrix products, arithmetic and copies ran while one was open for 4% -> 4% of each run, Pallas kernels for 0% -> 1%
where the time goes in v1:
time: 68.4 us; the launch traced here: 68 us
  blocking collectives  19.4 us (28%)
  Pallas kernels  14.6 us (21%)
  waiting for transfers between devices  12.7 us (19%)
  local copies, waits for them, and re-layouts  8.49 us (12%)
  starting transfers between devices  8.06 us (12%)
  other arithmetic  3.8 us (6%)
  between operations  1.01 us (1%)
    all_to_all x1, blocking collectives, per_device(): lax.all_to_all(picked.reshape(peer_count, cap, width), 'seq', split_axis=...  19.4 us
    ppermute x5, waiting for transfers between devices, swap(): lax.ppermute(array, 'seq', [(i, i ^ 1 << bit) for i in range(peer_count)])  12.7 us
    ppermute x5, starting transfers between devices, swap(): lax.ppermute(array, 'seq', [(i, i ^ 1 << bit) for i in range(peer_count)])  8.06 us
    pallas_call x1, Pallas kernels, per_device(): pl.pallas_call(imagine_kernel, out_shape=(shape_of((horizon, starts), F32...  6.96 us
    unnamed x35, local copies, waits for them, and re-layouts  6.5 us
    pallas_call x1, Pallas kernels, per_device(): pl.pallas_call(after_kernel, out_shape=(shape_of((rows, width), BF16), sh...  5.68 us
    convert_element_type x1, other arithmetic, per_device(): back = swap(jnp.where(upper, prefix, second_entry).astype(BF16), 0)  1.46 us
  transfers between devices with their start and end apart: 5, of which 5 were waited for; matrix products, arithmetic and copies ran while one was open for 4% of the time, Pallas kernels for 1%

profile of v1, /device:TPU:0, one launch (start us, length us, event | category | flops | bytes accessed | tf_op | source)
XLA Modules:
  0.0 68.0 jit_solution(8978463198295377017)
XLA Ops:
  0.7 0.8 %copy.23.write_ref = bf16[128,64]{1,0:T(8,128)(2,1)S(1)} copy(bf16[128,64]{0,1:T(8,128)(2,1)} %param.14) | data formatting | bytes 32768 | tf_op args[1]
  1.5 0.8 %copy.22.decay_ref = f32[128,32]{1,0:T(8,128)S(1)} copy(f32[128,32]{0,1:T(8,128)} %param.16) | data formatting | bytes 32768 | tf_op args[3]
  2.3 1.0 %copy-done.2 = bf16[128,2048]{1,0:T(8,128)(2,1)S(1)} copy-done((bf16[128,2048]{1,0:T(8,128)(2,1)S(1)}, bf16[128,2048]{1,0:T(8,128)(2,1)}, u32[]{:S(2)}) %copy-start.2) | copy-done | bytes 524312
  3.4 0.7 copy-done.8
  4.0 1.1 %shard_map.148 = (f32[2,64,1152]{2,1,0:T(8,128)S(1)}, f32[128,32]{1,0:T(8,128)S(1)}, f32[32,128]{1,0:T(8,128)S(1)}, bf16[128,128]{1,0:T(8,128)(2,1)S(1)}, f32[1,32]{1,0:T(1,128)S(1)}) custom-call(bf16[128,2048]{1,0:T(8,128)(2,1)S(1)} %copy-done.2, bf16[128,64]{1,0:T(8,128)(2,1)S(1)} %copy.23.write_ref, f32[128,32]{1,0:T(8,128)S(1)} %copy.22.decay_ref, ...), custom_call_target="tpu_custom_call" | custom-call | tf_op jit(solution)/shard_map/pallas_call | solution.py:181
  5.2 0.6 collective-permute-start
  5.8 1.0 %collective-permute-done = bf16[64,1152]{1,0:T(8,128)(2,1)S(1)} collective-permute-done((bf16[64,1152]{1,0:T(8,128)(2,1)S(1)}, bf16[64,1152]{1,0:T(8,128)(2,1)S(1)}, u32[]{:S(2)}, u32[]{:S(2)}) %collective-permute-start) | collective-permute-done | bytes 147488 | tf_op jit(solution)/shard_map/ppermute | solution.py:200
  6.8 0.1 fusion.24
  7.1 0.3 copy-done.9
  7.5 2.9 %collective-permute-start.1 = (bf16[64,1152]{1,0:T(8,128)(2,1)S(1)}, bf16[64,1152]{1,0:T(8,128)(2,1)S(1)}, u32[]{:S(2)}, u32[]{:S(2)}) collective-permute-start(bf16[64,1152]{1,0:T(8,128)(2,1)S(1)} %fusion.4), channel_id=1, source_target_pairs={{0,2},{1,3},{2,0},{3,1},{4,6},{5,7},{6,4},{7,5},{8,10},{9,11},{10,... | collective-permute-start | bytes 442376 | tf_op jit(solution)/shard_map/ppermute | solution.py:200
  10.6 3.9 %collective-permute-done.1 = bf16[64,1152]{1,0:T(8,128)(2,1)S(1)} collective-permute-done((bf16[64,1152]{1,0:T(8,128)(2,1)S(1)}, bf16[64,1152]{1,0:T(8,128)(2,1)S(1)}, u32[]{:S(2)}, u32[]{:S(2)}) %collective-permute-start.1) | collective-permute-done | bytes 147488 | tf_op jit(solution)/shard_map/ppermute | solution.py:200
  14.6 0.1 fusion.27
  15.0 1.9 %collective-permute-start.2 = (bf16[64,1152]{1,0:T(8,128)(2,1)S(1)}, bf16[64,1152]{1,0:T(8,128)(2,1)S(1)}, u32[]{:S(2)}, u32[]{:S(2)}) collective-permute-start(bf16[64,1152]{1,0:T(8,128)(2,1)S(1)} %fusion.5), channel_id=1, source_target_pairs={{0,4},{1,5},{2,6},{3,7},{4,0},{5,1},{6,2},{7,3},{8,12},{9,13},{10,... | collective-permute-start | bytes 442376 | tf_op jit(solution)/shard_map/ppermute | solution.py:200
  17.1 3.3 %collective-permute-done.2 = bf16[64,1152]{1,0:T(8,128)(2,1)S(1)} collective-permute-done((bf16[64,1152]{1,0:T(8,128)(2,1)S(1)}, bf16[64,1152]{1,0:T(8,128)(2,1)S(1)}, u32[]{:S(2)}, u32[]{:S(2)}) %collective-permute-start.2) | collective-permute-done | bytes 147488 | tf_op jit(solution)/shard_map/ppermute | solution.py:200
  20.4 0.1 fusion.29
  20.6 0.4 copy-done.12
  21.1 0.1 select_convert_fusion.2
  21.3 0.7 fusion.6
  21.9 2.6 %collective-permute-start.3 = (bf16[64,1152]{1,0:T(8,128)(2,1)}, bf16[64,1152]{1,0:T(8,128)(2,1)S(1)}, u32[]{:S(2)}, u32[]{:S(2)}) collective-permute-start(bf16[64,1152]{1,0:T(8,128)(2,1)} %fusion.6), channel_id=1, source_target_pairs={{0,8},{1,9},{2,10},{3,11},{4,12},{5,13},{6,14},{7,15},{8,0},{9,1},... | collective-permute-start | bytes 442376 | tf_op jit(solution)/shard_map/ppermute | solution.py:200
  24.6 0.1 copy.24.read_ref
  24.8 0.1 reshape.76.skip_ref
  24.9 0.9 %shard_map.149.local_ref = f32[128,2048]{1,0:T(8,128)S(1)} custom-call(bf16[128,2048]{1,0:T(8,128)(2,1)S(1)} %copy-done.3, bf16[128,64]{1,0:T(8,128)(2,1)S(1)} %copy.23.write_ref, bf16[128,64]{1,0:T(8,128)(2,1)S(1)} %copy.24.read_ref, f32[128,32]{1,0:T(8,128)S(1)} %get-tuple-element.12.run_ref, f32[32,128]{1,0:T(8,128)S(1)} %get-tuple-element.13.run_t_ref, ...), custom_call_target="tpu_custom_call" | custom-call | flops 134217728 | bytes 524288 | tf_op jit(solution)/shard_map/pallas_call | solution.py:244
  26.3 4.3 %collective-permute-done.3 = bf16[64,1152]{1,0:T(8,128)(2,1)S(1)} collective-permute-done((bf16[64,1152]{1,0:T(8,128)(2,1)}, bf16[64,1152]{1,0:T(8,128)(2,1)S(1)}, u32[]{:S(2)}, u32[]{:S(2)}) %collective-permute-start.3) | collective-permute-done | bytes 147488 | tf_op jit(solution)/shard_map/ppermute | solution.py:200
  30.8 0.1 eq.36
  30.9 1.5 %select_convert_fusion = (bf16[64,1024]{1,0:T(8,128)(2,1)S(1)}, f32[64,1024]{1,0:T(8,128)S(1)}) fusion(f32[1024]{0:T(1024)S(1)} %mul.145, pred[]{:T(512)S(6)} %eq.32, f32[64,1152]{1,0:T(8,128)} %copy-done.11, f32[64,1152]{1,0:T(8,128)} %copy-done.9, f32[64,1152]{1,0:T(8,128)S(1)} %convert_element_type.92, f32[1024]{0:T(1024)S(1)} %mul.135, ...), kind=kLoop, calls=%fused_computation.9 | loop fusion | flops 786432 | bytes 1716228 | tf_op jit(solution)/shard_map/convert_element_type | solution.py:274
  32.4 1.1 %select_convert_fusion.1.keep_ref = bf16[64,1024]{1,0:T(8,128)(2,1)S(1)} fusion(f32[64,1024]{1,0:T(8,128)S(1)} %get-tuple-element.22, f32[1024]{0:T(1024)S(1)} %mul.145, pred[]{:T(512)S(6)} %eq.32, f32[64,1152]{1,0:T(8,128)} %copy-done.11, f32[64,1152]{1,0:T(8,128)} %copy-done.9), kind=kLoop, calls=%fused_computation.10 | loop fusion | flops 327680 | bytes 921601 | tf_op jit(solution)/shard_map/convert_element_type | solution.py:273
  33.5 0.1 compare_convert_fusion.pick_ref
  33.6 0.2 collective-permute-done.4.got_ref
  33.8 5.7 %shard_map.150 = (bf16[128,2048]{1,0:T(8,128)(2,1)}, bf16[128,2048]{1,0:T(8,128)(2,1)S(1)}) custom-call(s32[1]{0:T(128)} %bitcast.core_ref, f32[128,2048]{1,0:T(8,128)S(1)} %shard_map.149.local_ref, bf16[128,64]{1,0:T(8,128)(2,1)S(1)} %copy.24.read_ref, f32[128,32]{1,0:T(8,128)S(1)} %get-tuple-element.12.run_ref, ...), custom_call_target="tpu_custom_call" | custom-call | tf_op jit(solution)/shard_map/pallas_call | solution.py:279
  39.5 19.4 %all_to_all.5 = bf16[16,8,2048]{2,1,0:T(8,128)(2,1)S(1)} all-to-all(bf16[16,8,2048]{2,1,0:T(8,128)(2,1)S(1)} %bitcast.28), channel_id=1, replica_groups=mesh['groups'=2,'seq'=16] {'seq'}, dimensions={0} | all-to-all | bytes 1048576 | tf_op jit(solution)/shard_map/all_to_all | solution.py:287
  58.9 2.2 %copy-done.1 = bf16[1024,2048]{1,0:T(8,128)(2,1)S(1)} copy-done((bf16[1024,2048]{1,0:T(8,128)(2,1)S(1)}, bf16[1024,2048]{1,0:T(8,128)(2,1)}, u32[]{:S(2)}) %copy-start.1) | copy-done | bytes 4194328
  61.1 7.0 %shard_map.151 = (f32[3,128]{1,0:T(4,128)}, bf16[128,2048]{1,0:T(8,128)(2,1)}) custom-call(bf16[128,2048]{1,0:T(8,128)(2,1)S(1)} %bitcast.27, bf16[128,128]{1,0:T(8,128)(2,1)S(1)} %get-tuple-element.18.perm_ref, bf16[3,128,1024]{2,1,0:T(8,128)(2,1)S(1)} %copy-done.4, bf16[2048,128]{1,0:T(8,128)(2,1)S(1)} %copy-done.5, bf16[2048,1024]{1,0:T(8,128)(2,1)S(1)} %copy-done, ...), custom_call_target="tpu_custom_call" | custom-call | tf_op jit(solution)/shard_map/pallas_call | solution.py:292
  (79 shorter events, 2.1 us)
Async XLA Ops:
  0.6 24.0 %copy-start.13 = (bf16[128,64]{0,1:T(8,128)(2,1)S(1)}, bf16[128,64]{0,1:T(8,128)(2,1)}, u32[]{:S(2)}) copy-start(bf16[128,64]{0,1:T(8,128)(2,1)} %param.15) | copy-start | bytes 49156
  0.6 24.1 %copy-start.15 = (f32[32]{0:T(128)S(1)}, f32[32]{0:T(128)}, u32[]{:S(2)}) copy-start(f32[32]{0:T(128)} %param.17) | copy-start | bytes 388
  2.3 1.0 %copy-start.2 = (bf16[128,2048]{1,0:T(8,128)(2,1)S(1)}, bf16[128,2048]{1,0:T(8,128)(2,1)}, u32[]{:S(2)}) copy-start(bf16[128,2048]{1,0:T(8,128)(2,1)} %x_ref.3) | copy-start | bytes 1572868
  3.4 0.7 copy-start.8
  4.0 20.8 %copy-start.3 = (bf16[128,2048]{1,0:T(8,128)(2,1)S(1)}, bf16[128,2048]{1,0:T(8,128)(2,1)}, u32[]{:S(2)}) copy-start(bf16[128,2048]{1,0:T(8,128)(2,1)} %x_ref.3) | copy-start | bytes 1572868
  5.2 1.6 %collective-permute-start = (bf16[64,1152]{1,0:T(8,128)(2,1)S(1)}, bf16[64,1152]{1,0:T(8,128)(2,1)S(1)}, u32[]{:S(2)}, u32[]{:S(2)}) collective-permute-start(bf16[64,1152]{1,0:T(8,128)(2,1)S(1)} %fusion.3), channel_id=1, source_target_pairs={{0,1},{1,0},{2,3},{3,2},{4,5},{5,4},{6,7},{7,6},{8,9},{9,8},{10,11... | collective-permute-start | bytes 442376 | tf_op jit(solution)/shard_map/ppermute | solution.py:200
  5.7 14.9 %copy-start.11 = (f32[64,1152]{1,0:T(8,128)}, f32[64,1152]{1,0:T(8,128)S(1)}, u32[]{:S(2)}) copy-start(f32[64,1152]{1,0:T(8,128)S(1)} %dynamic-slice_bitcast_fusion) | copy-start | bytes 884740
  6.7 0.7 %copy-start.9 = (f32[64,1152]{1,0:T(8,128)}, f32[64,1152]{1,0:T(8,128)S(1)}, u32[]{:S(2)}) copy-start(f32[64,1152]{1,0:T(8,128)S(1)} %convert_element_type.83) | copy-start | bytes 884740
  7.5 26.3 %copy-start.7 = (f32[2048]{0:T(1024)S(1)}, f32[2048]{0:T(1024)}, u32[]{:S(2)}) copy-start(f32[2048]{0:T(1024)} %param.18) | copy-start | bytes 24580
  7.5 7.1 %collective-permute-start.1 = (bf16[64,1152]{1,0:T(8,128)(2,1)S(1)}, bf16[64,1152]{1,0:T(8,128)(2,1)S(1)}, u32[]{:S(2)}, u32[]{:S(2)}) collective-permute-start(bf16[64,1152]{1,0:T(8,128)(2,1)S(1)} %fusion.4), channel_id=1, source_target_pairs={{0,2},{1,3},{2,0},{3,1},{4,6},{5,7},{6,4},{7,5},{8,10},{9,11},{10,... | collective-permute-start | bytes 442376 | tf_op jit(solution)/shard_map/ppermute | solution.py:200
  14.6 6.0 %copy-start.10 = (f32[64,1152]{1,0:T(8,128)}, f32[64,1152]{1,0:T(8,128)S(1)}, u32[]{:S(2)}) copy-start(f32[64,1152]{1,0:T(8,128)S(1)} %convert_element_type.86) | copy-start | bytes 884740
  15.0 5.4 %collective-permute-start.2 = (bf16[64,1152]{1,0:T(8,128)(2,1)S(1)}, bf16[64,1152]{1,0:T(8,128)(2,1)S(1)}, u32[]{:S(2)}, u32[]{:S(2)}) collective-permute-start(bf16[64,1152]{1,0:T(8,128)(2,1)S(1)} %fusion.5), channel_id=1, source_target_pairs={{0,4},{1,5},{2,6},{3,7},{4,0},{5,1},{6,2},{7,3},{8,12},{9,13},{10,... | collective-permute-start | bytes 442376 | tf_op jit(solution)/shard_map/ppermute | solution.py:200
  20.4 0.7 %copy-start.12 = (f32[64,1152]{1,0:T(8,128)}, f32[64,1152]{1,0:T(8,128)S(1)}, u32[]{:S(2)}) copy-start(f32[64,1152]{1,0:T(8,128)S(1)} %convert_element_type.89) | copy-start | bytes 884740
  21.1 37.7 %copy-start.14 = (bf16[1024]{0:T(1024)(128)(2,1)S(1)}, bf16[1024]{0:T(1024)(128)(2,1)}, u32[]{:S(2)}) copy-start(bf16[1024]{0:T(1024)(128)(2,1)} %param.25) | copy-start | bytes 6148
  21.2 37.6 %copy-start.4 = (bf16[3,128,1024]{2,1,0:T(8,128)(2,1)S(1)}, bf16[3,128,1024]{2,1,0:T(8,128)(2,1)}, u32[]{:S(2)}) copy-start(bf16[3,128,1024]{2,1,0:T(8,128)(2,1)} %noise_ref.1) | copy-start | bytes 2359300
  21.2 37.6 %copy-start.5 = (bf16[2048,128]{1,0:T(8,128)(2,1)S(1)}, bf16[2048,128]{1,0:T(8,128)(2,1)}, u32[]{:S(2)}) copy-start(bf16[2048,128]{1,0:T(8,128)(2,1)} %act_ref.1) | copy-start | bytes 1572868
  21.2 37.6 %copy-start.6 = (bf16[128,1024]{1,0:T(8,128)(2,1)S(1)}, bf16[128,1024]{1,0:T(8,128)(2,1)}, u32[]{:S(2)}) copy-start(bf16[128,1024]{1,0:T(8,128)(2,1)} %act_in_ref.1) | copy-start | bytes 786436
  21.9 8.7 %collective-permute-start.3 = (bf16[64,1152]{1,0:T(8,128)(2,1)}, bf16[64,1152]{1,0:T(8,128)(2,1)S(1)}, u32[]{:S(2)}, u32[]{:S(2)}) collective-permute-start(bf16[64,1152]{1,0:T(8,128)(2,1)} %fusion.6), channel_id=1, source_target_pairs={{0,8},{1,9},{2,10},{3,11},{4,12},{5,13},{6,14},{7,15},{8,0},{9,1},... | collective-permute-start | bytes 442376 | tf_op jit(solution)/shard_map/ppermute | solution.py:200
  30.9 28.0 %copy-start = (bf16[2048,1024]{1,0:T(8,128)(2,1)S(1)}, bf16[2048,1024]{1,0:T(8,128)(2,1)}, u32[]{:S(2)}) copy-start(bf16[2048,1024]{1,0:T(8,128)(2,1)} %dyn_ref.1) | copy-start | bytes 12582916
  32.4 1.4 %collective-permute-start.4 = (bf16[64,1024]{1,0:T(8,128)(2,1)S(1)}, bf16[64,1024]{1,0:T(8,128)(2,1)S(1)}, u32[]{:S(2)}, u32[]{:S(2)}) collective-permute-start(bf16[64,1024]{1,0:T(8,128)(2,1)S(1)} %get-tuple-element.21), channel_id=1, source_target_pairs={{0,1},{1,0},{2,3},{3,2},{4,5},{5,4},{6,7},{7,6},{8,9},{9,8},{10,11... | collective-permute-start | bytes 393224 | tf_op jit(solution)/shard_map/ppermute | solution.py:200
  58.9 2.2 %copy-start.1 = (bf16[1024,2048]{1,0:T(8,128)(2,1)S(1)}, bf16[1024,2048]{1,0:T(8,128)(2,1)}, u32[]{:S(2)}) copy-start(bf16[1024,2048]{1,0:T(8,128)(2,1)} %out_ref.1) | copy-start | bytes 12582916

commit v2 on v1

v2 whole, which is shorter than its diff:
```python
import functools
import jax
import jax.numpy as jnp
from jax import lax
from jax.experimental import pallas as pl
from jax.experimental.pallas import tpu as pltpu
from jax.sharding import PartitionSpec as P

F32 = jnp.float32
BF16 = jnp.bfloat16
LANES = 128
VMEM = pl.BlockSpec(memory_space=pltpu.VMEM)
SMEM = pl.BlockSpec(memory_space=pltpu.SMEM)


def iota(shape, dim):
    return lax.broadcasted_iota(jnp.int32, shape, dim)


def two_heads(cols, pair, head_width, shape):
    first = jnp.broadcast_to(cols[:, 2 * pair : 2 * pair + 1], shape)
    second = jnp.broadcast_to(cols[:, 2 * pair + 1 : 2 * pair + 2], shape)
    return jnp.where(iota(shape, 1) < head_width, first, second)


def before_kernel(peer_count, mine_ref, x_hbm, write_hbm, decay_hbm, start_hbm, own_ref, send_ref, run_ref, run_t_ref, perm_ref, aux_ref, expand_ref, x_ref, write_ref, decay_ref, start_ref, sems):
    copies = [
        pltpu.make_async_copy(source, target, sems.at[k])
        for k, (source, target) in enumerate(
            ((decay_hbm, decay_ref), (start_hbm, start_ref), (write_hbm, write_ref), (x_hbm, x_ref))
        )
    ]
    for copy in copies:
        copy.start()
    rows, width = x_ref.shape
    head_count = decay_ref.shape[0]
    head_width = width // head_count
    state_size = write_ref.shape[0]
    half = width // 2
    mine = mine_ref[0]
    core = mine % 2
    expand_shape = (LANES, half)
    expand_ref[...] = (
        iota(expand_shape, 0) == iota(expand_shape, 1) // head_width + core * (head_count // 2)
    ).astype(F32).astype(BF16)
    upper = (iota((rows, rows), 0) <= iota((rows, rows), 1)).astype(F32)
    copies[0].wait()
    running_t = jnp.dot(decay_ref[...], upper, precision=lax.Precision.HIGHEST, preferred_element_type=F32)
    running = running_t.T
    run_ref[...] = running
    run_t_ref[...] = running_t
    last = running[rows - 1 : rows, :]
    total = jnp.exp(last)
    tail = jnp.exp(last - running)
    copies[1].wait()
    starts = start_ref.shape[1]
    cap = starts // peer_count
    index = jnp.broadcast_to(start_ref[...].astype(F32), (starts, starts))
    index_t = index.T
    owner = jnp.floor(index * (1.0 / rows))
    owner_t = jnp.floor(index_t * (1.0 / rows))
    earlier = (iota((starts, starts), 1) < iota((starts, starts), 0)) & (owner == owner_t)
    rank = jnp.sum(earlier.astype(F32), axis=1, keepdims=True)
    slot = owner_t * cap + rank
    perm = (slot == iota((starts, starts), 1).astype(F32)).astype(F32)
    perm_ref[...] = perm.astype(BF16)
    offset = index_t - owner_t * rows
    wanted = jnp.sum(perm * offset, axis=0, keepdims=True)
    total = jnp.concatenate([total, jnp.zeros((1, LANES - head_count), F32)], axis=1)
    aux_ref[...] = stack_rows([total, wanted], aux_ref.shape[0])
    write_meta(send_ref, total, wanted, half, state_size)
    copies[2].wait()
    write_t = write_ref[...]
    copies[3].wait()
    pairs = head_count // 2
    for pair in range(pairs // 2):
        ends = []
        for at in (pair, pair + pairs // 2):
            lanes = slice(at * LANES, (at + 1) * LANES)
            scaled = x_ref[:, lanes].astype(F32) * two_heads(tail, at, head_width, (rows, LANES))
            ends.append(jnp.dot(write_t, scaled.astype(BF16), preferred_element_type=F32))
        lanes = slice(pair * LANES, (pair + 1) * LANES)
        own_ref[:, lanes] = jnp.where(core == 0, ends[0], ends[1])
        send_ref[:, lanes] = jnp.where(core == 0, ends[1], ends[0]).astype(BF16)


def stack_rows(rows, count):
    used = sum(row.shape[0] for row in rows)
    if used < count:
        rows = list(rows) + [jnp.zeros((count - used, LANES), F32)]
    return jnp.concatenate(rows, axis=0)


def write_meta(send_ref, decay, wanted, half, state_size):
    high = decay.astype(BF16).astype(F32)
    blocks = (send_ref.shape[1] - half) // LANES
    meta = stack_rows([high, decay - high, wanted], blocks * state_size).astype(BF16)
    for block in range(blocks):
        send_ref[:, half + block * LANES : half + (block + 1) * LANES] = meta[
            block * state_size : (block + 1) * state_size
        ]


def read_meta(got_ref, count, half, state_size):
    blocks = (got_ref.shape[1] - half) // LANES
    meta = jnp.concatenate(
        [got_ref[:, half + block * LANES : half + (block + 1) * LANES].astype(F32) for block in range(blocks)], axis=0
    )
    return meta[0:1] + meta[1:2], meta[2 : 2 + count]


def spread_rows(rows, expand_ref):
    pieces = []
    for row in rows:
        high = row.astype(BF16).astype(F32)
        pieces += [high, row - high]
    table = stack_rows(pieces, 16).astype(BF16)
    wide = jnp.dot(table, expand_ref[...], preferred_element_type=F32)
    return [wide[2 * k : 2 * k + 1] + wide[2 * k + 1 : 2 * k + 2] for k in range(len(rows))]


def pair_kernel(mine_ref, own_ref, got_ref, aux_ref, expand_ref, first_ref, group_ref, send_ref, aux_out_ref):
    state_size, half = own_ref.shape
    upper = mine_ref[0] % 2 == 1
    new_decay, new_wanted = read_meta(got_ref, 1, half, state_size)
    decay, wanted = aux_ref[0:1], aux_ref[1:2]
    first_decay = jnp.where(upper, new_decay, decay)
    second_decay = jnp.where(upper, decay, new_decay)
    (factor,) = spread_rows([second_decay], expand_ref)
    own, got = own_ref[...], got_ref[:, :half].astype(F32)
    first = jnp.where(upper, got, own)
    group = first * factor + jnp.where(upper, own, got)
    first_ref[...] = first
    group_ref[...] = group
    send_ref[:, :half] = group.astype(BF16)
    group_decay = first_decay * second_decay
    wanted = jnp.concatenate(
        [jnp.where(upper, new_wanted, wanted), jnp.where(upper, wanted, new_wanted)], axis=0
    )
    write_meta(send_ref, group_decay, wanted, half, state_size)
    aux_out_ref[...] = stack_rows(
        [group_decay, jnp.ones((1, LANES), F32), first_decay, wanted], aux_out_ref.shape[0]
    )


def stage_kernel(bit, mine_ref, group_ref, prefix_ref, aux_ref, got_ref, expand_ref, group_out, prefix_out, send_ref, aux_out):
    state_size, half = group_ref.shape
    count = 1 << bit
    later = (mine_ref[0] >> bit) % 2 == 1
    new_decay, new_wanted = read_meta(got_ref, count, half, state_size)
    decay, prefix_decay, first_decay = aux_ref[0:1], aux_ref[1:2], aux_ref[2:3]
    wanted = aux_ref[3 : 3 + count]
    into, across = spread_rows([prefix_decay, jnp.where(later, decay, new_decay)], expand_ref)
    group, got = group_ref[...], got_ref[:, :half].astype(F32)
    moved = into * got
    if prefix_ref is not None:
        moved = prefix_ref[...] + moved
        prefix_out[...] = jnp.where(later, moved, prefix_ref[...])
    else:
        prefix_out[...] = jnp.where(later, moved, jnp.zeros_like(moved))
    total = jnp.where(later, got, group) * across + jnp.where(later, group, got)
    group_out[...] = total
    send_ref[:, :half] = total.astype(BF16)
    wanted = jnp.concatenate(
        [jnp.where(later, new_wanted, wanted), jnp.where(later, wanted, new_wanted)], axis=0
    )
    write_meta(send_ref, decay * new_decay, wanted, half, state_size)
    aux_out[...] = stack_rows(
        [decay * new_decay, jnp.where(later, prefix_decay * new_decay, prefix_decay), first_decay, wanted],
        aux_out.shape[0],
    )


def first_stage_kernel(bit, mine_ref, group_ref, aux_ref, got_ref, expand_ref, *outs):
    stage_kernel(bit, mine_ref, group_ref, None, aux_ref, got_ref, expand_ref, *outs)


def last_stage_kernel(bit, rows, mine_ref, prefix_ref, aux_ref, got_ref, expand_ref, first_ref, keep_ref, back_ref, pick_ref):
    state_size, half = first_ref.shape
    count = 1 << bit
    mine = mine_ref[0]
    later = (mine >> bit) % 2 == 1
    upper = mine % 2 == 1
    _, new_wanted = read_meta(got_ref, count, half, state_size)
    into, across = spread_rows([aux_ref[1:2], aux_ref[2:3]], expand_ref)
    prefix = prefix_ref[...]
    prefix = jnp.where(later, prefix + into * got_ref[:, :half].astype(F32), prefix)
    entry = prefix * across + first_ref[...]
    keep_ref[...] = jnp.where(upper, entry, prefix).astype(BF16)
    back_ref[...] = jnp.where(upper, prefix, entry).astype(BF16)
    wanted = aux_ref[3 : 3 + count]
    wanted = jnp.concatenate(
        [jnp.where(later, new_wanted, wanted), jnp.where(later, wanted, new_wanted)], axis=0
    )
    peers = 2 * count
    starts = pick_ref.shape[0]
    cap = starts // peers
    table = jnp.concatenate([wanted, jnp.zeros((LANES - peers, LANES), F32)], axis=0) if peers < LANES else wanted
    asker = (iota((starts, LANES), 0) // cap == iota((starts, LANES), 1)).astype(F32).astype(BF16)
    by_slot = jnp.dot(asker, table.astype(BF16), preferred_element_type=F32)
    here = iota((starts, LANES), 1) == mine * cap + iota((starts, LANES), 0) % cap
    asked = jnp.sum(jnp.where(here, by_slot, 0.0), axis=1, keepdims=True)
    pick_ref[...] = (asked == iota((starts, rows), 1).astype(F32)).astype(F32).astype(BF16)


def local_kernel(x_ref, write_ref, read_ref, run_ref, run_t_ref, skip_ref, out_ref):
    rows, width = x_ref.shape
    head_count = run_ref.shape[1]
    head_width = width // head_count
    gram = jnp.dot(read_ref[...].T, write_ref[...], preferred_element_type=F32)
    square = (rows, rows)
    mask = iota(square, 0) >= iota(square, 1)
    lane = iota((rows, LANES), 1)
    for pair in range(head_count // 2):
        lanes = slice(pair * LANES, (pair + 1) * LANES)
        weights = []
        for head in (2 * pair, 2 * pair + 1):
            spread = run_ref[:, head : head + 1] - run_t_ref[head : head + 1, :]
            weights.append((jnp.exp(jnp.where(mask, spread, -jnp.inf)) * gram).astype(BF16))
        x = x_ref[:, lanes]
        zero = jnp.zeros_like(x)
        split = jnp.concatenate([jnp.where(lane < head_width, x, zero), jnp.where(lane < head_width, zero, x)], axis=0)
        inner = jnp.dot(jnp.concatenate(weights, axis=1), split, preferred_element_type=F32)
        out_ref[:, lanes] = inner + skip_ref[:, lanes] * x.astype(F32)


def after_kernel(mine_ref, local_ref, read_ref, run_ref, keep_ref, got_ref, gain_ref, pick_ref, post_ref, sent_ref, mixed_ref, total_ref):
    rows, width = local_ref.shape
    head_count = run_ref.shape[1]
    head_width = width // head_count
    half = width // 2
    entered = jnp.exp(run_ref[...])
    read = read_ref[...].T
    mine_first = mine_ref[0] % 2 == 0
    square = (LANES, LANES)
    same_head = (iota(square, 0) // head_width == iota(square, 1) // head_width).astype(F32).astype(BF16)
    blocks = [slice(k * LANES, (k + 1) * LANES) for k in range(width // LANES)]
    keep, got = keep_ref[...], got_ref[...]
    for side in range(2):
        carry = jnp.where(mine_first, keep, got) if side == 0 else jnp.where(mine_first, got, keep)
        total_ref[:, side * half : (side + 1) * half] = jnp.dot(read, carry, preferred_element_type=F32)
    for pair, lanes in enumerate(blocks):
        mixed_ref[:, lanes] = local_ref[:, lanes] + total_ref[:, lanes] * two_heads(
            entered, pair, head_width, (rows, LANES)
        )
    for lanes in blocks:
        mixed = mixed_ref[:, lanes]
        squares = mixed * mixed
        high = squares.astype(BF16)
        low = (squares - high.astype(F32)).astype(BF16)
        total_ref[:, lanes] = jnp.dot(high, same_head, preferred_element_type=F32) + jnp.dot(
            low, same_head, preferred_element_type=F32
        )
    for lanes in blocks:
        scale = lax.rsqrt(total_ref[:, lanes] * (1.0 / head_width) + 1e-05)
        post_ref[:, lanes] = (mixed_ref[:, lanes] * scale * gain_ref[:, lanes]).astype(BF16)
    sent_ref[...] = jnp.dot(pick_ref[...], post_ref[...], preferred_element_type=F32).astype(BF16)


def flush_kernel(from_ref, to_ref):
    to_ref[...] = from_ref[...]


def imagine_kernel(landed_ref, perm_ref, noise_ref, act_ref, dyn_ref, act_in_ref, out_ref, value_ref, values_ref, final_ref):
    horizon = noise_ref.shape[0]
    latent = jnp.dot(perm_ref[...], landed_ref[...], preferred_element_type=F32)
    rows = []
    for step in range(horizon):
        scale = lax.rsqrt(jnp.mean(latent * latent, axis=1, keepdims=True) + 1e-06)
        normed = (latent * scale).astype(BF16)
        action = jnp.tanh(jnp.dot(normed, act_ref[...], preferred_element_type=F32)).astype(BF16)
        inner = jnp.dot(normed, dyn_ref[...], preferred_element_type=F32) + jnp.dot(
            action, act_in_ref[...], preferred_element_type=F32
        )
        hidden = (inner / (1.0 + jnp.exp(-inner)) + noise_ref[step].astype(F32)).astype(BF16)
        value = lax.dot_general(
            value_ref[...], hidden, (((1,), (1,)), ((), ())), preferred_element_type=F32
        )
        rows.append(value[0:1, :])
        moved = latent + jnp.dot(hidden, out_ref[...], preferred_element_type=F32)
        latent = moved.astype(BF16).astype(F32)
    final_ref[...] = latent.astype(BF16)
    values_ref[...] = jnp.concatenate(rows, axis=0)


def shape_of(shape, dtype):
    return jax.ShapeDtypeStruct(shape, dtype)


def cost(flops, read):
    return pl.CostEstimate(flops=flops, bytes_accessed=read, transcendentals=0)


def per_device(
    peer_count,
    features,
    state_write,
    state_read,
    log_decay,
    skip_gain,
    post_gain,
    start_index,
    step_noise,
    act_weight,
    dyn_weight,
    act_in_weight,
    out_weight,
    value_weight,
):
    rows, width = features.shape
    head_count = log_decay.shape[1]
    head_width = width // head_count
    state_size = state_write.shape[1]
    half = width // 2
    starts = start_index.shape[0]
    cap = starts // peer_count
    mine = lax.axis_index("seq").reshape(1)
    params = pltpu.CompilerParams(vmem_limit_bytes=12 << 20)
    hbm = pl.BlockSpec(memory_space=pltpu.HBM)
    read_t = state_read.T
    write_t = state_write.T
    bits = peer_count.bit_length() - 1

    def payload(count):
        blocks = -(-(2 + count) // state_size)
        return shape_of((state_size, half + blocks * LANES), BF16)

    def auxiliary(count):
        return shape_of((-(-(3 + count) // 8) * 8, LANES), F32)

    own, send, running, running_t, perm, aux, expand = pl.pallas_call(
        functools.partial(before_kernel, peer_count),
        out_shape=(
            shape_of((state_size, half), F32),
            payload(1),
            shape_of((rows, head_count), F32),
            shape_of((head_count, rows), F32),
            shape_of((starts, starts), BF16),
            auxiliary(1),
            shape_of((LANES, half), BF16),
        ),
        in_specs=[SMEM] + [hbm] * 4,
        out_specs=(VMEM,) * 7,
        scratch_shapes=[
            pltpu.VMEM((rows, width), BF16),
            pltpu.VMEM((state_size, rows), BF16),
            pltpu.VMEM((head_count, rows), F32),
            pltpu.VMEM((1, starts), jnp.int32),
            pltpu.SemaphoreType.DMA((4,)),
        ],
        compiler_params=params,
    )(mine, features, write_t, log_decay.T, start_index.reshape(1, starts))

    def swap(array, bit):
        return lax.ppermute(array, "seq", [(i, i ^ (1 << bit)) for i in range(peer_count)])

    wide = shape_of((state_size, half), F32)
    got = swap(send, 0)
    first, group, send, aux = pl.pallas_call(
        pair_kernel,
        out_shape=(wide, wide, payload(2), auxiliary(2)),
        in_specs=[SMEM] + [VMEM] * 4,
        out_specs=(VMEM,) * 4,
        compiler_params=params,
    )(mine, own, got, aux, expand)

    local_out = pl.pallas_call(
        local_kernel,
        out_shape=shape_of((rows, width), F32),
        in_specs=[VMEM] * 6,
        out_specs=VMEM,
        compiler_params=params,
        cost_estimate=cost(4 * rows * rows * width, 2 * rows * width),
    )(
        features,
        write_t,
        read_t,
        running,
        running_t,
        jnp.broadcast_to(skip_gain[:, None], (head_count, head_width)).reshape(1, width),
    )

    prefix = None
    for bit in range(1, bits - 1):
        got = swap(send, bit)
        held = (group, aux, got, expand) if prefix is None else (group, prefix, aux, got, expand)
        group, prefix, send, aux = pl.pallas_call(
            functools.partial(first_stage_kernel if prefix is None else stage_kernel, bit),
            out_shape=(wide, wide, payload(2 << bit), auxiliary(2 << bit)),
            in_specs=[SMEM] + [VMEM] * len(held),
            out_specs=(VMEM,) * 4,
            compiler_params=params,
        )(mine, *held)
    got = swap(send, bits - 1)
    keep, back, pick = pl.pallas_call(
        functools.partial(last_stage_kernel, bits - 1, rows),
        out_shape=(
            shape_of((state_size, half), BF16),
            shape_of((state_size, half), BF16),
            shape_of((starts, rows), BF16),
        ),
        in_specs=[SMEM] + [VMEM] * 5,
        out_specs=(VMEM,) * 3,
        compiler_params=params,
    )(mine, prefix, aux, got, expand, first)
    got = swap(back, 0)

    posterior, picked = pl.pallas_call(
        after_kernel,
        out_shape=(shape_of((rows, width), BF16), shape_of((starts, width), BF16)),
        in_specs=[SMEM] + [VMEM] * 7,
        out_specs=(VMEM, VMEM),
        scratch_shapes=[pltpu.VMEM((rows, width), F32), pltpu.VMEM((rows, width), F32)],
        compiler_params=params,
    )(mine, local_out, read_t, running, keep, got, post_gain[None, :], pick)
    posterior = pl.pallas_call(
        flush_kernel,
        out_shape=shape_of((rows, width), BF16),
        in_specs=[VMEM],
        out_specs=VMEM,
        compiler_params=params,
        cost_estimate=cost(0, 4 * rows * width),
    )(posterior)

    landed = lax.all_to_all(
        picked.reshape(peer_count, cap, width), "seq", split_axis=0, concat_axis=0, tiled=True
    ).reshape(starts, width)

    horizon = step_noise.shape[0]
    values, final_latent = pl.pallas_call(
        imagine_kernel,
        out_shape=(shape_of((horizon, starts), F32), shape_of((starts, width), BF16)),
        in_specs=[VMEM] * 8,
        out_specs=(VMEM, VMEM),
        compiler_params=pltpu.CompilerParams(vmem_limit_bytes=16 << 20),
    )(
        landed,
        perm,
        step_noise,
        act_weight,
        dyn_weight,
        act_in_weight,
        out_weight,
        jnp.broadcast_to(value_weight[None, :], (16, value_weight.shape[0])),
    )
    return (posterior, values, final_latent)


def solution(mesh):
    whole = P()
    by_row = P(("groups", "seq"), None)
    placed = (
        by_row,
        by_row,
        by_row,
        by_row,
        whole,
        whole,
        P(("groups", "seq")),
        P(None, ("groups", "seq"), None),
        whole,
        whole,
        whole,
        whole,
        whole,
    )
    return jax.shard_map(
        functools.partial(per_device, mesh.shape["seq"]),
        mesh=mesh,
        in_specs=placed,
        out_specs=(by_row, P(None, ("groups", "seq")), by_row),
        check_vma=False,
    )
```

time: 68.4 us -> 66.4 us (0.971)
  blocking collectives: 19.4 us -> 0 us
  waiting for transfers between devices: 12.7 us -> 28 us
  starting transfers between devices: 8.06 us -> 13.5 us
  other arithmetic: 3.8 us -> 0 us
  local copies, waits for them, and re-layouts: 8.49 us -> 9.76 us
  Pallas kernels: 14.6 us -> 13.8 us
    all_to_all x1 -> x0, blocking collectives: 19.4 us -> none  [per_device(): lax.all_to_all(picked.reshape(peer_count, cap, width), 'seq', split_axis=...]
    all_to_all x0 -> x1, waiting for transfers between devices: none -> 13.4 us  [per_device(): lax.all_to_all(picked.reshape(peer_count, cap, width), 'seq', split_axis=...]
    all_to_all x0 -> x1, starting transfers between devices: none -> 5.4 us  [per_device(): lax.all_to_all(picked.reshape(peer_count, cap, width), 'seq', split_axis=...]
    pallas_call x1, Pallas kernels: 5.68 us -> 2.03 us  [per_device(): pl.pallas_call(after_kernel, out_shape=(shape_of((rows, width), BF16), sh...]
    convert_element_type x11 -> x0, other arithmetic: 2.74 us -> none  [the longest x1 1.46 us: per_device(): back = swap(jnp.where(upper, prefix, second_entry).astype(BF16), 0)]
    pallas_call x0 -> x5, Pallas kernels: none -> 2.46 us  [the longest x2 1.14 us: per_device(): pl.pallas_call(functools.partial(first_stage_kernel if prefix is None els...]
    unnamed x35 -> x28, local copies, waits for them, and re-layouts: 6.5 us -> 8.95 us
    ppermute x5, waiting for transfers between devices: 12.7 us -> 14.6 us  [swap(): lax.ppermute(array, 'seq', [(i, i ^ 1 << bit) for i in range(peer_count)])]
  transfers between devices with their start and end apart: 5 -> 6, of which waited for: 5 -> 5; matrix products, arithmetic and copies ran while one was open for 4% -> 1% of each run, Pallas kernels for 1% -> 3%
where the time goes in v2:
time: 66.4 us; the launch traced here: 65.8 us
  waiting for transfers between devices  28 us (42%)
  Pallas kernels  13.8 us (21%)
  starting transfers between devices  13.5 us (20%)
  local copies, waits for them, and re-layouts  9.76 us (15%)
  between operations  0.78 us (1%)
    ppermute x5, waiting for transfers between devices, swap(): lax.ppermute(array, 'seq', [(i, i ^ 1 << bit) for i in range(peer_count)])  14.6 us
    all_to_all x1, waiting for transfers between devices, per_device(): lax.all_to_all(picked.reshape(peer_count, cap, width), 'seq', split_axis=...  13.4 us
    unnamed x28, local copies, waits for them, and re-layouts  8.95 us
    ppermute x5, starting transfers between devices, swap(): lax.ppermute(array, 'seq', [(i, i ^ 1 << bit) for i in range(peer_count)])  8.07 us
    pallas_call x1, Pallas kernels, per_device(): pl.pallas_call(imagine_kernel, out_shape=(shape_of((horizon, starts), F32...  6.89 us
    all_to_all x1, starting transfers between devices, per_device(): lax.all_to_all(picked.reshape(peer_count, cap, width), 'seq', split_axis=...  5.4 us
    pallas_call x1, Pallas kernels, per_device(): pl.pallas_call(after_kernel, out_shape=(shape_of((rows, width), BF16), sh...  2.03 us
    pallas_call x1, Pallas kernels, per_device(): pl.pallas_call(functools.partial(before_kernel, peer_count), out_shape=(s...  1.5 us
  transfers between devices with their start and end apart: 6, of which 5 were waited for; matrix products, arithmetic and copies ran while one was open for 1% of the time, Pallas kernels for 3%

profile of v2, /device:TPU:0, one launch (start us, length us, event | category | flops | bytes accessed | tf_op | source)
XLA Modules:
  0.0 65.8 jit_solution(15537888416582029578)
XLA Ops:
  0.7 1.0 %copy-done.2 = bf16[128,2048]{1,0:T(8,128)(2,1)S(1)} copy-done((bf16[128,2048]{1,0:T(8,128)(2,1)S(1)}, bf16[128,2048]{1,0:T(8,128)(2,1)}, u32[]{:S(2)}) %copy-start.2) | copy-done | bytes 524312
  1.7 0.7 %copy-done.7 = bf16[128,64]{0,1:T(8,128)(2,1)S(1)} copy-done((bf16[128,64]{0,1:T(8,128)(2,1)S(1)}, bf16[128,64]{0,1:T(8,128)(2,1)}, u32[]{:S(2)}) %copy-start.7) | copy-done | bytes 16408
  2.4 0.7 %copy-done.10 = f32[128,32]{0,1:T(8,128)S(1)} copy-done((f32[128,32]{0,1:T(8,128)S(1)}, f32[128,32]{0,1:T(8,128)}, u32[]{:S(2)}) %copy-start.10) | copy-done | bytes 16408
  3.1 0.7 copy-done.12
  3.8 1.5 %shard_map.148 = (f32[64,1024]{1,0:T(8,128)S(1)}, bf16[64,1152]{1,0:T(8,128)(2,1)S(1)}, f32[128,32]{1,0:T(8,128)S(1)}, f32[32,128]{1,0:T(8,128)S(1)}, bf16[128,1...) custom-call(s32[1]{0:T(128)} %bitcast.mine_ref, bf16[128,2048]{1,0:T(8,128)(2,1)S(1)} %copy-done.2, ...), custom_call_target="tpu_custom_call" | custom-call | tf_op jit(solution)/shard_map/pallas_call | solution.py:331
  5.3 0.6 collective-permute-start
  5.8 1.0 %collective-permute-done.got_ref = bf16[64,1152]{1,0:T(8,128)(2,1)S(1)} collective-permute-done((bf16[64,1152]{1,0:T(8,128)(2,1)S(1)}, bf16[64,1152]{1,0:T(8,128)(2,1)S(1)}, u32[]{:S(2)}, u32[]{:S(2)}) %collective-permute-start) | collective-permute-done | bytes 147488 | tf_op jit(solution)/shard_map/ppermute | solution.py:355
  6.9 0.2 shard_map.150
  7.0 2.9 %collective-permute-start.1 = (bf16[64,1152]{1,0:T(8,128)(2,1)S(1)}, bf16[64,1152]{1,0:T(8,128)(2,1)S(1)}, u32[]{:S(2)}, u32[]{:S(2)}) collective-permute-start(bf16[64,1152]{1,0:T(8,128)(2,1)S(1)} %get-tuple-element.36), channel_id=1, source_target_pairs={{0,2},{1,3},{2,0},{3,1},{4,6},{5,7},{6,4},{7,5},{8,10},{9,11},{10,... | collective-permute-start | bytes 442376 | tf_op jit(solution)/shard_map/ppermute | solution.py:355
  10.0 4.2 %collective-permute-done.1.got_ref = bf16[64,1152]{1,0:T(8,128)(2,1)S(1)} collective-permute-done((bf16[64,1152]{1,0:T(8,128)(2,1)S(1)}, bf16[64,1152]{1,0:T(8,128)(2,1)S(1)}, u32[]{:S(2)}, u32[]{:S(2)}) %collective-permute-start.1) | collective-permute-done | bytes 147488 | tf_op jit(solution)/shard_map/ppermute | solution.py:355
  14.1 0.2 shard_map.151
  14.4 1.9 %collective-permute-start.2 = (bf16[64,1152]{1,0:T(8,128)(2,1)S(1)}, bf16[64,1152]{1,0:T(8,128)(2,1)S(1)}, u32[]{:S(2)}, u32[]{:S(2)}) collective-permute-start(bf16[64,1152]{1,0:T(8,128)(2,1)S(1)} %get-tuple-element.40), channel_id=1, source_target_pairs={{0,4},{1,5},{2,6},{3,7},{4,0},{5,1},{6,2},{7,3},{8,12},{9,13},{10,... | collective-permute-start | bytes 442376 | tf_op jit(solution)/shard_map/ppermute | solution.py:355
  16.2 3.5 %collective-permute-done.2.got_ref = bf16[64,1152]{1,0:T(8,128)(2,1)S(1)} collective-permute-done((bf16[64,1152]{1,0:T(8,128)(2,1)S(1)}, bf16[64,1152]{1,0:T(8,128)(2,1)S(1)}, u32[]{:S(2)}, u32[]{:S(2)}) %collective-permute-start.2) | collective-permute-done | bytes 147488 | tf_op jit(solution)/shard_map/ppermute | solution.py:355
  19.7 0.9 %shard_map.152 = (f32[64,1024]{1,0:T(8,128)}, f32[64,1024]{1,0:T(8,128)S(1)}, bf16[64,1152]{1,0:T(8,128)(2,1)S(1)}, f32[16,128]{1,0:T(8,128)S(1)}) custom-call(s32[1]{0:T(128)} %bitcast.mine_ref, f32[64,1024]{1,0:T(8,128)S(1)} %get-tuple-element.37.group_ref, f32[64,1024]{1,0:T(8,128)S(1)} %get-tuple-element.38.prefix_ref, ...), custom_call_target="tpu_custom_call" | custom-call | tf_op jit(solution)/shard_map/pallas_call | solution.py:387
  20.7 2.6 %collective-permute-start.3 = (bf16[64,1152]{1,0:T(8,128)(2,1)S(1)}, bf16[64,1152]{1,0:T(8,128)(2,1)S(1)}, u32[]{:S(2)}, u32[]{:S(2)}) collective-permute-start(bf16[64,1152]{1,0:T(8,128)(2,1)S(1)} %get-tuple-element.43), channel_id=1, source_target_pairs={{0,8},{1,9},{2,10},{3,11},{4,12},{5,13},{6,14},{7,15},{8,0},{9,1},... | collective-permute-start | bytes 442376 | tf_op jit(solution)/shard_map/ppermute | solution.py:355
  23.3 5.9 %collective-permute-done.3.got_ref = bf16[64,1152]{1,0:T(8,128)(2,1)S(1)} collective-permute-done((bf16[64,1152]{1,0:T(8,128)(2,1)S(1)}, bf16[64,1152]{1,0:T(8,128)(2,1)S(1)}, u32[]{:S(2)}, u32[]{:S(2)}) %collective-permute-start.3) | collective-permute-done | bytes 147488 | tf_op jit(solution)/shard_map/ppermute | solution.py:355
  29.2 0.3 shard_map.153
  29.5 0.1 collective-permute-start.4
  29.6 0.7 %broadcast_in_dim.6 = f32[32,64]{1,0:T(8,128)S(1)} broadcast(f32[32]{0:T(128)} %param.17), dimensions={0} | broadcast | bytes 8320 | tf_op jit(solution)/shard_map/broadcast_in_dim | solution.py:380
  30.3 0.1 reshape.25.skip_ref
  30.4 0.0 copy-start.8
  30.4 0.7 %copy-done.8 = bf16[128,64]{0,1:T(8,128)(2,1)S(1)} copy-done((bf16[128,64]{0,1:T(8,128)(2,1)S(1)}, bf16[128,64]{0,1:T(8,128)(2,1)}, u32[]{:S(2)}) %copy-start.8) | copy-done | bytes 16408
  31.1 0.7 %copy-done.9 = bf16[128,64]{0,1:T(8,128)(2,1)S(1)} copy-done((bf16[128,64]{0,1:T(8,128)(2,1)S(1)}, bf16[128,64]{0,1:T(8,128)(2,1)}, u32[]{:S(2)}) %copy-start.9) | copy-done | bytes 16408
  31.8 0.9 %shard_map.149.local_ref = f32[128,2048]{1,0:T(8,128)S(1)} custom-call(bf16[128,2048]{1,0:T(8,128)(2,1)S(1)} %copy-done.3, bf16[64,128]{1,0:T(8,128)(2,1)S(1)} %bitcast.10, bf16[64,128]{1,0:T(8,128)(2,1)S(1)} %bitcast.11, f32[128,32]{1,0:T(8,128)S(1)} %get-tuple-element.28.run_ref, f32[32,128]{1,0:T(8,128)S(1)} %get-tuple-element.29.run_t_ref, ...), custom_call_target="tpu_custom_call" | custom-call | flops 134217728 | bytes 524288 | tf_op jit(solution)/shard_map/pallas_call | solution.py:367
  32.8 2.0 %shard_map.154 = (bf16[128,2048]{1,0:T(8,128)(2,1)S(1)}, bf16[128,2048]{1,0:T(8,128)(2,1)}) custom-call(s32[1]{0:T(128)} %bitcast.mine_ref, f32[128,2048]{1,0:T(8,128)S(1)} %shard_map.149.local_ref, bf16[64,128]{1,0:T(8,128)(2,1)S(1)} %bitcast.12, f32[128,32]{1,0:T(8,128)S(1)} %get-tuple-element.28.run_ref, bf16[64,1024]{1,0:T(8,128)(2,1)S(1)} %get-tuple-element.45.keep_ref, ...), custom_call_target="tpu_custom_call" | custom-call | tf_op jit(solution)/shard_map/pallas_call | solution.py:408
  34.8 5.4 %all-to-all-start = ((bf16[16,8,2048]{2,1,0:T(8,128)(2,1)}), bf16[16,8,2048]{2,1,0:T(8,128)(2,1)S(1)}, u32[]{:S(2)}, u32[]{:S(2)}) async-start(bf16[16,8,2048]{2,1,0:T(8,128)(2,1)} %bitcast.6), calls=%async_computation | async-start | bytes 1048576 | tf_op jit(solution)/shard_map/all_to_all | solution.py:425
  40.2 0.8 %shard_map.155 = bf16[128,2048]{1,0:T(8,128)(2,1)} custom-call(bf16[128,2048]{1,0:T(8,128)(2,1)S(1)} %get-tuple-element.48.from_ref), custom_call_target="tpu_custom_call" | custom-call | bytes 1048576 | tf_op jit(solution)/shard_map/pallas_call | solution.py:416
  41.0 13.4 %all-to-all-done = bf16[16,8,2048]{2,1,0:T(8,128)(2,1)S(1)} async-done(((bf16[16,8,2048]{2,1,0:T(8,128)(2,1)}), bf16[16,8,2048]{2,1,0:T(8,128)(2,1)S(1)}, u32[]{:S(2)}, u32[]{:S(2)}) %all-to-all-start) | async-done | bytes 524320 | tf_op jit(solution)/shard_map/all_to_all | solution.py:425
  54.5 0.0 copy-start
  54.5 2.2 %copy-done = bf16[2048,1024]{1,0:T(8,128)(2,1)S(1)} copy-done((bf16[2048,1024]{1,0:T(8,128)(2,1)S(1)}, bf16[2048,1024]{1,0:T(8,128)(2,1)}, u32[]{:S(2)}) %copy-start) | copy-done | bytes 4194328
  56.7 2.2 %copy-done.1 = bf16[1024,2048]{1,0:T(8,128)(2,1)S(1)} copy-done((bf16[1024,2048]{1,0:T(8,128)(2,1)S(1)}, bf16[1024,2048]{1,0:T(8,128)(2,1)}, u32[]{:S(2)}) %copy-start.1) | copy-done | bytes 4194328
  58.9 6.9 %shard_map.156 = (f32[3,128]{1,0:T(4,128)}, bf16[128,2048]{1,0:T(8,128)(2,1)}) custom-call(bf16[128,2048]{1,0:T(8,128)(2,1)S(1)} %bitcast.8, bf16[128,128]{1,0:T(8,128)(2,1)S(1)} %get-tuple-element.50.perm_ref, bf16[3,128,1024]{2,1,0:T(8,128)(2,1)S(1)} %copy-done.4, bf16[2048,128]{1,0:T(8,128)(2,1)S(1)} %copy-done.5, bf16[2048,1024]{1,0:T(8,128)(2,1)S(1)} %copy-done, ...), custom_call_target="tpu_custom_call" | custom-call | tf_op jit(solution)/shard_map/pallas_call | solution.py:430
  (20 shorter events, 0.0 us)
Async XLA Ops:
  0.6 32.1 %copy-start.11 = (f32[2048]{0:T(1024)S(1)}, f32[2048]{0:T(1024)}, u32[]{:S(2)}) copy-start(f32[2048]{0:T(1024)} %param.18) | copy-start | bytes 24580
  0.6 1.0 %copy-start.2 = (bf16[128,2048]{1,0:T(8,128)(2,1)S(1)}, bf16[128,2048]{1,0:T(8,128)(2,1)}, u32[]{:S(2)}) copy-start(bf16[128,2048]{1,0:T(8,128)(2,1)} %x_ref.1) | copy-start | bytes 1572868
  1.7 0.7 %copy-start.7 = (bf16[128,64]{0,1:T(8,128)(2,1)S(1)}, bf16[128,64]{0,1:T(8,128)(2,1)}, u32[]{:S(2)}) copy-start(bf16[128,64]{0,1:T(8,128)(2,1)} %param.14) | copy-start | bytes 49156
  2.4 0.7 %copy-start.10 = (f32[128,32]{0,1:T(8,128)S(1)}, f32[128,32]{0,1:T(8,128)}, u32[]{:S(2)}) copy-start(f32[128,32]{0,1:T(8,128)} %param.16) | copy-start | bytes 49156
  3.1 0.7 copy-start.12
  3.8 26.6 %copy-start.3 = (bf16[128,2048]{1,0:T(8,128)(2,1)S(1)}, bf16[128,2048]{1,0:T(8,128)(2,1)}, u32[]{:S(2)}) copy-start(bf16[128,2048]{1,0:T(8,128)(2,1)} %x_ref.1) | copy-start | bytes 1572868
  5.3 1.6 %collective-permute-start = (bf16[64,1152]{1,0:T(8,128)(2,1)S(1)}, bf16[64,1152]{1,0:T(8,128)(2,1)S(1)}, u32[]{:S(2)}, u32[]{:S(2)}) collective-permute-start(bf16[64,1152]{1,0:T(8,128)(2,1)S(1)} %get-tuple-element.31), channel_id=1, source_target_pairs={{0,1},{1,0},{2,3},{3,2},{4,5},{5,4},{6,7},{7,6},{8,9},{9,8},{10,11... | collective-permute-start | bytes 442376 | tf_op jit(solution)/shard_map/ppermute | solution.py:355
  6.9 47.6 %copy-start.13 = (bf16[1024]{0:T(1024)(128)(2,1)S(1)}, bf16[1024]{0:T(1024)(128)(2,1)}, u32[]{:S(2)}) copy-start(bf16[1024]{0:T(1024)(128)(2,1)} %param.25) | copy-start | bytes 6148
  6.9 47.6 %copy-start.4 = (bf16[3,128,1024]{2,1,0:T(8,128)(2,1)S(1)}, bf16[3,128,1024]{2,1,0:T(8,128)(2,1)}, u32[]{:S(2)}) copy-start(bf16[3,128,1024]{2,1,0:T(8,128)(2,1)} %noise_ref.1) | copy-start | bytes 2359300
  6.9 47.6 %copy-start.5 = (bf16[2048,128]{1,0:T(8,128)(2,1)S(1)}, bf16[2048,128]{1,0:T(8,128)(2,1)}, u32[]{:S(2)}) copy-start(bf16[2048,128]{1,0:T(8,128)(2,1)} %act_ref.1) | copy-start | bytes 1572868
  6.9 47.6 %copy-start.6 = (bf16[128,1024]{1,0:T(8,128)(2,1)S(1)}, bf16[128,1024]{1,0:T(8,128)(2,1)}, u32[]{:S(2)}) copy-start(bf16[128,1024]{1,0:T(8,128)(2,1)} %act_in_ref.1) | copy-start | bytes 786436
  7.0 7.1 %collective-permute-start.1 = (bf16[64,1152]{1,0:T(8,128)(2,1)S(1)}, bf16[64,1152]{1,0:T(8,128)(2,1)S(1)}, u32[]{:S(2)}, u32[]{:S(2)}) collective-permute-start(bf16[64,1152]{1,0:T(8,128)(2,1)S(1)} %get-tuple-element.36), channel_id=1, source_target_pairs={{0,2},{1,3},{2,0},{3,1},{4,6},{5,7},{6,4},{7,5},{8,10},{9,11},{10,... | collective-permute-start | bytes 442376 | tf_op jit(solution)/shard_map/ppermute | solution.py:355
  14.4 5.4 %collective-permute-start.2 = (bf16[64,1152]{1,0:T(8,128)(2,1)S(1)}, bf16[64,1152]{1,0:T(8,128)(2,1)S(1)}, u32[]{:S(2)}, u32[]{:S(2)}) collective-permute-start(bf16[64,1152]{1,0:T(8,128)(2,1)S(1)} %get-tuple-element.40), channel_id=1, source_target_pairs={{0,4},{1,5},{2,6},{3,7},{4,0},{5,1},{6,2},{7,3},{8,12},{9,13},{10,... | collective-permute-start | bytes 442376 | tf_op jit(solution)/shard_map/ppermute | solution.py:355
  20.7 8.5 %collective-permute-start.3 = (bf16[64,1152]{1,0:T(8,128)(2,1)S(1)}, bf16[64,1152]{1,0:T(8,128)(2,1)S(1)}, u32[]{:S(2)}, u32[]{:S(2)}) collective-permute-start(bf16[64,1152]{1,0:T(8,128)(2,1)S(1)} %get-tuple-element.43), channel_id=1, source_target_pairs={{0,8},{1,9},{2,10},{3,11},{4,12},{5,13},{6,14},{7,15},{8,0},{9,1},... | collective-permute-start | bytes 442376 | tf_op jit(solution)/shard_map/ppermute | solution.py:355
  29.5 3.2 %collective-permute-start.4 = (bf16[64,1024]{1,0:T(8,128)(2,1)S(1)}, bf16[64,1024]{1,0:T(8,128)(2,1)S(1)}, u32[]{:S(2)}, u32[]{:S(2)}) collective-permute-start(bf16[64,1024]{1,0:T(8,128)(2,1)S(1)} %get-tuple-element.46), channel_id=1, source_target_pairs={{0,1},{1,0},{2,3},{3,2},{4,5},{5,4},{6,7},{7,6},{8,9},{9,8},{10,11... | collective-permute-start | bytes 393224 | tf_op jit(solution)/shard_map/ppermute | solution.py:355
  30.4 0.7 %copy-start.8 = (bf16[128,64]{0,1:T(8,128)(2,1)S(1)}, bf16[128,64]{0,1:T(8,128)(2,1)}, u32[]{:S(2)}) copy-start(bf16[128,64]{0,1:T(8,128)(2,1)} %param.14) | copy-start | bytes 49156
  31.1 0.7 %copy-start.9 = (bf16[128,64]{0,1:T(8,128)(2,1)S(1)}, bf16[128,64]{0,1:T(8,128)(2,1)}, u32[]{:S(2)}) copy-start(bf16[128,64]{0,1:T(8,128)(2,1)} %param.15) | copy-start | bytes 49156
  34.8 19.7 %all-to-all-start = ((bf16[16,8,2048]{2,1,0:T(8,128)(2,1)}), bf16[16,8,2048]{2,1,0:T(8,128)(2,1)S(1)}, u32[]{:S(2)}, u32[]{:S(2)}) async-start(bf16[16,8,2048]{2,1,0:T(8,128)(2,1)} %bitcast.6), calls=%async_computation | async-start | bytes 1048576 | tf_op jit(solution)/shard_map/all_to_all | solution.py:425
  54.5 2.2 %copy-start = (bf16[2048,1024]{1,0:T(8,128)(2,1)S(1)}, bf16[2048,1024]{1,0:T(8,128)(2,1)}, u32[]{:S(2)}) copy-start(bf16[2048,1024]{1,0:T(8,128)(2,1)} %dyn_ref.1) | copy-start | bytes 12582916
  56.7 2.2 %copy-start.1 = (bf16[1024,2048]{1,0:T(8,128)(2,1)S(1)}, bf16[1024,2048]{1,0:T(8,128)(2,1)}, u32[]{:S(2)}) copy-start(bf16[1024,2048]{1,0:T(8,128)(2,1)} %out_ref.1) | copy-start | bytes 12582916

commit v3 on v2

v3 whole, which is shorter than its diff:
```python
import functools
import jax
import jax.numpy as jnp
from jax import lax
from jax.experimental import pallas as pl
from jax.experimental.pallas import tpu as pltpu
from jax.sharding import PartitionSpec as P

F32 = jnp.float32
BF16 = jnp.bfloat16
LANES = 128
VMEM = pl.BlockSpec(memory_space=pltpu.VMEM)
SMEM = pl.BlockSpec(memory_space=pltpu.SMEM)
HBM = pl.BlockSpec(memory_space=pltpu.HBM)
ANY = pl.BlockSpec(memory_space=pl.ANY)


def iota(shape, dim):
    return lax.broadcasted_iota(jnp.int32, shape, dim)


def mask16(condition):
    return condition.astype(F32).astype(BF16)


def two_heads(cols, pair, head_width, shape):
    first = jnp.broadcast_to(cols[:, 2 * pair : 2 * pair + 1], shape)
    second = jnp.broadcast_to(cols[:, 2 * pair + 1 : 2 * pair + 2], shape)
    return jnp.where(iota(shape, 1) < head_width, first, second)


def stack_rows(rows, count):
    used = sum(row.shape[0] for row in rows)
    if used < count:
        rows = list(rows) + [jnp.zeros((count - used, LANES), F32)]
    return jnp.concatenate(rows, axis=0)


def write_meta(send_ref, decay, wanted, half, state_size):
    high = decay.astype(BF16).astype(F32)
    blocks = (send_ref.shape[1] - half) // LANES
    meta = stack_rows([high, decay - high, wanted], blocks * state_size).astype(BF16)
    for block in range(blocks):
        send_ref[:, half + block * LANES : half + (block + 1) * LANES] = meta[
            block * state_size : (block + 1) * state_size
        ]


def read_meta(got_ref, count, half, state_size):
    blocks = (got_ref.shape[1] - half) // LANES
    meta = jnp.concatenate(
        [got_ref[:, half + block * LANES : half + (block + 1) * LANES].astype(F32) for block in range(blocks)], axis=0
    )
    return meta[0:1] + meta[1:2], meta[2 : 2 + count]


def spread_rows(rows, half, head_width):
    pieces = []
    for row in rows:
        high = row.astype(BF16).astype(F32)
        pieces += [high, row - high]
    expand = mask16(iota((LANES, half), 0) == iota((LANES, half), 1) // head_width)
    wide = jnp.dot(stack_rows(pieces, 16).astype(BF16), expand, preferred_element_type=F32)
    return [wide[2 * k : 2 * k + 1] + wide[2 * k + 1 : 2 * k + 2] for k in range(len(rows))]


def requests(start_row, rows, cap):
    starts = start_row.shape[1]
    square = (starts, starts)
    index = jnp.broadcast_to(start_row.astype(F32), square)
    index_t = index.T
    owner = jnp.floor(index * (1.0 / rows))
    owner_t = jnp.floor(index_t * (1.0 / rows))
    earlier = (iota(square, 1) < iota(square, 0)) & (owner == owner_t)
    rank = jnp.sum(earlier.astype(F32), axis=1, keepdims=True)
    perm = (owner_t * cap + rank == iota(square, 1).astype(F32)).astype(F32)
    wanted = jnp.sum(perm * (index_t - owner_t * rows), axis=0, keepdims=True)
    return perm, wanted


def before_kernel(
    cap, mine_ref, x_hbm, x_other_ref, write_hbm, write_other_ref, decay_hbm, decay_other_ref, start_hbm,
    start_other_ref, send_ref, ends_ref, x_ref, write_ref, run_ref, run_t_ref, perm_ref, aux_ref,
    write_own_ref, decay_own_ref, start_own_ref, sems,
):
    core = mine_ref[0] % 2
    first = core == 0
    rows, half = x_ref.shape[0] // 2, x_ref.shape[1]
    state_size = write_ref.shape[0]
    heads = run_ref.shape[1]
    head_width = half // heads
    lanes_at = pl.multiple_of(core * half, LANES)
    rows_at = pl.multiple_of(core * rows, rows)
    others_at = pl.multiple_of((1 - core) * rows, rows)
    copies = [
        pltpu.make_async_copy(source, target, sems.at[k])
        for k, (source, target) in enumerate(
            (
                (decay_hbm, decay_own_ref),
                (write_hbm, write_own_ref),
                (x_hbm.at[:, pl.ds(lanes_at, half)], x_ref.at[pl.ds(rows_at, rows), :]),
                (start_hbm, start_own_ref),
            )
        )
    ]
    for copy in copies:
        copy.start()
    x_ref[pl.ds(others_at, rows), :] = x_other_ref[:, pl.ds(lanes_at, half)]
    upper = (iota((rows, rows), 0) <= iota((rows, rows), 1)).astype(F32)
    copies[0].wait()
    own, other = decay_own_ref[...], decay_other_ref[...]
    own = jnp.where(first, own[:heads], own[heads:])
    other = jnp.where(first, other[:heads], other[heads:])
    decays = jnp.concatenate([jnp.where(first, own, other), jnp.where(first, other, own)], axis=0)
    sums = jnp.dot(decays, upper, precision=lax.Precision.HIGHEST, preferred_element_type=F32)
    run_t = jnp.concatenate([sums[:heads], sums[heads:] + sums[:heads, rows - 1 :]], axis=1)
    run_t_ref[...] = run_t
    run = run_t.T
    run_ref[...] = run
    last = run[2 * rows - 1 :]
    tail = jnp.exp(last - run)
    copies[1].wait()
    own, other = write_own_ref[...], write_other_ref[...]
    write = jnp.concatenate([jnp.where(first, own, other), jnp.where(first, other, own)], axis=1)
    write_ref[...] = write
    copies[2].wait()
    for pair in range(heads // 2):
        lanes = slice(pair * LANES, (pair + 1) * LANES)
        scaled = x_ref[:, lanes].astype(F32) * two_heads(tail, pair, head_width, (2 * rows, LANES))
        ends = jnp.dot(write, scaled.astype(BF16), preferred_element_type=F32)
        ends_ref[:, lanes] = ends
        send_ref[:, lanes] = ends.astype(BF16)
    copies[3].wait()
    perm, wanted = requests(start_own_ref[...], rows, cap)
    perm_ref[...] = perm.astype(BF16)
    _, other_wanted = requests(start_other_ref[...], rows, cap)
    wanted = jnp.concatenate(
        [jnp.where(first, wanted, other_wanted), jnp.where(first, other_wanted, wanted)], axis=0
    )
    total = jnp.concatenate([jnp.exp(last), jnp.zeros((1, LANES - heads), F32)], axis=1)
    aux_ref[...] = stack_rows([total, jnp.ones((1, LANES), F32), wanted], aux_ref.shape[0])
    write_meta(send_ref, total, wanted, half, state_size)


def local_kernel(mine_ref, x_ref, write_ref, read_ref, read_other_ref, run_ref, run_t_ref, skip_ref, out_ref, read_out):
    first = mine_ref[0] % 2 == 0
    rows, half = x_ref.shape[0] // 2, x_ref.shape[1]
    heads = run_ref.shape[1]
    head_width = half // heads
    own, other = read_ref[...], read_other_ref[...]
    read = jnp.concatenate([jnp.where(first, own, other), jnp.where(first, other, own)], axis=1).T
    read_out[...] = read
    gram = jnp.dot(read, write_ref[...], preferred_element_type=F32)
    skip = jnp.where(first, skip_ref[:, :heads], skip_ref[:, heads:])
    mask = iota((rows, rows), 0) >= iota((rows, rows), 1)
    for chunk in range(2):
        at, count = chunk * rows, (chunk + 1) * rows
        lane = iota((count, LANES), 1)
        for pair in range(heads // 2):
            lanes = slice(pair * LANES, (pair + 1) * LANES)
            weights = []
            for head in (2 * pair, 2 * pair + 1):
                for back in range(chunk + 1):
                    seen = slice(back * rows, (back + 1) * rows)
                    spread = run_ref[at:count, head : head + 1] - run_t_ref[head : head + 1, seen]
                    if back == chunk:
                        spread = jnp.where(mask, spread, -jnp.inf)
                    weights.append((jnp.exp(spread) * gram[at:count, seen]).astype(BF16))
            x = x_ref[:count, lanes]
            zero = jnp.zeros_like(x)
            split = jnp.concatenate(
                [jnp.where(lane < head_width, x, zero), jnp.where(lane < head_width, zero, x)], axis=0
            )
            inner = jnp.dot(jnp.concatenate(weights, axis=1), split, preferred_element_type=F32)
            factor = two_heads(skip, pair, head_width, (1, LANES))
            out_ref[at:count, lanes] = inner + factor * x[at:count].astype(F32)


def stage_kernel(bit, has_prefix, head_width, mine_ref, group_ref, aux_ref, got_ref, prefix_ref, prefix_out, send_ref, aux_out, *group_out):
    state_size, half = group_ref.shape
    count = 1 << bit
    later = (mine_ref[0] >> bit) % 2 == 1
    new_decay, new_wanted = read_meta(got_ref, count, half, state_size)
    decay, prefix_decay = aux_ref[0:1], aux_ref[1:2]
    wanted = aux_ref[2 : 2 + count]
    into, across = spread_rows([prefix_decay, jnp.where(later, decay, new_decay)], half, head_width)
    group, got = group_ref[...], got_ref[:, :half].astype(F32)
    moved = into * got
    if has_prefix:
        moved = prefix_ref[...] + moved
        prefix_out[...] = jnp.where(later, moved, prefix_ref[...])
    else:
        prefix_out[...] = jnp.where(later, moved, jnp.zeros_like(moved))
    total = jnp.where(later, got, group) * across + jnp.where(later, group, got)
    for ref in group_out:
        ref[...] = total
    send_ref[:, :half] = total.astype(BF16)
    wanted = jnp.concatenate(
        [jnp.where(later, new_wanted, wanted), jnp.where(later, wanted, new_wanted)], axis=0
    )
    write_meta(send_ref, decay * new_decay, wanted, half, state_size)
    aux_out[...] = stack_rows(
        [decay * new_decay, jnp.where(later, prefix_decay * new_decay, prefix_decay), wanted], aux_out.shape[0]
    )


def last_stage_kernel(bit, rows, head_width, mine_ref, prefix_ref, aux_ref, got_ref, carry_ref, pick_ref):
    state_size, half = prefix_ref.shape
    count = 1 << bit
    mine = mine_ref[0]
    later = (mine >> bit) % 2 == 1
    _, new_wanted = read_meta(got_ref, count, half, state_size)
    (into,) = spread_rows([aux_ref[1:2]], half, head_width)
    prefix = prefix_ref[...]
    carry_ref[...] = jnp.where(later, prefix + into * got_ref[:, :half].astype(F32), prefix).astype(BF16)
    wanted = aux_ref[2 : 2 + count]
    wanted = jnp.concatenate(
        [jnp.where(later, new_wanted, wanted), jnp.where(later, wanted, new_wanted)], axis=0
    )
    peers = 2 * count
    picks = pick_ref.shape[0]
    both = picks // peers
    table = stack_rows([wanted], LANES) if peers < LANES else wanted
    asker = mask16(iota((picks, LANES), 0) // both == iota((picks, LANES), 1))
    by_slot = jnp.dot(asker, table.astype(BF16), preferred_element_type=F32)
    turn = iota((picks, LANES), 0) % both
    here = iota((picks, LANES), 1) == (mine // 2) * both + turn
    asked = jnp.sum(jnp.where(here, by_slot + ((turn // (both // 2)) * rows).astype(F32), 0.0), axis=1, keepdims=True)
    pick_ref[...] = mask16(asked == iota(pick_ref.shape, 1).astype(F32))


def after_kernel(
    mine_ref, local_ref, read_ref, run_ref, carry_ref, gain_ref, pick_ref, sent_ref, stay_ref, go_ref,
    mixed_ref, total_ref, post_ref,
):
    core = mine_ref[0] % 2
    rows, half = local_ref.shape[0] // 2, local_ref.shape[1]
    heads = run_ref.shape[1]
    head_width = half // heads
    entered = jnp.exp(run_ref[...])
    square = (LANES, LANES)
    same_head = mask16(iota(square, 0) // head_width == iota(square, 1) // head_width)
    gain = jnp.where(core == 0, gain_ref[:, :half], gain_ref[:, half:])
    blocks = [slice(k * LANES, (k + 1) * LANES) for k in range(half // LANES)]
    total_ref[...] = jnp.dot(read_ref[...], carry_ref[...], preferred_element_type=F32)
    for pair, lanes in enumerate(blocks):
        mixed_ref[:, lanes] = local_ref[:, lanes] + total_ref[:, lanes] * two_heads(
            entered, pair, head_width, (2 * rows, LANES)
        )
    for lanes in blocks:
        mixed = mixed_ref[:, lanes]
        squares = mixed * mixed
        high = squares.astype(BF16)
        low = (squares - high.astype(F32)).astype(BF16)
        total_ref[:, lanes] = jnp.dot(high, same_head, preferred_element_type=F32) + jnp.dot(
            low, same_head, preferred_element_type=F32
        )
    for lanes in blocks:
        scale = lax.rsqrt(total_ref[:, lanes] * (1.0 / head_width) + 1e-05)
        post_ref[:, lanes] = (mixed_ref[:, lanes] * scale * gain[:, lanes]).astype(BF16)
    sent_ref[...] = jnp.dot(pick_ref[...], post_ref[...], preferred_element_type=F32).astype(BF16)
    stay_ref[...] = post_ref[pl.ds(pl.multiple_of(core * rows, rows), rows), :]
    go_ref[...] = post_ref[pl.ds(pl.multiple_of((1 - core) * rows, rows), rows), :]


def fetch_kernel(token_ref, act_hbm, dyn_hbm, act_ref, dyn_ref, sems):
    copies = [
        pltpu.make_async_copy(act_hbm, act_ref, sems.at[0]),
        pltpu.make_async_copy(dyn_hbm.at[: dyn_ref.shape[0], :], dyn_ref, sems.at[1]),
    ]
    for copy in copies:
        copy.start()
    for copy in copies:
        copy.wait()


def flush_kernel(mine_ref, stay_ref, got_ref, post_ref):
    first = mine_ref[0] % 2 == 0
    half = stay_ref.shape[1]
    stay, got = stay_ref[...], got_ref[...]
    post_ref[:, :half] = jnp.where(first, stay, got)
    post_ref[:, half:] = jnp.where(first, got, stay)


def imagine_kernel(
    landed_ref, perm_ref, act_ref, head_ref, value_ref, noise_hbm, dyn_hbm, act_in_hbm, out_hbm,
    values_ref, final_ref, noise_ref, dyn_ref, act_in_ref, out_ref, sems,
):
    horizon = noise_ref.shape[0]
    starts = perm_ref.shape[0]
    half = landed_ref.shape[-1]
    depth = head_ref.shape[0]
    parts = dyn_hbm.shape[0] // depth
    wide = out_hbm.shape[0] // parts

    def dyn_part(k):
        rows = slice(k * depth, (k + 1) * depth)
        return pltpu.make_async_copy(dyn_hbm.at[rows, :], dyn_ref.at[rows, :], sems.at[k])

    def out_part(k):
        rows = slice(k * wide, (k + 1) * wide)
        return pltpu.make_async_copy(out_hbm.at[rows, :], out_ref.at[rows, :], sems.at[parts + k])

    small = [
        pltpu.make_async_copy(act_in_hbm, act_in_ref, sems.at[0]),
        pltpu.make_async_copy(noise_hbm, noise_ref, sems.at[2 * parts]),
    ]
    for k in range(1, parts):
        dyn_part(k).start()
    for copy in small:
        copy.start()
    dyn_ref[:depth, :] = head_ref[...]
    perm = perm_ref[...]
    latent = jnp.concatenate(
        [
            jnp.dot(perm, landed_ref[:, side].reshape(starts, half), preferred_element_type=F32)
            for side in range(2)
        ],
        axis=1,
    )
    rows = []
    for step in range(horizon):
        scale = lax.rsqrt(jnp.mean(latent * latent, axis=1, keepdims=True) + 1e-06)
        normed = (latent * scale).astype(BF16)
        action = jnp.tanh(jnp.dot(normed, act_ref[...], preferred_element_type=F32)).astype(BF16)
        if step == 0:
            inner = jnp.dot(normed[:, :depth], head_ref[...], preferred_element_type=F32)
            for k in range(1, parts):
                dyn_part(k).wait()
                if k == parts - 1:
                    for part in range(parts):
                        out_part(part).start()
                columns = slice(k * depth, (k + 1) * depth)
                inner = inner + jnp.dot(normed[:, columns], dyn_ref[columns, :], preferred_element_type=F32)
            for copy in small:
                copy.wait()
        else:
            inner = jnp.dot(normed, dyn_ref[...], preferred_element_type=F32)
        inner = inner + jnp.dot(action, act_in_ref[...], preferred_element_type=F32)
        hidden = (inner / (1.0 + jnp.exp(-inner)) + noise_ref[step].astype(F32)).astype(BF16)
        value = lax.dot_general(
            value_ref[...], hidden, (((1,), (1,)), ((), ())), preferred_element_type=F32
        )
        rows.append(value[0:1, :])
        if step == 0:
            moved = latent
            for k in range(parts):
                out_part(k).wait()
                columns = slice(k * wide, (k + 1) * wide)
                moved = moved + jnp.dot(hidden[:, columns], out_ref[columns, :], preferred_element_type=F32)
        else:
            moved = latent + jnp.dot(hidden, out_ref[...], preferred_element_type=F32)
        latent = moved.astype(BF16).astype(F32)
    final_ref[...] = latent.astype(BF16)
    values_ref[...] = jnp.concatenate(rows, axis=0)


def cost(flops, read):
    return pl.CostEstimate(flops=flops, bytes_accessed=read, transcendentals=0)


def in_hbm(array):
    return pltpu.with_memory_space_constraint(array, pltpu.HBM)


def per_device(
    peer_count,
    features,
    state_write,
    state_read,
    log_decay,
    skip_gain,
    post_gain,
    start_index,
    step_noise,
    act_weight,
    dyn_weight,
    act_in_weight,
    out_weight,
    value_weight,
):
    rows, width = features.shape
    head_count = log_decay.shape[1]
    head_width = width // head_count
    state_size = state_write.shape[1]
    half = width // 2
    heads = head_count // 2
    starts = start_index.shape[0]
    cap = starts // peer_count
    bits = peer_count.bit_length() - 1
    mine = lax.axis_index("seq").reshape(1)
    params = pltpu.CompilerParams(vmem_limit_bytes=12 << 20)
    held = pltpu.VMEM

    def swap(array, bit):
        return lax.ppermute(array, "seq", [(i, i ^ (1 << bit)) for i in range(peer_count)])

    def payload(count):
        blocks = -(-(2 + count) // state_size)
        return held((state_size, half + blocks * LANES), BF16)

    def auxiliary(count):
        return held((-(-(2 + count) // 8) * 8, LANES), F32)

    write_t, read_t, decay_t = state_write.T, state_read.T, log_decay.T
    start_row = start_index.reshape(1, starts)
    x_other = swap(features, 0)
    decay_other, write_other = swap(decay_t, 0), swap(write_t, 0)
    start_other, read_other = swap(start_row, 0), swap(read_t, 0)

    send, group, chip_x, write, run, run_t, perm, aux = pl.pallas_call(
        functools.partial(before_kernel, cap),
        out_shape=(
            payload(2),
            held((state_size, half), F32),
            held((2 * rows, half), BF16),
            held((state_size, 2 * rows), BF16),
            held((2 * rows, heads), F32),
            held((heads, 2 * rows), F32),
            held((starts, starts), BF16),
            auxiliary(2),
        ),
        in_specs=[SMEM, HBM, VMEM, HBM, VMEM, HBM, VMEM, HBM, VMEM],
        out_specs=(VMEM,) * 8,
        scratch_shapes=[
            pltpu.VMEM((state_size, rows), BF16),
            pltpu.VMEM((head_count, rows), F32),
            pltpu.VMEM((1, starts), jnp.int32),
            pltpu.SemaphoreType.DMA((4,)),
        ],
        compiler_params=params,
    )(
        mine,
        in_hbm(features),
        x_other,
        in_hbm(write_t),
        write_other,
        in_hbm(decay_t),
        decay_other,
        in_hbm(start_row),
        start_other,
    )

    local_out, read = pl.pallas_call(
        local_kernel,
        out_shape=(held((2 * rows, half), F32), held((2 * rows, state_size), BF16)),
        in_specs=[SMEM] + [VMEM] * 7,
        out_specs=(VMEM, VMEM),
        compiler_params=params,
        cost_estimate=cost(8 * rows * rows * width, 4 * rows * width),
    )(mine, chip_x, write, read_t, read_other, run, run_t, skip_gain[None, :])

    prefix, group = local_out, [group]
    for bit in range(1, bits - 1):
        got = swap(send, bit)
        goes_on = int(bit < bits - 2)
        prefix, send, aux, *group = pl.pallas_call(
            functools.partial(stage_kernel, bit, bit > 1, head_width),
            out_shape=(
                held((state_size, half), F32),
                payload(2 << bit),
                auxiliary(2 << bit),
            )
            + (held((state_size, half), F32),) * goes_on,
            in_specs=[SMEM] + [VMEM] * 3 + [VMEM if bit > 1 else ANY],
            out_specs=(VMEM,) * (3 + goes_on),
            compiler_params=params,
        )(mine, *group, aux, got, prefix)
    got = swap(send, bits - 1)
    carry, pick = pl.pallas_call(
        functools.partial(last_stage_kernel, bits - 1, rows, head_width),
        out_shape=(held((state_size, half), BF16), held((2 * starts, 2 * rows), BF16)),
        in_specs=[SMEM] + [VMEM] * 3,
        out_specs=(VMEM,) * 2,
        compiler_params=params,
    )(mine, prefix, aux, got)

    picked, stay, go = pl.pallas_call(
        after_kernel,
        out_shape=(
            held((2 * starts, half), BF16),
            held((rows, half), BF16),
            held((rows, half), BF16),
        ),
        in_specs=[SMEM] + [VMEM] * 6,
        out_specs=(VMEM,) * 3,
        scratch_shapes=[
            pltpu.VMEM((2 * rows, half), F32),
            pltpu.VMEM((2 * rows, half), F32),
            pltpu.VMEM((2 * rows, half), BF16),
        ],
        compiler_params=params,
    )(mine, local_out, read, run, carry, post_gain[None, :], pick)

    landed = lax.all_to_all(
        picked.reshape(peer_count, 2 * cap, half), "seq", split_axis=0, concat_axis=0, tiled=True
    ).reshape(peer_count // 2, 2, 2 * cap, half)

    head_rows = width // 8
    act, dyn_head = pl.pallas_call(
        fetch_kernel,
        out_shape=(held(act_weight.shape, BF16), held((head_rows, dyn_weight.shape[1]), BF16)),
        in_specs=[ANY, HBM, HBM],
        out_specs=(VMEM, VMEM),
        scratch_shapes=[pltpu.SemaphoreType.DMA((2,))],
        compiler_params=params,
        cost_estimate=cost(0, 4 * (act_weight.size + head_rows * dyn_weight.shape[1])),
    )(picked, in_hbm(act_weight), in_hbm(dyn_weight))

    posterior = pl.pallas_call(
        flush_kernel,
        out_shape=jax.ShapeDtypeStruct((rows, width), BF16),
        in_specs=[SMEM, VMEM, VMEM],
        out_specs=VMEM,
        compiler_params=params,
        cost_estimate=cost(0, 4 * rows * width),
    )(mine, stay, swap(go, 0))

    horizon = step_noise.shape[0]
    values, final_latent = pl.pallas_call(
        imagine_kernel,
        out_shape=(
            jax.ShapeDtypeStruct((horizon, starts), F32),
            jax.ShapeDtypeStruct((starts, width), BF16),
        ),
        in_specs=[VMEM] * 5 + [HBM] * 4,
        out_specs=(VMEM, VMEM),
        scratch_shapes=[
            pltpu.VMEM(step_noise.shape, BF16),
            pltpu.VMEM(dyn_weight.shape, BF16),
            pltpu.VMEM(act_in_weight.shape, BF16),
            pltpu.VMEM(out_weight.shape, BF16),
            pltpu.SemaphoreType.DMA((17,)),
        ],
        compiler_params=pltpu.CompilerParams(vmem_limit_bytes=40 << 20),
    )(
        landed,
        perm,
        act,
        dyn_head,
        jnp.broadcast_to(value_weight[None, :], (16, value_weight.shape[0])),
        *(in_hbm(array) for array in (step_noise, dyn_weight, act_in_weight, out_weight)),
    )
    return (posterior, values, final_latent)


def solution(mesh):
    whole = P()
    by_row = P(("groups", "seq"), None)
    placed = (
        by_row,
        by_row,
        by_row,
        by_row,
        whole,
        whole,
        P(("groups", "seq")),
        P(None, ("groups", "seq"), None),
        whole,
        whole,
        whole,
        whole,
        whole,
    )
    return jax.shard_map(
        functools.partial(per_device, mesh.shape["seq"]),
        mesh=mesh,
        in_specs=placed,
        out_specs=(by_row, P(None, ("groups", "seq")), by_row),
        check_vma=False,
    )
```

time: 66.4 us -> 60.2 us (0.907)
  local copies, waits for them, and re-layouts: 9.76 us -> 1.39 us
  Pallas kernels: 13.8 us -> 19.2 us
  waiting for transfers between devices: 28 us -> 24.9 us
    unnamed x28 -> x8, local copies, waits for them, and re-layouts: 8.95 us -> 1.38 us
    pallas_call x9, Pallas kernels: 13.8 us -> 19.2 us  [the longest x1 10.7 us: per_device(): pl.pallas_call(imagine_kernel, out_shape=(jax.ShapeDtypeStruct((horizon,...]
    all_to_all x1, waiting for transfers between devices: 13.4 us -> 11.7 us  [per_device(): lax.all_to_all(picked.reshape(peer_count, 2 * cap, half), 'seq', split_ax...]
    ppermute x5 -> x9, waiting for transfers between devices: 14.6 us -> 13.2 us  [swap(): lax.ppermute(array, 'seq', [(i, i ^ 1 << bit) for i in range(peer_count)])]
    ppermute x5 -> x9, starting transfers between devices: 8.07 us -> 9 us  [swap(): lax.ppermute(array, 'seq', [(i, i ^ 1 << bit) for i in range(peer_count)])]
    all_to_all x1, starting transfers between devices: 5.4 us -> 4.65 us  [per_device(): lax.all_to_all(picked.reshape(peer_count, 2 * cap, half), 'seq', split_ax...]
    broadcast_in_dim x1 -> x0, local copies, waits for them, and re-layouts: 0.73 us -> none  [per_device(): jnp.broadcast_to(skip_gain[:, None], (head_count, head_width))]
  transfers between devices with their start and end apart: 6 -> 10, of which waited for: 5 -> 6; matrix products, arithmetic and copies ran while one was open for 1% -> 0% of each run, Pallas kernels for 3% -> 6%
where the time goes in v3:
time: 60.2 us; the launch traced here: 59.9 us
  waiting for transfers between devices  24.9 us (41%)
  Pallas kernels  19.2 us (32%)
  starting transfers between devices  13.7 us (23%)
  local copies, waits for them, and re-layouts  1.39 us (2%)
  between operations  0.73 us (1%)
    ppermute x9, waiting for transfers between devices, swap(): lax.ppermute(array, 'seq', [(i, i ^ 1 << bit) for i in range(peer_count)])  13.2 us
    all_to_all x1, waiting for transfers between devices, per_device(): lax.all_to_all(picked.reshape(peer_count, 2 * cap, half), 'seq', split_ax...  11.7 us
    pallas_call x1, Pallas kernels, per_device(): pl.pallas_call(imagine_kernel, out_shape=(jax.ShapeDtypeStruct((horizon,...  10.7 us
    ppermute x9, starting transfers between devices, swap(): lax.ppermute(array, 'seq', [(i, i ^ 1 << bit) for i in range(peer_count)])  9 us
    all_to_all x1, starting transfers between devices, per_device(): lax.all_to_all(picked.reshape(peer_count, 2 * cap, half), 'seq', split_ax...  4.65 us
    pallas_call x1, Pallas kernels, per_device(): pl.pallas_call(functools.partial(before_kernel, cap), out_shape=(payload(...  2.23 us
    pallas_call x1, Pallas kernels, per_device(): pl.pallas_call(after_kernel, out_shape=(held((2 * starts, half), BF16), h...  2.19 us
    unnamed x8, local copies, waits for them, and re-layouts  1.38 us
  transfers between devices with their start and end apart: 10, of which 6 were waited for; matrix products, arithmetic and copies ran while one was open for 0% of the time, Pallas kernels for 6%

profile of v3, /device:TPU:0, one launch (start us, length us, event | category | flops | bytes accessed | tf_op | source)
XLA Modules:
  0.0 59.9 jit_solution(16969134800048894807)
XLA Ops:
  0.6 0.6 collective-permute-start
  1.2 0.1 collective-permute-start.1
  1.3 0.4 collective-permute-start.2
  1.7 0.1 collective-permute-start.3
  1.8 1.2 %collective-permute-done.3.start_other_ref = s32[1,128]{1,0:T(1,128)S(1)} collective-permute-done((s32[1,128]{1,0:T(1,128)}, s32[1,128]{1,0:T(1,128)S(1)}, u32[]{:S(2)}, u32[]{:S(2)}) %collective-permute-start.3) | collective-permute-done | bytes 544 | tf_op jit(solution)/shard_map/ppermute | solution.py:396
  3.0 0.0 collective-permute-done.1.write_other_ref
  3.0 0.0 collective-permute-done.2.decay_other_ref
  3.0 0.0 collective-permute-done.x_other_ref
  3.0 2.2 %shard_map.148 = (bf16[64,1152]{1,0:T(8,128)(2,1)S(1)}, f32[64,1024]{1,0:T(8,128)S(1)}, bf16[256,1024]{1,0:T(8,128)(2,1)S(1)}, bf16[64,256]{1,0:T(8,128)(2,1)S(1...) custom-call(s32[1]{0:T(128)} %bitcast.mine_ref, ...), custom_call_target="tpu_custom_call" | custom-call | tf_op jit(solution)/shard_map/pallas_call | solution.py:411
  5.3 2.9 %collective-permute-start.5 = (bf16[64,1152]{1,0:T(8,128)(2,1)S(1)}, bf16[64,1152]{1,0:T(8,128)(2,1)S(1)}, u32[]{:S(2)}, u32[]{:S(2)}) collective-permute-start(bf16[64,1152]{1,0:T(8,128)(2,1)S(1)} %get-tuple-element.37), channel_id=1, source_target_pairs={{0,2},{1,3},{2,0},{3,1},{4,6},{5,7},{6,4},{7,5},{8,10},{9,11},{10,... | collective-permute-start | bytes 442376 | tf_op jit(solution)/shard_map/ppermute | solution.py:396
  8.2 0.0 collective-permute-start.4
  8.2 1.4 %collective-permute-done.4.read_other_ref = bf16[64,128]{1,0:T(8,128)(2,1)S(1)} collective-permute-done((bf16[64,128]{1,0:T(8,128)(2,1)}, bf16[64,128]{1,0:T(8,128)(2,1)S(1)}, u32[]{:S(2)}, u32[]{:S(2)}) %collective-permute-start.4) | collective-permute-done | bytes 16416 | tf_op jit(solution)/shard_map/ppermute | solution.py:396
  9.6 0.7 %copy-done.1 = bf16[128,64]{0,1:T(8,128)(2,1)S(1)} copy-done((bf16[128,64]{0,1:T(8,128)(2,1)S(1)}, bf16[128,64]{0,1:T(8,128)(2,1)}, u32[]{:S(2)}) %copy-start.1) | copy-done | bytes 16408
  10.3 0.7 %copy-done.2 = f32[32]{0:T(128)S(1)} copy-done((f32[32]{0:T(128)S(1)}, f32[32]{0:T(128)}, u32[]{:S(2)}) %copy-start.2) | copy-done | bytes 152
  11.0 1.3 %shard_map.149 = (f32[256,1024]{1,0:T(8,128)S(1)}, bf16[256,64]{1,0:T(8,128)(2,1)S(1)}) custom-call(s32[1]{0:T(128)} %bitcast.mine_ref, bf16[256,1024]{1,0:T(8,128)(2,1)S(1)} %get-tuple-element.29.x_ref, bf16[64,256]{1,0:T(8,128)(2,1)S(1)} %get-tuple-element.30.write_ref, bf16[64,128]{1,0:T(8,128)(2,1)S(1)} %bitcast.12, ...), custom_call_target="tpu_custom_call" | custom-call | flops 268435456 | bytes 1048576 | tf_op jit(solution)/shard_map/pallas_call | solution.py:444
  12.3 0.1 collective-permute-done.5.got_ref
  12.3 0.2 shard_map.150
  12.6 1.9 %collective-permute-start.6 = (bf16[64,1152]{1,0:T(8,128)(2,1)S(1)}, bf16[64,1152]{1,0:T(8,128)(2,1)S(1)}, u32[]{:S(2)}, u32[]{:S(2)}) collective-permute-start(bf16[64,1152]{1,0:T(8,128)(2,1)S(1)} %get-tuple-element.40), channel_id=1, source_target_pairs={{0,4},{1,5},{2,6},{3,7},{4,0},{5,1},{6,2},{7,3},{8,12},{9,13},{10,... | collective-permute-start | bytes 442376 | tf_op jit(solution)/shard_map/ppermute | solution.py:396
  14.4 4.0 %collective-permute-done.6.got_ref = bf16[64,1152]{1,0:T(8,128)(2,1)S(1)} collective-permute-done((bf16[64,1152]{1,0:T(8,128)(2,1)S(1)}, bf16[64,1152]{1,0:T(8,128)(2,1)S(1)}, u32[]{:S(2)}, u32[]{:S(2)}) %collective-permute-start.6) | collective-permute-done | bytes 147488 | tf_op jit(solution)/shard_map/ppermute | solution.py:396
  18.5 0.2 shard_map.151
  18.7 2.7 %collective-permute-start.7 = (bf16[64,1152]{1,0:T(8,128)(2,1)S(1)}, bf16[64,1152]{1,0:T(8,128)(2,1)S(1)}, u32[]{:S(2)}, u32[]{:S(2)}) collective-permute-start(bf16[64,1152]{1,0:T(8,128)(2,1)S(1)} %get-tuple-element.44), channel_id=1, source_target_pairs={{0,8},{1,9},{2,10},{3,11},{4,12},{5,13},{6,14},{7,15},{8,0},{9,1},... | collective-permute-start | bytes 442376 | tf_op jit(solution)/shard_map/ppermute | solution.py:396
  21.3 6.5 %collective-permute-done.7.got_ref = bf16[64,1152]{1,0:T(8,128)(2,1)S(1)} collective-permute-done((bf16[64,1152]{1,0:T(8,128)(2,1)S(1)}, bf16[64,1152]{1,0:T(8,128)(2,1)S(1)}, u32[]{:S(2)}, u32[]{:S(2)}) %collective-permute-start.7) | collective-permute-done | bytes 147488 | tf_op jit(solution)/shard_map/ppermute | solution.py:396
  27.8 0.3 shard_map.152
  28.1 0.0 copy-start.3
  28.1 2.2 %shard_map.153 = (bf16[256,1024]{1,0:T(8,128)(2,1)}, bf16[128,1024]{1,0:T(8,128)(2,1)S(1)}, bf16[128,1024]{1,0:T(8,128)(2,1)S(1)}) custom-call(s32[1]{0:T(128)} %bitcast.mine_ref, f32[256,1024]{1,0:T(8,128)S(1)} %get-tuple-element.33.prefix_ref.local_ref, bf16[256,64]{1,0:T(8,128)(2,1)S(1)} %get-tuple-element.34.read_ref, ...), custom_call_target="tpu_custom_call" | custom-call | tf_op jit(solution)/shard_map/pallas_call | solution.py:478
  30.3 4.7 %all-to-all-start = ((bf16[16,16,1024]{2,1,0:T(8,128)(2,1)}), bf16[16,16,1024]{2,1,0:T(8,128)(2,1)S(1)}, u32[]{:S(2)}, u32[]{:S(2)}) async-start(bf16[16,16,1024]{2,1,0:T(8,128)(2,1)} %bitcast.7), calls=%async_computation | async-start | bytes 1048576 | tf_op jit(solution)/shard_map/all_to_all | solution.py:495
  34.9 0.4 collective-permute-start.8
  35.4 1.3 %shard_map.155 = (bf16[2048,128]{1,0:T(8,128)(2,1)S(1)}, bf16[256,1024]{1,0:T(8,128)(2,1)S(1)}) custom-call(bf16[256,1024]{1,0:T(8,128)(2,1)} %get-tuple-element.49.token_ref, bf16[2048,128]{1,0:T(8,128)(2,1)} %act_hbm.1, bf16[2048,1024]{1,0:T(8,128)(2,1)} %dyn_hbm.3), custom_call_target="tpu_custom_call" | custom-call | bytes 2097152 | tf_op jit(solution)/shard_map/pallas_call | solution.py:500
  36.6 0.0 collective-permute-done.8.got_ref
  36.6 0.9 %shard_map.154 = bf16[128,2048]{1,0:T(8,128)(2,1)} custom-call(s32[1]{0:T(128)} %bitcast.mine_ref, bf16[128,1024]{1,0:T(8,128)(2,1)S(1)} %get-tuple-element.47.stay_ref, bf16[128,1024]{1,0:T(8,128)(2,1)S(1)} %collective-permute-done.8.got_ref), custom_call_target="tpu_custom_call" | custom-call | bytes 1048576 | tf_op jit(solution)/shard_map/pallas_call | solution.py:510
  37.5 11.7 %all-to-all-done = bf16[16,16,1024]{2,1,0:T(8,128)(2,1)S(1)} async-done(((bf16[16,16,1024]{2,1,0:T(8,128)(2,1)}), bf16[16,16,1024]{2,1,0:T(8,128)(2,1)S(1)}, u32[]{:S(2)}, u32[]{:S(2)}) %all-to-all-start) | async-done | bytes 524320 | tf_op jit(solution)/shard_map/all_to_all | solution.py:495
  49.2 10.7 %shard_map.156 = (f32[3,128]{1,0:T(4,128)}, bf16[128,2048]{1,0:T(8,128)(2,1)}) custom-call(bf16[8,2,16,1024]{3,2,1,0:T(8,128)(2,1)S(1)} %bitcast.9, bf16[128,128]{1,0:T(8,128)(2,1)S(1)} %get-tuple-element.50.perm_ref, bf16[2048,128]{1,0:T(8,128)(2,1)S(1)} %get-tuple-element.51.act_ref, bf16[256,1024]{1,0:T(8,128)(2,1)S(1)} %get-tuple-element.52.head_ref, ...), custom_call_target="tpu_custom_call" | custom-call | tf_op jit(solution)/shard_map/pallas_call | solution.py:520
  (6 shorter events, 0.0 us)
Async XLA Ops:
  0.6 27.4 %copy-start = (f32[2048]{0:T(1024)S(1)}, f32[2048]{0:T(1024)}, u32[]{:S(2)}) copy-start(f32[2048]{0:T(1024)} %param.18) | copy-start | bytes 24580
  0.6 2.4 %collective-permute-start = (bf16[128,2048]{1,0:T(8,128)(2,1)}, bf16[128,2048]{1,0:T(8,128)(2,1)S(1)}, u32[]{:S(2)}, u32[]{:S(2)}) collective-permute-start(bf16[128,2048]{1,0:T(8,128)(2,1)} %x_hbm.1), channel_id=1, source_target_pairs={{0,1},{1,0},{2,3},{3,2},{4,5},{5,4},{6,7},{7,6},{8,9},{9,8},{10,11... | collective-permute-start | bytes 1572872 | tf_op jit(solution)/shard_map/ppermute | solution.py:396
  1.2 1.8 %collective-permute-start.1 = (bf16[64,128]{1,0:T(8,128)(2,1)}, bf16[64,128]{1,0:T(8,128)(2,1)S(1)}, u32[]{:S(2)}, u32[]{:S(2)}) collective-permute-start(bf16[64,128]{1,0:T(8,128)(2,1)} %bitcast.14), channel_id=1, source_target_pairs={{0,1},{1,0},{2,3},{3,2},{4,5},{5,4},{6,7},{7,6},{8,9},{9,8},{10,11... | collective-permute-start | bytes 49160 | tf_op jit(solution)/shard_map/ppermute | solution.py:396
  1.3 1.7 %collective-permute-start.2 = (f32[32,128]{1,0:T(8,128)}, f32[32,128]{1,0:T(8,128)S(1)}, u32[]{:S(2)}, u32[]{:S(2)}) collective-permute-start(f32[32,128]{1,0:T(8,128)} %bitcast.16), channel_id=1, source_target_pairs={{0,1},{1,0},{2,3},{3,2},{4,5},{5,4},{6,7},{7,6},{8,9},{9,8},{10,11... | collective-permute-start | bytes 49160 | tf_op jit(solution)/shard_map/ppermute | solution.py:396
  1.7 1.3 %collective-permute-start.3 = (s32[1,128]{1,0:T(1,128)}, s32[1,128]{1,0:T(1,128)S(1)}, u32[]{:S(2)}, u32[]{:S(2)}) collective-permute-start(s32[1,128]{1,0:T(1,128)} %bitcast.18), channel_id=1, source_target_pairs={{0,1},{1,0},{2,3},{3,2},{4,5},{5,4},{6,7},{7,6},{8,9},{9,8},{10,11... | collective-permute-start | bytes 1544 | tf_op jit(solution)/shard_map/ppermute | solution.py:396
  5.3 7.1 %collective-permute-start.5 = (bf16[64,1152]{1,0:T(8,128)(2,1)S(1)}, bf16[64,1152]{1,0:T(8,128)(2,1)S(1)}, u32[]{:S(2)}, u32[]{:S(2)}) collective-permute-start(bf16[64,1152]{1,0:T(8,128)(2,1)S(1)} %get-tuple-element.37), channel_id=1, source_target_pairs={{0,2},{1,3},{2,0},{3,1},{4,6},{5,7},{6,4},{7,5},{8,10},{9,11},{10,... | collective-permute-start | bytes 442376 | tf_op jit(solution)/shard_map/ppermute | solution.py:396
  8.2 1.4 %collective-permute-start.4 = (bf16[64,128]{1,0:T(8,128)(2,1)}, bf16[64,128]{1,0:T(8,128)(2,1)S(1)}, u32[]{:S(2)}, u32[]{:S(2)}) collective-permute-start(bf16[64,128]{1,0:T(8,128)(2,1)} %bitcast.11), channel_id=1, source_target_pairs={{0,1},{1,0},{2,3},{3,2},{4,5},{5,4},{6,7},{7,6},{8,9},{9,8},{10,11... | collective-permute-start | bytes 49160 | tf_op jit(solution)/shard_map/ppermute | solution.py:396
  9.6 0.7 %copy-start.1 = (bf16[128,64]{0,1:T(8,128)(2,1)S(1)}, bf16[128,64]{0,1:T(8,128)(2,1)}, u32[]{:S(2)}) copy-start(bf16[128,64]{0,1:T(8,128)(2,1)} %param.15) | copy-start | bytes 49156
  10.3 0.7 %copy-start.2 = (f32[32]{0:T(128)S(1)}, f32[32]{0:T(128)}, u32[]{:S(2)}) copy-start(f32[32]{0:T(128)} %param.17) | copy-start | bytes 388
  12.6 5.9 %collective-permute-start.6 = (bf16[64,1152]{1,0:T(8,128)(2,1)S(1)}, bf16[64,1152]{1,0:T(8,128)(2,1)S(1)}, u32[]{:S(2)}, u32[]{:S(2)}) collective-permute-start(bf16[64,1152]{1,0:T(8,128)(2,1)S(1)} %get-tuple-element.40), channel_id=1, source_target_pairs={{0,4},{1,5},{2,6},{3,7},{4,0},{5,1},{6,2},{7,3},{8,12},{9,13},{10,... | collective-permute-start | bytes 442376 | tf_op jit(solution)/shard_map/ppermute | solution.py:396
  18.7 9.1 %collective-permute-start.7 = (bf16[64,1152]{1,0:T(8,128)(2,1)S(1)}, bf16[64,1152]{1,0:T(8,128)(2,1)S(1)}, u32[]{:S(2)}, u32[]{:S(2)}) collective-permute-start(bf16[64,1152]{1,0:T(8,128)(2,1)S(1)} %get-tuple-element.44), channel_id=1, source_target_pairs={{0,8},{1,9},{2,10},{3,11},{4,12},{5,13},{6,14},{7,15},{8,0},{9,1},... | collective-permute-start | bytes 442376 | tf_op jit(solution)/shard_map/ppermute | solution.py:396
  28.1 21.1 %copy-start.3 = (bf16[1024]{0:T(1024)(128)(2,1)S(1)}, bf16[1024]{0:T(1024)(128)(2,1)}, u32[]{:S(2)}) copy-start(bf16[1024]{0:T(1024)(128)(2,1)} %param.25) | copy-start | bytes 6148
  30.3 18.9 %all-to-all-start = ((bf16[16,16,1024]{2,1,0:T(8,128)(2,1)}), bf16[16,16,1024]{2,1,0:T(8,128)(2,1)S(1)}, u32[]{:S(2)}, u32[]{:S(2)}) async-start(bf16[16,16,1024]{2,1,0:T(8,128)(2,1)} %bitcast.7), calls=%async_computation | async-start | bytes 1048576 | tf_op jit(solution)/shard_map/all_to_all | solution.py:495
  34.9 1.7 %collective-permute-start.8 = (bf16[128,1024]{1,0:T(8,128)(2,1)S(1)}, bf16[128,1024]{1,0:T(8,128)(2,1)S(1)}, u32[]{:S(2)}, u32[]{:S(2)}) collective-permute-start(bf16[128,1024]{1,0:T(8,128)(2,1)S(1)} %get-tuple-element.48), channel_id=1, source_target_pairs={{0,1},{1,0},{2,3},{3,2},{4,5},{5,4},{6,7},{7,6},{8,9},{9,8},{10,11... | collective-permute-start | bytes 786440 | tf_op jit(solution)/shard_map/ppermute | solution.py:396

commit v4 on v3

--- a/solution.py
+++ b/solution.py
@@ -78,71 +78,94 @@
     return perm, wanted
 
 
-def before_kernel(
-    cap, mine_ref, x_hbm, x_other_ref, write_hbm, write_other_ref, decay_hbm, decay_other_ref, start_hbm,
-    start_other_ref, send_ref, ends_ref, x_ref, write_ref, run_ref, run_t_ref, perm_ref, aux_ref,
-    write_own_ref, decay_own_ref, start_own_ref, sems,
+def own_kernel(
+    cap, mine_ref, x_hbm, write_hbm, decay_hbm, start_hbm, x_ref, write_ref, sums_ref, perm_ref, wanted_ref,
+    decay_ref, start_ref, sems,
 ):
     core = mine_ref[0] % 2
-    first = core == 0
-    rows, half = x_ref.shape[0] // 2, x_ref.shape[1]
-    state_size = write_ref.shape[0]
-    heads = run_ref.shape[1]
-    head_width = half // heads
+    rows, half = x_ref.shape
+    heads = sums_ref.shape[0]
     lanes_at = pl.multiple_of(core * half, LANES)
-    rows_at = pl.multiple_of(core * rows, rows)
-    others_at = pl.multiple_of((1 - core) * rows, rows)
     copies = [
         pltpu.make_async_copy(source, target, sems.at[k])
         for k, (source, target) in enumerate(
             (
-                (decay_hbm, decay_own_ref),
-                (write_hbm, write_own_ref),
-                (x_hbm.at[:, pl.ds(lanes_at, half)], x_ref.at[pl.ds(rows_at, rows), :]),
-                (start_hbm, start_own_ref),
+                (start_hbm, start_ref),
+                (decay_hbm, decay_ref),
+                (write_hbm, write_ref),
+                (x_hbm.at[:, pl.ds(lanes_at, half)], x_ref),
             )
         )
     ]
     for copy in copies:
         copy.start()
-    x_ref[pl.ds(others_at, rows), :] = x_other_ref[:, pl.ds(lanes_at, half)]
+    copies[0].wait()
+    perm, wanted = requests(start_ref[...], rows, cap)
+    perm_ref[...] = perm.astype(BF16)
+    wanted_ref[...] = wanted
+    copies[1].wait()
+    sums_ref[...] = running_sums(jnp.where(core == 0, decay_ref[:heads], decay_ref[heads:]))
+    copies[2].wait()
+    copies[3].wait()
+
+
+def running_sums(decays):
+    rows = decays.shape[1]
     upper = (iota((rows, rows), 0) <= iota((rows, rows), 1)).astype(F32)
-    copies[0].wait()
-    own, other = decay_own_ref[...], decay_other_ref[...]
-    own = jnp.where(first, own[:heads], own[heads:])
-    other = jnp.where(first, other[:heads], other[heads:])
-    decays = jnp.concatenate([jnp.where(first, own, other), jnp.where(first, other, own)], axis=0)
-    sums = jnp.dot(decays, upper, precision=lax.Precision.HIGHEST, preferred_element_type=F32)
-    run_t = jnp.concatenate([sums[:heads], sums[heads:] + sums[:heads, rows - 1 :]], axis=1)
+    return jnp.dot(decays, upper, precision=lax.Precision.HIGHEST, preferred_element_type=F32)
+
+
+def before_kernel(
+    cap, mine_ref, x_own_ref, x_other_ref, write_own_ref, write_other_ref, sums_ref, decay_other_ref, wanted_ref,
+    start_other_ref, send_ref, ends_ref, x_ref, write_ref, run_ref, run_t_ref, aux_ref,
+):
+    core = mine_ref[0] % 2
+    first = core == 0
+    rows, half = x_own_ref.shape
+    state_size = write_ref.shape[0]
+    heads = run_ref.shape[1]
+    head_width = half // heads
+    own, other = x_own_ref[...], x_other_ref[:, pl.ds(pl.multiple_of(core * half, LANES), half)]
+    x_ref[:rows, :] = jnp.where(first, own, other)
+    x_ref[rows:, :] = jnp.where(first, other, own)
+    own = sums_ref[...]
+    other = running_sums(jnp.where(first, decay_other_ref[:heads], decay_other_ref[heads:]))
+    one, two = jnp.where(first, own, other), jnp.where(first, other, own)
+    run_t = jnp.concatenate([one, two + one[:, rows - 1 :]], axis=1)
     run_t_ref[...] = run_t
     run = run_t.T
     run_ref[...] = run
     last = run[2 * rows - 1 :]
     tail = jnp.exp(last - run)
-    copies[1].wait()
     own, other = write_own_ref[...], write_other_ref[...]
     write = jnp.concatenate([jnp.where(first, own, other), jnp.where(first, other, own)], axis=1)
     write_ref[...] = write
-    copies[2].wait()
     for pair in range(heads // 2):
         lanes = slice(pair * LANES, (pair + 1) * LANES)
         scaled = x_ref[:, lanes].astype(F32) * two_heads(tail, pair, head_width, (2 * rows, LANES))
         ends = jnp.dot(write, scaled.astype(BF16), preferred_element_type=F32)
         ends_ref[:, lanes] = ends
         send_ref[:, lanes] = ends.astype(BF16)
-    copies[3].wait()
-    perm, wanted = requests(start_own_ref[...], rows, cap)
-    perm_ref[...] = perm.astype(BF16)
-    _, other_wanted = requests(start_other_ref[...], rows, cap)
-    wanted = jnp.concatenate(
-        [jnp.where(first, wanted, other_wanted), jnp.where(first, other_wanted, wanted)], axis=0
-    )
+    _, other = requests(start_other_ref[...], rows, cap)
+    own = wanted_ref[...]
+    wanted = jnp.concatenate([jnp.where(first, own, other), jnp.where(first, other, own)], axis=0)
     total = jnp.concatenate([jnp.exp(last), jnp.zeros((1, LANES - heads), F32)], axis=1)
     aux_ref[...] = stack_rows([total, jnp.ones((1, LANES), F32), wanted], aux_ref.shape[0])
     write_meta(send_ref, total, wanted, half, state_size)
 
 
-def local_kernel(mine_ref, x_ref, write_ref, read_ref, read_other_ref, run_ref, run_t_ref, skip_ref, out_ref, read_out):
+def local_kernel(
+    mine_ref, x_ref, write_ref, read_hbm, read_other_ref, run_ref, run_t_ref, skip_hbm, out_ref, read_out,
+    read_ref, skip_ref, sems,
+):
+    copies = [
+        pltpu.make_async_copy(read_hbm, read_ref, sems.at[0]),
+        pltpu.make_async_copy(skip_hbm, skip_ref, sems.at[1]),
+    ]
+    for copy in copies:
+        copy.start()
+    for copy in copies:
+        copy.wait()
     first = mine_ref[0] % 2 == 0
     rows, half = x_ref.shape[0] // 2, x_ref.shape[1]
     heads = run_ref.shape[1]
@@ -204,7 +227,7 @@
     )
 
 
-def last_stage_kernel(bit, rows, head_width, mine_ref, prefix_ref, aux_ref, got_ref, carry_ref, pick_ref):
+def last_stage_kernel(bit, rows, head_width, mine_ref, prefix_ref, aux_ref, got_ref, token_ref, carry_ref, pick_ref):
     state_size, half = prefix_ref.shape
     count = 1 << bit
     mine = mine_ref[0]
@@ -263,53 +286,38 @@
     go_ref[...] = post_ref[pl.ds(pl.multiple_of((1 - core) * rows, rows), rows), :]
 
 
-def fetch_kernel(token_ref, act_hbm, dyn_hbm, act_ref, dyn_ref, sems):
-    copies = [
-        pltpu.make_async_copy(act_hbm, act_ref, sems.at[0]),
-        pltpu.make_async_copy(dyn_hbm.at[: dyn_ref.shape[0], :], dyn_ref, sems.at[1]),
-    ]
+def fetch_kernel(token_ref, *refs):
+    count = (len(refs) - 1) // 2
+    sems = refs[-1]
+    copies = [pltpu.make_async_copy(refs[k], refs[count + k], sems.at[k]) for k in range(count)]
     for copy in copies:
         copy.start()
     for copy in copies:
         copy.wait()
 
 
-def flush_kernel(mine_ref, stay_ref, got_ref, post_ref):
-    first = mine_ref[0] % 2 == 0
-    half = stay_ref.shape[1]
-    stay, got = stay_ref[...], got_ref[...]
-    post_ref[:, :half] = jnp.where(first, stay, got)
-    post_ref[:, half:] = jnp.where(first, got, stay)
-
-
-def imagine_kernel(
-    landed_ref, perm_ref, act_ref, head_ref, value_ref, noise_hbm, dyn_hbm, act_in_hbm, out_hbm,
-    values_ref, final_ref, noise_ref, dyn_ref, act_in_ref, out_ref, sems,
-):
-    horizon = noise_ref.shape[0]
+def imagined_steps(latent, noise_ref, act_ref, dyn_ref, act_in_ref, out_ref, value_ref, steps):
+    rows = []
+    for step in steps:
+        scale = lax.rsqrt(jnp.mean(latent * latent, axis=1, keepdims=True) + 1e-06)
+        normed = (latent * scale).astype(BF16)
+        action = jnp.tanh(jnp.dot(normed, act_ref[...], preferred_element_type=F32)).astype(BF16)
+        inner = jnp.dot(normed, dyn_ref[...], preferred_element_type=F32) + jnp.dot(
+            action, act_in_ref[...], preferred_element_type=F32
+        )
+        hidden = (inner / (1.0 + jnp.exp(-inner)) + noise_ref[step].astype(F32)).astype(BF16)
+        value = lax.dot_general(
+            value_ref[...], hidden, (((1,), (1,)), ((), ())), preferred_element_type=F32
+        )
+        rows.append(value[0:1, :])
+        moved = latent + jnp.dot(hidden, out_ref[...], preferred_element_type=F32)
+        latent = moved.astype(BF16).astype(F32)
+    return latent, rows
+
+
+def first_step_kernel(landed_ref, perm_ref, noise_ref, act_ref, dyn_ref, act_in_ref, out_ref, value_ref, latent_ref, row_ref):
     starts = perm_ref.shape[0]
     half = landed_ref.shape[-1]
-    depth = head_ref.shape[0]
-    parts = dyn_hbm.shape[0] // depth
-    wide = out_hbm.shape[0] // parts
-
-    def dyn_part(k):
-        rows = slice(k * depth, (k + 1) * depth)
-        return pltpu.make_async_copy(dyn_hbm.at[rows, :], dyn_ref.at[rows, :], sems.at[k])
-
-    def out_part(k):
-        rows = slice(k * wide, (k + 1) * wide)
-        return pltpu.make_async_copy(out_hbm.at[rows, :], out_ref.at[rows, :], sems.at[parts + k])
-
-    small = [
-        pltpu.make_async_copy(act_in_hbm, act_in_ref, sems.at[0]),
-        pltpu.make_async_copy(noise_hbm, noise_ref, sems.at[2 * parts]),
-    ]
-    for k in range(1, parts):
-        dyn_part(k).start()
-    for copy in small:
-        copy.start()
-    dyn_ref[:depth, :] = head_ref[...]
     perm = perm_ref[...]
     latent = jnp.concatenate(
         [
@@ -318,41 +326,39 @@
         ],
         axis=1,
     )
-    rows = []
-    for step in range(horizon):
-        scale = lax.rsqrt(jnp.mean(latent * latent, axis=1, keepdims=True) + 1e-06)
-        normed = (latent * scale).astype(BF16)
-        action = jnp.tanh(jnp.dot(normed, act_ref[...], preferred_element_type=F32)).astype(BF16)
-        if step == 0:
-            inner = jnp.dot(normed[:, :depth], head_ref[...], preferred_element_type=F32)
-            for k in range(1, parts):
-                dyn_part(k).wait()
-                if k == parts - 1:
-                    for part in range(parts):
-                        out_part(part).start()
-                columns = slice(k * depth, (k + 1) * depth)
-                inner = inner + jnp.dot(normed[:, columns], dyn_ref[columns, :], preferred_element_type=F32)
-            for copy in small:
-                copy.wait()
-        else:
-            inner = jnp.dot(normed, dyn_ref[...], preferred_element_type=F32)
-        inner = inner + jnp.dot(action, act_in_ref[...], preferred_element_type=F32)
-        hidden = (inner / (1.0 + jnp.exp(-inner)) + noise_ref[step].astype(F32)).astype(BF16)
-        value = lax.dot_general(
-            value_ref[...], hidden, (((1,), (1,)), ((), ())), preferred_element_type=F32
-        )
-        rows.append(value[0:1, :])
-        if step == 0:
-            moved = latent
-            for k in range(parts):
-                out_part(k).wait()
-                columns = slice(k * wide, (k + 1) * wide)
-                moved = moved + jnp.dot(hidden[:, columns], out_ref[columns, :], preferred_element_type=F32)
-        else:
-            moved = latent + jnp.dot(hidden, out_ref[...], preferred_element_type=F32)
-        latent = moved.astype(BF16).astype(F32)
+    latent, rows = imagined_steps(
+        latent, noise_ref, act_ref, dyn_ref, act_in_ref, out_ref, value_ref, range(1)
+    )
+    latent_ref[...] = latent.astype(BF16)
+    row_ref[...] = rows[0]
+
+
+def later_steps_kernel(
+    mine_ref, stay_ref, got_ref, latent_ref, row_ref, noise_ref, act_ref, dyn_ref, act_in_ref, out_ref, value_ref,
+    post_hbm, values_ref, final_ref, sems,
+):
+    core = mine_ref[0] % 2
+    half = stay_ref.shape[1]
+    copies = [
+        pltpu.make_async_copy(source, post_hbm.at[:, pl.ds(pl.multiple_of(side * half, LANES), half)], sems.at[k])
+        for k, (source, side) in enumerate(((stay_ref, core), (got_ref, 1 - core)))
+    ]
+    for copy in copies:
+        copy.start()
+    latent, rows = imagined_steps(
+        latent_ref[...].astype(F32),
+        noise_ref,
+        act_ref,
+        dyn_ref,
+        act_in_ref,
+        out_ref,
+        value_ref,
+        range(1, noise_ref.shape[0]),
+    )
     final_ref[...] = latent.astype(BF16)
-    values_ref[...] = jnp.concatenate(rows, axis=0)
+    values_ref[...] = jnp.concatenate([row_ref[...]] + rows, axis=0)
+    for copy in copies:
+        copy.wait()
 
 
 def cost(flops, read):
@@ -408,7 +414,27 @@
     decay_other, write_other = swap(decay_t, 0), swap(write_t, 0)
     start_other, read_other = swap(start_row, 0), swap(read_t, 0)
 
-    send, group, chip_x, write, run, run_t, perm, aux = pl.pallas_call(
+    x_own, write_own, sums, perm, wanted = pl.pallas_call(
+        functools.partial(own_kernel, cap),
+        out_shape=(
+            held((rows, half), BF16),
+            held((state_size, rows), BF16),
+            held((heads, rows), F32),
+            held((starts, starts), BF16),
+            held((1, starts), F32),
+        ),
+        in_specs=[SMEM] + [HBM] * 4,
+        out_specs=(VMEM,) * 5,
+        scratch_shapes=[
+            pltpu.VMEM((head_count, rows), F32),
+            pltpu.VMEM((1, starts), jnp.int32),
+            pltpu.SemaphoreType.DMA((4,)),
+        ],
+        compiler_params=params,
+        cost_estimate=cost(0, 4 * rows * width),
+    )(mine, in_hbm(features), in_hbm(write_t), in_hbm(decay_t), in_hbm(start_row))
+
+    send, group, chip_x, write, run, run_t, aux = pl.pallas_call(
         functools.partial(before_kernel, cap),
         out_shape=(
             payload(2),
@@ -417,42 +443,44 @@
             held((state_size, 2 * rows), BF16),
             held((2 * rows, heads), F32),
             held((heads, 2 * rows), F32),
-            held((starts, starts), BF16),
             auxiliary(2),
         ),
-        in_specs=[SMEM, HBM, VMEM, HBM, VMEM, HBM, VMEM, HBM, VMEM],
-        out_specs=(VMEM,) * 8,
-        scratch_shapes=[
-            pltpu.VMEM((state_size, rows), BF16),
-            pltpu.VMEM((head_count, rows), F32),
-            pltpu.VMEM((1, starts), jnp.int32),
-            pltpu.SemaphoreType.DMA((4,)),
-        ],
+        in_specs=[SMEM] + [VMEM] * 8,
+        out_specs=(VMEM,) * 7,
         compiler_params=params,
-    )(
-        mine,
-        in_hbm(features),
-        x_other,
-        in_hbm(write_t),
-        write_other,
-        in_hbm(decay_t),
-        decay_other,
-        in_hbm(start_row),
-        start_other,
-    )
+    )(mine, x_own, x_other, write_own, write_other, sums, decay_other, wanted, start_other)
 
     local_out, read = pl.pallas_call(
         local_kernel,
         out_shape=(held((2 * rows, half), F32), held((2 * rows, state_size), BF16)),
-        in_specs=[SMEM] + [VMEM] * 7,
+        in_specs=[SMEM, VMEM, VMEM, HBM, VMEM, VMEM, VMEM, HBM],
         out_specs=(VMEM, VMEM),
+        scratch_shapes=[
+            pltpu.VMEM((state_size, rows), BF16),
+            pltpu.VMEM((1, head_count), F32),
+            pltpu.SemaphoreType.DMA((2,)),
+        ],
         compiler_params=params,
         cost_estimate=cost(8 * rows * rows * width, 4 * rows * width),
-    )(mine, chip_x, write, read_t, read_other, run, run_t, skip_gain[None, :])
+    )(mine, chip_x, write, in_hbm(read_t), read_other, run, run_t, in_hbm(skip_gain[None, :]))
+
+    def fetch(token, *weights):
+        return pl.pallas_call(
+            fetch_kernel,
+            out_shape=tuple(held(weight.shape, weight.dtype) for weight in weights),
+            in_specs=[ANY] + [HBM] * len(weights),
+            out_specs=(VMEM,) * len(weights),
+            scratch_shapes=[pltpu.SemaphoreType.DMA((len(weights),))],
+            compiler_params=params,
+            cost_estimate=cost(0, 2 * sum(weight.size * 2 for weight in weights)),
+        )(token, *(in_hbm(weight) for weight in weights))
 
     prefix, group = local_out, [group]
     for bit in range(1, bits - 1):
         got = swap(send, bit)
+        if bit == 2:
+            (dyn,) = fetch(aux, dyn_weight)
+            aux, _ = lax.optimization_barrier((aux, dyn))
         goes_on = int(bit < bits - 2)
         prefix, send, aux, *group = pl.pallas_call(
             functools.partial(stage_kernel, bit, bit > 1, head_width),
@@ -467,13 +495,14 @@
             compiler_params=params,
         )(mine, *group, aux, got, prefix)
     got = swap(send, bits - 1)
+    out, act, act_in, noise = fetch(aux, out_weight, act_weight, act_in_weight, step_noise)
     carry, pick = pl.pallas_call(
         functools.partial(last_stage_kernel, bits - 1, rows, head_width),
         out_shape=(held((state_size, half), BF16), held((2 * starts, 2 * rows), BF16)),
-        in_specs=[SMEM] + [VMEM] * 3,
+        in_specs=[SMEM] + [VMEM] * 3 + [ANY],
         out_specs=(VMEM,) * 2,
         compiler_params=params,
-    )(mine, prefix, aux, got)
+    )(mine, prefix, aux, got, act_in)
 
     picked, stay, go = pl.pallas_call(
         after_kernel,
@@ -496,51 +525,31 @@
         picked.reshape(peer_count, 2 * cap, half), "seq", split_axis=0, concat_axis=0, tiled=True
     ).reshape(peer_count // 2, 2, 2 * cap, half)
 
-    head_rows = width // 8
-    act, dyn_head = pl.pallas_call(
-        fetch_kernel,
-        out_shape=(held(act_weight.shape, BF16), held((head_rows, dyn_weight.shape[1]), BF16)),
-        in_specs=[ANY, HBM, HBM],
+    value_rows = jnp.broadcast_to(value_weight[None, :], (16, value_weight.shape[0]))
+    go, landed = lax.optimization_barrier((go, landed))
+    got = swap(go, 0)
+    horizon = step_noise.shape[0]
+    big = pltpu.CompilerParams(vmem_limit_bytes=16 << 20)
+    latent, row = pl.pallas_call(
+        first_step_kernel,
+        out_shape=(held((starts, width), BF16), held((1, starts), F32)),
+        in_specs=[VMEM] * 8,
         out_specs=(VMEM, VMEM),
-        scratch_shapes=[pltpu.SemaphoreType.DMA((2,))],
-        compiler_params=params,
-        cost_estimate=cost(0, 4 * (act_weight.size + head_rows * dyn_weight.shape[1])),
-    )(picked, in_hbm(act_weight), in_hbm(dyn_weight))
-
-    posterior = pl.pallas_call(
-        flush_kernel,
-        out_shape=jax.ShapeDtypeStruct((rows, width), BF16),
-        in_specs=[SMEM, VMEM, VMEM],
-        out_specs=VMEM,
-        compiler_params=params,
-        cost_estimate=cost(0, 4 * rows * width),
-    )(mine, stay, swap(go, 0))
-
-    horizon = step_noise.shape[0]
-    values, final_latent = pl.pallas_call(
-        imagine_kernel,
+        compiler_params=big,
+        cost_estimate=cost(2 * starts * 2 * dyn_weight.size, 4 * dyn_weight.size),
+    )(landed, perm, noise, act, dyn, act_in, out, value_rows)
+    posterior, values, final_latent = pl.pallas_call(
+        later_steps_kernel,
         out_shape=(
+            jax.ShapeDtypeStruct((rows, width), BF16),
             jax.ShapeDtypeStruct((horizon, starts), F32),
             jax.ShapeDtypeStruct((starts, width), BF16),
         ),
-        in_specs=[VMEM] * 5 + [HBM] * 4,
-        out_specs=(VMEM, VMEM),
-        scratch_shapes=[
-            pltpu.VMEM(step_noise.shape, BF16),
-            pltpu.VMEM(dyn_weight.shape, BF16),
-            pltpu.VMEM(act_in_weight.shape, BF16),
-            pltpu.VMEM(out_weight.shape, BF16),
-            pltpu.SemaphoreType.DMA((17,)),
-        ],
-        compiler_params=pltpu.CompilerParams(vmem_limit_bytes=40 << 20),
-    )(
-        landed,
-        perm,
-        act,
-        dyn_head,
-        jnp.broadcast_to(value_weight[None, :], (16, value_weight.shape[0])),
-        *(in_hbm(array) for array in (step_noise, dyn_weight, act_in_weight, out_weight)),
-    )
+        in_specs=[SMEM] + [VMEM] * 10,
+        out_specs=(HBM, VMEM, VMEM),
+        scratch_shapes=[pltpu.SemaphoreType.DMA((2,))],
+        compiler_params=big,
+    )(mine, stay, got, latent, row, noise, act, dyn, act_in, out, value_rows)
     return (posterior, values, final_latent)
 
 

time: 60.2 us -> 54.7 us (0.909)
  blocking collectives: 0 us -> 19.4 us
  waiting for transfers between devices: 24.9 us -> 6.84 us
  starting transfers between devices: 13.7 us -> 8.78 us
  local copies, waits for them, and re-layouts: 1.39 us -> 0.02 us
    all_to_all x0 -> x1, blocking collectives: none -> 19.4 us  [per_device(): lax.all_to_all(picked.reshape(peer_count, 2 * cap, half), 'seq', split_ax...]
    all_to_all x1 -> x0, waiting for transfers between devices: 11.7 us -> none  [per_device(): lax.all_to_all(picked.reshape(peer_count, 2 * cap, half), 'seq', split_ax...]
    ppermute x9, waiting for transfers between devices: 13.2 us -> 6.84 us  [swap(): lax.ppermute(array, 'seq', [(i, i ^ 1 << bit) for i in range(peer_count)])]
    all_to_all x1 -> x0, starting transfers between devices: 4.65 us -> none  [per_device(): lax.all_to_all(picked.reshape(peer_count, 2 * cap, half), 'seq', split_ax...]
    unnamed x8 -> x4, local copies, waits for them, and re-layouts: 1.38 us -> 0.01 us
    pallas_call x1, Pallas kernels: 2.23 us -> 1.26 us  [per_device(): pl.pallas_call(functools.partial(before_kernel, cap), out_shape=(payload(...]
    pallas_call x1, Pallas kernels: 2.19 us -> 1.38 us  [per_device(): pl.pallas_call(after_kernel, out_shape=(held((2 * starts, half), BF16), h...]
    pallas_call x1, Pallas kernels: 1.29 us -> 2.01 us  [per_device(): pl.pallas_call(local_kernel, out_shape=(held((2 * rows, half), F32), held...]
  transfers between devices with their start and end apart: 10 -> 9, of which waited for: 6 -> 5; matrix products, arithmetic and copies ran while one was open for 0% -> 0% of each run, Pallas kernels for 6% -> 19%
where the time goes in v4:
time: 54.7 us; the launch traced here: 54.4 us
  blocking collectives  19.4 us (35%)
  Pallas kernels  18.7 us (34%)
  starting transfers between devices  8.78 us (16%)
  waiting for transfers between devices  6.84 us (13%)
  between operations  0.74 us (1%)
    all_to_all x1, blocking collectives, per_device(): lax.all_to_all(picked.reshape(peer_count, 2 * cap, half), 'seq', split_ax...  19.4 us
    ppermute x9, starting transfers between devices, swap(): lax.ppermute(array, 'seq', [(i, i ^ 1 << bit) for i in range(peer_count)])  8.78 us
    ppermute x9, waiting for transfers between devices, swap(): lax.ppermute(array, 'seq', [(i, i ^ 1 << bit) for i in range(peer_count)])  6.84 us
    pallas_call x1, Pallas kernels, per_device(): pl.pallas_call(later_steps_kernel, out_shape=(jax.ShapeDtypeStruct((rows,...  5.07 us
    pallas_call x2, Pallas kernels, fetch(): pl.pallas_call(fetch_kernel, out_shape=tuple((held(weight.shape, weight.d...  4.87 us
    pallas_call x1, Pallas kernels, per_device(): pl.pallas_call(first_step_kernel, out_shape=(held((starts, width), BF16),...  2.34 us
    pallas_call x1, Pallas kernels, per_device(): pl.pallas_call(local_kernel, out_shape=(held((2 * rows, half), F32), held...  2.01 us
    pallas_call x1, Pallas kernels, per_device(): pl.pallas_call(after_kernel, out_shape=(held((2 * starts, half), BF16), h...  1.38 us
  transfers between devices with their start and end apart: 9, of which 5 were waited for; matrix products, arithmetic and copies ran while one was open for 0% of the time, Pallas kernels for 19%

profile of v4, /device:TPU:0, one launch (start us, length us, event | category | flops | bytes accessed | tf_op | source)
XLA Modules:
  0.0 54.4 jit_solution(11075814688222236160)
XLA Ops:
  0.6 0.6 %collective-permute-start = (bf16[128,2048]{1,0:T(8,128)(2,1)}, bf16[128,2048]{1,0:T(8,128)(2,1)S(1)}, u32[]{:S(2)}, u32[]{:S(2)}) collective-permute-start(bf16[128,2048]{1,0:T(8,128)(2,1)} %x_hbm.1), channel_id=1, source_target_pairs={{0,1},{1,0},{2,3},{3,2},{4,5},{5,4},{6,7},{7,6},{8,9},{9,8},{10,11... | collective-permute-start | bytes 1572872 | tf_op jit(solution)/shard_map/ppermute | solution.py:402
  1.2 0.1 collective-permute-start.1
  1.3 0.4 collective-permute-start.2
  1.7 0.1 collective-permute-start.3
  1.8 1.1 %shard_map.148 = (bf16[128,1024]{1,0:T(8,128)(2,1)S(1)}, bf16[64,128]{1,0:T(8,128)(2,1)S(1)}, f32[16,128]{1,0:T(8,128)S(1)}, bf16[128,128]{1,0:T(8,128)(2,1)S(1)}, f32[1,128]{1,0:T(1,128)S(1)}) custom-call(s32[1]{0:T(128)} %bitcast.mine_ref, bf16[128,2048]{1,0:T(8,128)(2,1)} %x_hbm.1, bf16[64,128]{1,0:T(8,128)(2,1)} %bitcast.13, f32[32,128]{1,0:T(8,128)} %bitcast.15, ...), custom_call_target="tpu_custom_call" | custom-call | bytes 1048576 | tf_op jit(solution)/shard_map/pallas_call | solution.py:417
  2.8 0.2 collective-permute-done.3.start_other_ref
  3.0 0.0 collective-permute-done.1.write_other_ref
  3.0 0.0 collective-permute-done.2.decay_other_ref
  3.0 0.0 collective-permute-done.x_other_ref
  3.0 1.3 %shard_map.149 = (bf16[64,1152]{1,0:T(8,128)(2,1)S(1)}, f32[64,1024]{1,0:T(8,128)S(1)}, bf16[256,1024]{1,0:T(8,128)(2,1)S(1)}, bf16[64,256]{1,0:T(8,128)(2,1)S(1...) custom-call(s32[1]{0:T(128)} %bitcast.mine_ref, ...), custom_call_target="tpu_custom_call" | custom-call | tf_op jit(solution)/shard_map/pallas_call | solution.py:437
  4.3 2.9 %collective-permute-start.5 = (bf16[64,1152]{1,0:T(8,128)(2,1)S(1)}, bf16[64,1152]{1,0:T(8,128)(2,1)S(1)}, u32[]{:S(2)}, u32[]{:S(2)}) collective-permute-start(bf16[64,1152]{1,0:T(8,128)(2,1)S(1)} %get-tuple-element.50), channel_id=1, source_target_pairs={{0,2},{1,3},{2,0},{3,1},{4,6},{5,7},{6,4},{7,5},{8,10},{9,11},{10,... | collective-permute-start | bytes 442376 | tf_op jit(solution)/shard_map/ppermute | solution.py:402
  7.2 0.0 collective-permute-start.4
  7.2 1.4 %collective-permute-done.4.read_other_ref = bf16[64,128]{1,0:T(8,128)(2,1)S(1)} collective-permute-done((bf16[64,128]{1,0:T(8,128)(2,1)}, bf16[64,128]{1,0:T(8,128)(2,1)S(1)}, u32[]{:S(2)}, u32[]{:S(2)}) %collective-permute-start.4) | collective-permute-done | bytes 16416 | tf_op jit(solution)/shard_map/ppermute | solution.py:402
  8.6 2.0 %shard_map.150 = (f32[256,1024]{1,0:T(8,128)S(1)}, bf16[256,64]{1,0:T(8,128)(2,1)S(1)}) custom-call(s32[1]{0:T(128)} %bitcast.mine_ref, bf16[256,1024]{1,0:T(8,128)(2,1)S(1)} %get-tuple-element.42.x_ref, bf16[64,256]{1,0:T(8,128)(2,1)S(1)} %get-tuple-element.43.write_ref, bf16[64,128]{1,0:T(8,128)(2,1)} %bitcast.19, ...), custom_call_target="tpu_custom_call" | custom-call | flops 268435456 | bytes 1048576 | tf_op jit(solution)/shard_map/pallas_call | solution.py:453
  10.6 0.8 %collective-permute-done.5.got_ref = bf16[64,1152]{1,0:T(8,128)(2,1)S(1)} collective-permute-done((bf16[64,1152]{1,0:T(8,128)(2,1)S(1)}, bf16[64,1152]{1,0:T(8,128)(2,1)S(1)}, u32[]{:S(2)}, u32[]{:S(2)}) %collective-permute-start.5) | collective-permute-done | bytes 147488 | tf_op jit(solution)/shard_map/ppermute | solution.py:402
  11.4 0.2 shard_map.151
  11.6 1.9 %collective-permute-start.6 = (bf16[64,1152]{1,0:T(8,128)(2,1)S(1)}, bf16[64,1152]{1,0:T(8,128)(2,1)S(1)}, u32[]{:S(2)}, u32[]{:S(2)}) collective-permute-start(bf16[64,1152]{1,0:T(8,128)(2,1)S(1)} %get-tuple-element.54), channel_id=1, source_target_pairs={{0,4},{1,5},{2,6},{3,7},{4,0},{5,1},{6,2},{7,3},{8,12},{9,13},{10,... | collective-permute-start | bytes 442376 | tf_op jit(solution)/shard_map/ppermute | solution.py:402
  13.4 2.2 %shard_map.152.dyn_ref = bf16[2048,1024]{1,0:T(8,128)(2,1)S(1)} custom-call(f32[8,128]{1,0:T(8,128)S(1)} %get-tuple-element.53.token_ref.aux_ref, bf16[2048,1024]{1,0:T(8,128)(2,1)} %refs_0_.2), custom_call_target="tpu_custom_call" | custom-call | bytes 8388608 | tf_op jit(solution)/shard_map/pallas_call | solution.py:468
  15.6 0.0 copy-start
  15.7 1.3 %collective-permute-done.6.got_ref = bf16[64,1152]{1,0:T(8,128)(2,1)S(1)} collective-permute-done((bf16[64,1152]{1,0:T(8,128)(2,1)S(1)}, bf16[64,1152]{1,0:T(8,128)(2,1)S(1)}, u32[]{:S(2)}, u32[]{:S(2)}) %collective-permute-start.6) | collective-permute-done | bytes 147488 | tf_op jit(solution)/shard_map/ppermute | solution.py:402
  17.0 0.2 shard_map.153
  17.2 2.7 %collective-permute-start.7 = (bf16[64,1152]{1,0:T(8,128)(2,1)S(1)}, bf16[64,1152]{1,0:T(8,128)(2,1)S(1)}, u32[]{:S(2)}, u32[]{:S(2)}) collective-permute-start(bf16[64,1152]{1,0:T(8,128)(2,1)S(1)} %get-tuple-element.58), channel_id=1, source_target_pairs={{0,8},{1,9},{2,10},{3,11},{4,12},{5,13},{6,14},{7,15},{8,0},{9,1},... | collective-permute-start | bytes 442376 | tf_op jit(solution)/shard_map/ppermute | solution.py:402
  19.9 2.7 %shard_map.154 = (bf16[1024,2048]{1,0:T(8,128)(2,1)S(1)}, bf16[2048,128]{1,0:T(8,128)(2,1)S(1)}, bf16[128,1024]{1,0:T(8,128)(2,1)S(1)}, bf16[3,128,1024]{2,1,0:T(8,128)(2,1)S(1)}) custom-call(f32[16,128]{1,0:T(8,128)S(1)} %get-tuple-element.57.token_ref.aux_ref, bf16[1024,2048]{1,0:T(8,128)(2,1)} %refs_0_.3, bf16[2048,128]{1,0:T(8,128)(2,1)} %refs_1_.1, ...), custom_call_target="tpu_custom_call" | custom-call | bytes 11534336 | tf_op jit(solution)/shard_map/pallas_call | solution.py:468
  22.6 3.2 %collective-permute-done.7.got_ref = bf16[64,1152]{1,0:T(8,128)(2,1)S(1)} collective-permute-done((bf16[64,1152]{1,0:T(8,128)(2,1)S(1)}, bf16[64,1152]{1,0:T(8,128)(2,1)S(1)}, u32[]{:S(2)}, u32[]{:S(2)}) %collective-permute-start.7) | collective-permute-done | bytes 147488 | tf_op jit(solution)/shard_map/ppermute | solution.py:402
  25.8 0.3 shard_map.155
  26.1 0.0 copy-done
  26.1 1.4 %shard_map.156 = (bf16[256,1024]{1,0:T(8,128)(2,1)S(1)}, bf16[128,1024]{1,0:T(8,128)(2,1)S(1)}, bf16[128,1024]{1,0:T(8,128)(2,1)S(1)}) custom-call(s32[1]{0:T(128)} %bitcast.mine_ref, f32[256,1024]{1,0:T(8,128)S(1)} %get-tuple-element.46.prefix_ref.local_ref, bf16[256,64]{1,0:T(8,128)(2,1)S(1)} %get-tuple-element.47.read_ref, ...), custom_call_target="tpu_custom_call" | custom-call | tf_op jit(solution)/shard_map/pallas_call | solution.py:507
  27.5 19.4 %all_to_all.5 = bf16[16,16,1024]{2,1,0:T(8,128)(2,1)S(1)} all-to-all(bf16[16,16,1024]{2,1,0:T(8,128)(2,1)S(1)} %bitcast.10), channel_id=1, replica_groups=mesh['groups'=2,'seq'=16] {'seq'}, dimensions={0} | all-to-all | bytes 1048576 | tf_op jit(solution)/shard_map/all_to_all | solution.py:524
  46.8 0.1 collective-permute-start.8
  47.0 2.3 %shard_map.157 = (bf16[128,2048]{1,0:T(8,128)(2,1)S(1)}, f32[1,128]{1,0:T(1,128)S(1)}) custom-call(bf16[8,2,16,1024]{3,2,1,0:T(8,128)(2,1)S(1)} %bitcast.9, bf16[128,128]{1,0:T(8,128)(2,1)S(1)} %get-tuple-element.67.perm_ref, bf16[3,128,1024]{2,1,0:T(8,128)(2,1)S(1)} %get-tuple-element.68.noise_ref, bf16[2048,128]{1,0:T(8,128)(2,1)S(1)} %get-tuple-element.69.act_ref, ...), custom_call_target="tpu_custom_call" | custom-call | flops 1073741824 | bytes 8388608 | tf_op jit(solution)/shard_map/pallas_call | solution.py:533
  49.3 0.0 collective-permute-done.8.got_ref
  49.3 5.1 %shard_map.158 = (bf16[128,2048]{1,0:T(8,128)(2,1)}, f32[3,128]{1,0:T(4,128)}, bf16[128,2048]{1,0:T(8,128)(2,1)}) custom-call(s32[1]{0:T(128)} %bitcast.mine_ref, bf16[128,1024]{1,0:T(8,128)(2,1)S(1)} %get-tuple-element.62.stay_ref, bf16[128,1024]{1,0:T(8,128)(2,1)S(1)} %collective-permute-done.8.got_ref, ...), custom_call_target="tpu_custom_call" | custom-call | tf_op jit(solution)/shard_map/pallas_call | solution.py:541
  (3 shorter events, 0.0 us)
Async XLA Ops:
  0.6 2.4 %collective-permute-start = (bf16[128,2048]{1,0:T(8,128)(2,1)}, bf16[128,2048]{1,0:T(8,128)(2,1)S(1)}, u32[]{:S(2)}, u32[]{:S(2)}) collective-permute-start(bf16[128,2048]{1,0:T(8,128)(2,1)} %x_hbm.1), channel_id=1, source_target_pairs={{0,1},{1,0},{2,3},{3,2},{4,5},{5,4},{6,7},{7,6},{8,9},{9,8},{10,11... | collective-permute-start | bytes 1572872 | tf_op jit(solution)/shard_map/ppermute | solution.py:402
  1.2 1.8 %collective-permute-start.1 = (bf16[64,128]{1,0:T(8,128)(2,1)}, bf16[64,128]{1,0:T(8,128)(2,1)S(1)}, u32[]{:S(2)}, u32[]{:S(2)}) collective-permute-start(bf16[64,128]{1,0:T(8,128)(2,1)} %bitcast.12), channel_id=1, source_target_pairs={{0,1},{1,0},{2,3},{3,2},{4,5},{5,4},{6,7},{7,6},{8,9},{9,8},{10,11... | collective-permute-start | bytes 49160 | tf_op jit(solution)/shard_map/ppermute | solution.py:402
  1.3 1.7 %collective-permute-start.2 = (f32[32,128]{1,0:T(8,128)}, f32[32,128]{1,0:T(8,128)S(1)}, u32[]{:S(2)}, u32[]{:S(2)}) collective-permute-start(f32[32,128]{1,0:T(8,128)} %bitcast.14), channel_id=1, source_target_pairs={{0,1},{1,0},{2,3},{3,2},{4,5},{5,4},{6,7},{7,6},{8,9},{9,8},{10,11... | collective-permute-start | bytes 49160 | tf_op jit(solution)/shard_map/ppermute | solution.py:402
  1.7 1.3 %collective-permute-start.3 = (s32[1,128]{1,0:T(1,128)}, s32[1,128]{1,0:T(1,128)S(1)}, u32[]{:S(2)}, u32[]{:S(2)}) collective-permute-start(s32[1,128]{1,0:T(1,128)} %bitcast.16), channel_id=1, source_target_pairs={{0,1},{1,0},{2,3},{3,2},{4,5},{5,4},{6,7},{7,6},{8,9},{9,8},{10,11... | collective-permute-start | bytes 1544 | tf_op jit(solution)/shard_map/ppermute | solution.py:402
  4.3 7.1 %collective-permute-start.5 = (bf16[64,1152]{1,0:T(8,128)(2,1)S(1)}, bf16[64,1152]{1,0:T(8,128)(2,1)S(1)}, u32[]{:S(2)}, u32[]{:S(2)}) collective-permute-start(bf16[64,1152]{1,0:T(8,128)(2,1)S(1)} %get-tuple-element.50), channel_id=1, source_target_pairs={{0,2},{1,3},{2,0},{3,1},{4,6},{5,7},{6,4},{7,5},{8,10},{9,11},{10,... | collective-permute-start | bytes 442376 | tf_op jit(solution)/shard_map/ppermute | solution.py:402
  7.2 1.4 %collective-permute-start.4 = (bf16[64,128]{1,0:T(8,128)(2,1)}, bf16[64,128]{1,0:T(8,128)(2,1)S(1)}, u32[]{:S(2)}, u32[]{:S(2)}) collective-permute-start(bf16[64,128]{1,0:T(8,128)(2,1)} %bitcast.18), channel_id=1, source_target_pairs={{0,1},{1,0},{2,3},{3,2},{4,5},{5,4},{6,7},{7,6},{8,9},{9,8},{10,11... | collective-permute-start | bytes 49160 | tf_op jit(solution)/shard_map/ppermute | solution.py:402
  11.6 5.4 %collective-permute-start.6 = (bf16[64,1152]{1,0:T(8,128)(2,1)S(1)}, bf16[64,1152]{1,0:T(8,128)(2,1)S(1)}, u32[]{:S(2)}, u32[]{:S(2)}) collective-permute-start(bf16[64,1152]{1,0:T(8,128)(2,1)S(1)} %get-tuple-element.54), channel_id=1, source_target_pairs={{0,4},{1,5},{2,6},{3,7},{4,0},{5,1},{6,2},{7,3},{8,12},{9,13},{10,... | collective-permute-start | bytes 442376 | tf_op jit(solution)/shard_map/ppermute | solution.py:402
  15.6 10.4 %copy-start = (f32[2048]{0:T(1024)S(1)}, f32[2048]{0:T(1024)}, u32[]{:S(2)}) copy-start(f32[2048]{0:T(1024)} %param.18) | copy-start | bytes 24580
  17.2 8.6 %collective-permute-start.7 = (bf16[64,1152]{1,0:T(8,128)(2,1)S(1)}, bf16[64,1152]{1,0:T(8,128)(2,1)S(1)}, u32[]{:S(2)}, u32[]{:S(2)}) collective-permute-start(bf16[64,1152]{1,0:T(8,128)(2,1)S(1)} %get-tuple-element.58), channel_id=1, source_target_pairs={{0,8},{1,9},{2,10},{3,11},{4,12},{5,13},{6,14},{7,15},{8,0},{9,1},... | collective-permute-start | bytes 442376 | tf_op jit(solution)/shard_map/ppermute | solution.py:402
  19.9 27.1 %copy-start.1 = (bf16[1024]{0:T(1024)(128)(2,1)S(1)}, bf16[1024]{0:T(1024)(128)(2,1)}, u32[]{:S(2)}) copy-start(bf16[1024]{0:T(1024)(128)(2,1)} %param.25) | copy-start | bytes 6148
  46.8 2.5 %collective-permute-start.8 = (bf16[128,1024]{1,0:T(8,128)(2,1)S(1)}, bf16[128,1024]{1,0:T(8,128)(2,1)S(1)}, u32[]{:S(2)}, u32[]{:S(2)}) collective-permute-start(bf16[128,1024]{1,0:T(8,128)(2,1)S(1)} %get-tuple-element.65), channel_id=1, source_target_pairs={{0,1},{1,0},{2,3},{3,2},{4,5},{5,4},{6,7},{7,6},{8,9},{9,8},{10,11... | collective-permute-start | bytes 786440 | tf_op jit(solution)/shard_map/ppermute | solution.py:402

commit v5 on v4

--- a/solution.py
+++ b/solution.py
@@ -296,46 +296,80 @@
         copy.wait()
 
 
-def imagined_steps(latent, noise_ref, act_ref, dyn_ref, act_in_ref, out_ref, value_ref, steps):
-    rows = []
+def folded(array):
+    total = array[:, :LANES]
+    for k in range(1, array.shape[1] // LANES):
+        total = total + array[:, k * LANES : (k + 1) * LANES]
+    return total
+
+
+def imagined_steps(held_refs, squares, noise_ref, act_ref, dyn_ref, act_in_ref, out_ref, value_ref, hidden_ref, steps):
+    width, inside = dyn_ref.shape
+    chunk = 256
+    columns = []
     for step in steps:
-        scale = lax.rsqrt(jnp.mean(latent * latent, axis=1, keepdims=True) + 1e-06)
-        normed = (latent * scale).astype(BF16)
-        action = jnp.tanh(jnp.dot(normed, act_ref[...], preferred_element_type=F32)).astype(BF16)
-        inner = jnp.dot(normed, dyn_ref[...], preferred_element_type=F32) + jnp.dot(
-            action, act_in_ref[...], preferred_element_type=F32
-        )
-        hidden = (inner / (1.0 + jnp.exp(-inner)) + noise_ref[step].astype(F32)).astype(BF16)
-        value = lax.dot_general(
-            value_ref[...], hidden, (((1,), (1,)), ((), ())), preferred_element_type=F32
-        )
-        rows.append(value[0:1, :])
-        moved = latent + jnp.dot(hidden, out_ref[...], preferred_element_type=F32)
-        latent = moved.astype(BF16).astype(F32)
-    return latent, rows
-
-
-def first_step_kernel(landed_ref, perm_ref, noise_ref, act_ref, dyn_ref, act_in_ref, out_ref, value_ref, latent_ref, row_ref):
+        latent_ref, next_ref = held_refs
+        scale = lax.rsqrt(jnp.sum(squares, axis=1, keepdims=True) * (1.0 / width) + 1e-06)
+        latent = latent_ref[...]
+        action = jnp.dot(latent, act_ref[...], preferred_element_type=F32)
+        action = jnp.tanh(action * scale).astype(BF16)
+        value = None
+        for at in range(0, inside, chunk):
+            part = slice(at, at + chunk)
+            inner = jnp.dot(latent, dyn_ref[:, part], preferred_element_type=F32) * scale + jnp.dot(
+                action, act_in_ref[:, part], preferred_element_type=F32
+            )
+            hidden = (inner / (1.0 + jnp.exp(-inner)) + noise_ref[step, :, part].astype(F32)).astype(BF16)
+            hidden_ref[:, part] = hidden
+            worth = folded(hidden.astype(F32) * value_ref[:, part].astype(F32))
+            value = worth if value is None else value + worth
+        columns.append(jnp.sum(value, axis=1, keepdims=True))
+        hidden = hidden_ref[...]
+        squares = None
+        for at in range(0, width, chunk):
+            part = slice(at, at + chunk)
+            moved = latent_ref[:, part].astype(F32) + jnp.dot(hidden, out_ref[:, part], preferred_element_type=F32)
+            rounded = moved.astype(BF16)
+            next_ref[:, part] = rounded
+            wide = rounded.astype(F32)
+            square = folded(wide * wide)
+            squares = square if squares is None else squares + square
+        held_refs = (next_ref, latent_ref)
+    return held_refs, squares, columns
+
+
+def first_step_kernel(
+    landed_ref, perm_ref, noise_ref, act_ref, dyn_ref, act_in_ref, out_ref, value_ref, latent_ref, squares_ref,
+    column_ref, start_ref, hidden_ref,
+):
     starts = perm_ref.shape[0]
     half = landed_ref.shape[-1]
     perm = perm_ref[...]
-    latent = jnp.concatenate(
-        [
-            jnp.dot(perm, landed_ref[:, side].reshape(starts, half), preferred_element_type=F32)
-            for side in range(2)
-        ],
-        axis=1,
+    squares = None
+    for side in range(2):
+        wide = jnp.dot(perm, landed_ref[:, side].reshape(starts, half), preferred_element_type=F32)
+        start_ref[:, side * half : (side + 1) * half] = wide.astype(BF16)
+        square = folded(wide * wide)
+        squares = square if squares is None else squares + square
+    _, squares, columns = imagined_steps(
+        (start_ref, latent_ref),
+        squares,
+        noise_ref,
+        act_ref,
+        dyn_ref,
+        act_in_ref,
+        out_ref,
+        value_ref,
+        hidden_ref,
+        range(1),
     )
-    latent, rows = imagined_steps(
-        latent, noise_ref, act_ref, dyn_ref, act_in_ref, out_ref, value_ref, range(1)
-    )
-    latent_ref[...] = latent.astype(BF16)
-    row_ref[...] = rows[0]
+    squares_ref[...] = squares
+    column_ref[...] = jnp.broadcast_to(columns[0], column_ref.shape)
 
 
 def later_steps_kernel(
-    mine_ref, stay_ref, got_ref, latent_ref, row_ref, noise_ref, act_ref, dyn_ref, act_in_ref, out_ref, value_ref,
-    post_hbm, values_ref, final_ref, sems,
+    mine_ref, stay_ref, got_ref, latent_ref, squares_ref, column_ref, noise_ref, act_ref, dyn_ref, act_in_ref,
+    out_ref, value_ref, post_hbm, values_ref, final_ref, spare_ref, hidden_ref, sems,
 ):
     core = mine_ref[0] % 2
     half = stay_ref.shape[1]
@@ -345,18 +379,28 @@
     ]
     for copy in copies:
         copy.start()
-    latent, rows = imagined_steps(
-        latent_ref[...].astype(F32),
-        noise_ref,
-        act_ref,
-        dyn_ref,
-        act_in_ref,
-        out_ref,
-        value_ref,
-        range(1, noise_ref.shape[0]),
-    )
-    final_ref[...] = latent.astype(BF16)
-    values_ref[...] = jnp.concatenate([row_ref[...]] + rows, axis=0)
+    horizon = noise_ref.shape[0]
+    refs, squares, columns = (latent_ref, None), squares_ref[...], []
+    for step in range(1, horizon):
+        target = final_ref if step == horizon - 1 else spare_ref.at[step % 2]
+        refs, squares, new = imagined_steps(
+            (refs[0], target),
+            squares,
+            noise_ref,
+            act_ref,
+            dyn_ref,
+            act_in_ref,
+            out_ref,
+            value_ref,
+            hidden_ref,
+            range(step, step + 1),
+        )
+        columns += new
+    lane = iota(column_ref.shape, 1)
+    table = column_ref[...]
+    for k, column in enumerate(columns):
+        table = jnp.where(lane == k + 1, column, table)
+    values_ref[...] = table.T[:horizon]
     for copy in copies:
         copy.wait()
 
@@ -525,19 +569,21 @@
         picked.reshape(peer_count, 2 * cap, half), "seq", split_axis=0, concat_axis=0, tiled=True
     ).reshape(peer_count // 2, 2, 2 * cap, half)
 
-    value_rows = jnp.broadcast_to(value_weight[None, :], (16, value_weight.shape[0]))
     go, landed = lax.optimization_barrier((go, landed))
     got = swap(go, 0)
     horizon = step_noise.shape[0]
     big = pltpu.CompilerParams(vmem_limit_bytes=16 << 20)
-    latent, row = pl.pallas_call(
+    weights = (noise, act, dyn, act_in, out, value_weight[None, :])
+    hidden = pltpu.VMEM((starts, dyn_weight.shape[1]), BF16)
+    latent, squares, column = pl.pallas_call(
         first_step_kernel,
-        out_shape=(held((starts, width), BF16), held((1, starts), F32)),
+        out_shape=(held((starts, width), BF16), held((starts, LANES), F32), held((starts, LANES), F32)),
         in_specs=[VMEM] * 8,
-        out_specs=(VMEM, VMEM),
+        out_specs=(VMEM,) * 3,
+        scratch_shapes=[pltpu.VMEM((starts, width), BF16), hidden],
         compiler_params=big,
         cost_estimate=cost(2 * starts * 2 * dyn_weight.size, 4 * dyn_weight.size),
-    )(landed, perm, noise, act, dyn, act_in, out, value_rows)
+    )(landed, perm, *weights)
     posterior, values, final_latent = pl.pallas_call(
         later_steps_kernel,
         out_shape=(
@@ -545,11 +591,11 @@
             jax.ShapeDtypeStruct((horizon, starts), F32),
             jax.ShapeDtypeStruct((starts, width), BF16),
         ),
-        in_specs=[SMEM] + [VMEM] * 10,
+        in_specs=[SMEM] + [VMEM] * 11,
         out_specs=(HBM, VMEM, VMEM),
-        scratch_shapes=[pltpu.SemaphoreType.DMA((2,))],
+        scratch_shapes=[pltpu.VMEM((2, starts, width), BF16), hidden, pltpu.SemaphoreType.DMA((2,))],
         compiler_params=big,
-    )(mine, stay, got, latent, row, noise, act, dyn, act_in, out, value_rows)
+    )(mine, stay, got, latent, squares, column, *weights)
     return (posterior, values, final_latent)
 
 

time: 54.7 us -> 53.9 us (0.985)
  Pallas kernels: 18.7 us -> 17.9 us
  transfers between devices with their start and end apart: 9 -> 9, of which waited for: 5 -> 5; matrix products, arithmetic and copies ran while one was open for 0% -> 0% of each run, Pallas kernels for 19% -> 18%
where the time goes in v5:
time: 53.9 us; the launch traced here: 53.7 us
  blocking collectives  19.4 us (36%)
  Pallas kernels  17.9 us (33%)
  starting transfers between devices  8.78 us (16%)
  waiting for transfers between devices  6.82 us (13%)
  between operations  0.74 us (1%)
    all_to_all x1, blocking collectives, per_device(): lax.all_to_all(picked.reshape(peer_count, 2 * cap, half), 'seq', split_ax...  19.4 us
    ppermute x9, starting transfers between devices, swap(): lax.ppermute(array, 'seq', [(i, i ^ 1 << bit) for i in range(peer_count)])  8.78 us
    ppermute x9, waiting for transfers between devices, swap(): lax.ppermute(array, 'seq', [(i, i ^ 1 << bit) for i in range(peer_count)])  6.82 us
    pallas_call x2, Pallas kernels, fetch(): pl.pallas_call(fetch_kernel, out_shape=tuple((held(weight.shape, weight.d...  4.87 us
    pallas_call x1, Pallas kernels, per_device(): pl.pallas_call(later_steps_kernel, out_shape=(jax.ShapeDtypeStruct((rows,...  4.73 us
    pallas_call x1, Pallas kernels, per_device(): pl.pallas_call(local_kernel, out_shape=(held((2 * rows, half), F32), held...  2.02 us
    pallas_call x1, Pallas kernels, per_device(): pl.pallas_call(first_step_kernel, out_shape=(held((starts, width), BF16),...  1.92 us
    pallas_call x1, Pallas kernels, per_device(): pl.pallas_call(after_kernel, out_shape=(held((2 * starts, half), BF16), h...  1.39 us
  transfers between devices with their start and end apart: 9, of which 5 were waited for; matrix products, arithmetic and copies ran while one was open for 0% of the time, Pallas kernels for 18%

profile of v5, /device:TPU:0, one launch (start us, length us, event | category | flops | bytes accessed | tf_op | source)
XLA Modules:
  0.0 53.7 jit_solution(15484333610435151069)
XLA Ops:
  0.6 0.6 %collective-permute-start = (bf16[128,2048]{1,0:T(8,128)(2,1)}, bf16[128,2048]{1,0:T(8,128)(2,1)S(1)}, u32[]{:S(2)}, u32[]{:S(2)}) collective-permute-start(bf16[128,2048]{1,0:T(8,128)(2,1)} %x_hbm.1), channel_id=1, source_target_pairs={{0,1},{1,0},{2,3},{3,2},{4,5},{5,4},{6,7},{7,6},{8,9},{9,8},{10,11... | collective-permute-start | bytes 1572872 | tf_op jit(solution)/shard_map/ppermute | solution.py:446
  1.2 0.1 collective-permute-start.1
  1.3 0.4 collective-permute-start.2
  1.7 0.1 collective-permute-start.3
  1.8 1.1 %shard_map.148 = (bf16[128,1024]{1,0:T(8,128)(2,1)S(1)}, bf16[64,128]{1,0:T(8,128)(2,1)S(1)}, f32[16,128]{1,0:T(8,128)S(1)}, bf16[128,128]{1,0:T(8,128)(2,1)S(1)}, f32[1,128]{1,0:T(1,128)S(1)}) custom-call(s32[1]{0:T(128)} %bitcast.mine_ref, bf16[128,2048]{1,0:T(8,128)(2,1)} %x_hbm.1, bf16[64,128]{1,0:T(8,128)(2,1)} %bitcast.13, f32[32,128]{1,0:T(8,128)} %bitcast.15, ...), custom_call_target="tpu_custom_call" | custom-call | bytes 1048576 | tf_op jit(solution)/shard_map/pallas_call | solution.py:461
  2.8 0.2 collective-permute-done.3.start_other_ref
  3.0 0.0 collective-permute-done.1.write_other_ref
  3.0 0.0 collective-permute-done.2.decay_other_ref
  3.0 0.0 collective-permute-done.x_other_ref
  3.0 1.3 %shard_map.149 = (bf16[64,1152]{1,0:T(8,128)(2,1)S(1)}, f32[64,1024]{1,0:T(8,128)S(1)}, bf16[256,1024]{1,0:T(8,128)(2,1)S(1)}, bf16[64,256]{1,0:T(8,128)(2,1)S(1...) custom-call(s32[1]{0:T(128)} %bitcast.mine_ref, ...), custom_call_target="tpu_custom_call" | custom-call | tf_op jit(solution)/shard_map/pallas_call | solution.py:481
  4.3 2.9 %collective-permute-start.5 = (bf16[64,1152]{1,0:T(8,128)(2,1)S(1)}, bf16[64,1152]{1,0:T(8,128)(2,1)S(1)}, u32[]{:S(2)}, u32[]{:S(2)}) collective-permute-start(bf16[64,1152]{1,0:T(8,128)(2,1)S(1)} %get-tuple-element.51), channel_id=1, source_target_pairs={{0,2},{1,3},{2,0},{3,1},{4,6},{5,7},{6,4},{7,5},{8,10},{9,11},{10,... | collective-permute-start | bytes 442376 | tf_op jit(solution)/shard_map/ppermute | solution.py:446
  7.2 0.0 collective-permute-start.4
  7.2 1.4 %collective-permute-done.4.read_other_ref = bf16[64,128]{1,0:T(8,128)(2,1)S(1)} collective-permute-done((bf16[64,128]{1,0:T(8,128)(2,1)}, bf16[64,128]{1,0:T(8,128)(2,1)S(1)}, u32[]{:S(2)}, u32[]{:S(2)}) %collective-permute-start.4) | collective-permute-done | bytes 16416 | tf_op jit(solution)/shard_map/ppermute | solution.py:446
  8.6 2.0 %shard_map.150 = (f32[256,1024]{1,0:T(8,128)S(1)}, bf16[256,64]{1,0:T(8,128)(2,1)S(1)}) custom-call(s32[1]{0:T(128)} %bitcast.mine_ref, bf16[256,1024]{1,0:T(8,128)(2,1)S(1)} %get-tuple-element.43.x_ref, bf16[64,256]{1,0:T(8,128)(2,1)S(1)} %get-tuple-element.44.write_ref, bf16[64,128]{1,0:T(8,128)(2,1)} %bitcast.19, ...), custom_call_target="tpu_custom_call" | custom-call | flops 268435456 | bytes 1048576 | tf_op jit(solution)/shard_map/pallas_call | solution.py:497
  10.6 0.7 %collective-permute-done.5.got_ref = bf16[64,1152]{1,0:T(8,128)(2,1)S(1)} collective-permute-done((bf16[64,1152]{1,0:T(8,128)(2,1)S(1)}, bf16[64,1152]{1,0:T(8,128)(2,1)S(1)}, u32[]{:S(2)}, u32[]{:S(2)}) %collective-permute-start.5) | collective-permute-done | bytes 147488 | tf_op jit(solution)/shard_map/ppermute | solution.py:446
  11.4 0.2 shard_map.151
  11.6 1.9 %collective-permute-start.6 = (bf16[64,1152]{1,0:T(8,128)(2,1)S(1)}, bf16[64,1152]{1,0:T(8,128)(2,1)S(1)}, u32[]{:S(2)}, u32[]{:S(2)}) collective-permute-start(bf16[64,1152]{1,0:T(8,128)(2,1)S(1)} %get-tuple-element.55), channel_id=1, source_target_pairs={{0,4},{1,5},{2,6},{3,7},{4,0},{5,1},{6,2},{7,3},{8,12},{9,13},{10,... | collective-permute-start | bytes 442376 | tf_op jit(solution)/shard_map/ppermute | solution.py:446
  13.4 2.2 %shard_map.152.dyn_ref = bf16[2048,1024]{1,0:T(8,128)(2,1)S(1)} custom-call(f32[8,128]{1,0:T(8,128)S(1)} %get-tuple-element.54.token_ref.aux_ref, bf16[2048,1024]{1,0:T(8,128)(2,1)} %refs_0_.2), custom_call_target="tpu_custom_call" | custom-call | bytes 8388608 | tf_op jit(solution)/shard_map/pallas_call | solution.py:512
  15.6 0.0 copy-start
  15.7 1.3 %collective-permute-done.6.got_ref = bf16[64,1152]{1,0:T(8,128)(2,1)S(1)} collective-permute-done((bf16[64,1152]{1,0:T(8,128)(2,1)S(1)}, bf16[64,1152]{1,0:T(8,128)(2,1)S(1)}, u32[]{:S(2)}, u32[]{:S(2)}) %collective-permute-start.6) | collective-permute-done | bytes 147488 | tf_op jit(solution)/shard_map/ppermute | solution.py:446
  17.0 0.2 shard_map.153
  17.2 2.7 %collective-permute-start.7 = (bf16[64,1152]{1,0:T(8,128)(2,1)S(1)}, bf16[64,1152]{1,0:T(8,128)(2,1)S(1)}, u32[]{:S(2)}, u32[]{:S(2)}) collective-permute-start(bf16[64,1152]{1,0:T(8,128)(2,1)S(1)} %get-tuple-element.59), channel_id=1, source_target_pairs={{0,8},{1,9},{2,10},{3,11},{4,12},{5,13},{6,14},{7,15},{8,0},{9,1},... | collective-permute-start | bytes 442376 | tf_op jit(solution)/shard_map/ppermute | solution.py:446
  19.9 2.7 %shard_map.154 = (bf16[1024,2048]{1,0:T(8,128)(2,1)S(1)}, bf16[2048,128]{1,0:T(8,128)(2,1)S(1)}, bf16[128,1024]{1,0:T(8,128)(2,1)S(1)}, bf16[3,128,1024]{2,1,0:T(8,128)(2,1)S(1)}) custom-call(f32[16,128]{1,0:T(8,128)S(1)} %get-tuple-element.58.token_ref.aux_ref, bf16[1024,2048]{1,0:T(8,128)(2,1)} %refs_0_.3, bf16[2048,128]{1,0:T(8,128)(2,1)} %refs_1_.1, ...), custom_call_target="tpu_custom_call" | custom-call | bytes 11534336 | tf_op jit(solution)/shard_map/pallas_call | solution.py:512
  22.6 3.2 %collective-permute-done.7.got_ref = bf16[64,1152]{1,0:T(8,128)(2,1)S(1)} collective-permute-done((bf16[64,1152]{1,0:T(8,128)(2,1)S(1)}, bf16[64,1152]{1,0:T(8,128)(2,1)S(1)}, u32[]{:S(2)}, u32[]{:S(2)}) %collective-permute-start.7) | collective-permute-done | bytes 147488 | tf_op jit(solution)/shard_map/ppermute | solution.py:446
  25.8 0.3 shard_map.155
  26.1 0.0 copy-done
  26.1 1.4 %shard_map.156 = (bf16[256,1024]{1,0:T(8,128)(2,1)S(1)}, bf16[128,1024]{1,0:T(8,128)(2,1)S(1)}, bf16[128,1024]{1,0:T(8,128)(2,1)S(1)}) custom-call(s32[1]{0:T(128)} %bitcast.mine_ref, f32[256,1024]{1,0:T(8,128)S(1)} %get-tuple-element.47.prefix_ref.local_ref, bf16[256,64]{1,0:T(8,128)(2,1)S(1)} %get-tuple-element.48.read_ref, ...), custom_call_target="tpu_custom_call" | custom-call | tf_op jit(solution)/shard_map/pallas_call | solution.py:551
  27.5 19.4 %all_to_all.5 = bf16[16,16,1024]{2,1,0:T(8,128)(2,1)S(1)} all-to-all(bf16[16,16,1024]{2,1,0:T(8,128)(2,1)S(1)} %bitcast.10), channel_id=1, replica_groups=mesh['groups'=2,'seq'=16] {'seq'}, dimensions={0} | all-to-all | bytes 1048576 | tf_op jit(solution)/shard_map/all_to_all | solution.py:568
  46.8 0.1 collective-permute-start.8
  47.0 1.9 %shard_map.157 = (bf16[128,2048]{1,0:T(8,128)(2,1)S(1)}, f32[128,128]{1,0:T(8,128)S(1)}, f32[128,128]{1,0:T(8,128)S(1)}) custom-call(bf16[8,2,16,1024]{3,2,1,0:T(8,128)(2,1)S(1)} %bitcast.9, bf16[128,128]{1,0:T(8,128)(2,1)S(1)} %get-tuple-element.68.perm_ref, bf16[3,128,1024]{2,1,0:T(8,128)(2,1)S(1)} %get-tuple-element.69.noise_ref, ...), custom_call_target="tpu_custom_call" | custom-call | flops 1073741824 | bytes 8388608 | tf_op jit(solution)/shard_map/pallas_call | solution.py:578
  48.9 0.0 collective-permute-done.8.got_ref
  48.9 4.7 %shard_map.158 = (bf16[128,2048]{1,0:T(8,128)(2,1)}, f32[3,128]{1,0:T(4,128)}, bf16[128,2048]{1,0:T(8,128)(2,1)}) custom-call(s32[1]{0:T(128)} %bitcast.mine_ref, bf16[128,1024]{1,0:T(8,128)(2,1)S(1)} %get-tuple-element.63.stay_ref, bf16[128,1024]{1,0:T(8,128)(2,1)S(1)} %collective-permute-done.8.got_ref, ...), custom_call_target="tpu_custom_call" | custom-call | tf_op jit(solution)/shard_map/pallas_call | solution.py:587
  (3 shorter events, 0.0 us)
Async XLA Ops:
  0.6 2.4 %collective-permute-start = (bf16[128,2048]{1,0:T(8,128)(2,1)}, bf16[128,2048]{1,0:T(8,128)(2,1)S(1)}, u32[]{:S(2)}, u32[]{:S(2)}) collective-permute-start(bf16[128,2048]{1,0:T(8,128)(2,1)} %x_hbm.1), channel_id=1, source_target_pairs={{0,1},{1,0},{2,3},{3,2},{4,5},{5,4},{6,7},{7,6},{8,9},{9,8},{10,11... | collective-permute-start | bytes 1572872 | tf_op jit(solution)/shard_map/ppermute | solution.py:446
  1.2 1.8 %collective-permute-start.1 = (bf16[64,128]{1,0:T(8,128)(2,1)}, bf16[64,128]{1,0:T(8,128)(2,1)S(1)}, u32[]{:S(2)}, u32[]{:S(2)}) collective-permute-start(bf16[64,128]{1,0:T(8,128)(2,1)} %bitcast.12), channel_id=1, source_target_pairs={{0,1},{1,0},{2,3},{3,2},{4,5},{5,4},{6,7},{7,6},{8,9},{9,8},{10,11... | collective-permute-start | bytes 49160 | tf_op jit(solution)/shard_map/ppermute | solution.py:446
  1.3 1.7 %collective-permute-start.2 = (f32[32,128]{1,0:T(8,128)}, f32[32,128]{1,0:T(8,128)S(1)}, u32[]{:S(2)}, u32[]{:S(2)}) collective-permute-start(f32[32,128]{1,0:T(8,128)} %bitcast.14), channel_id=1, source_target_pairs={{0,1},{1,0},{2,3},{3,2},{4,5},{5,4},{6,7},{7,6},{8,9},{9,8},{10,11... | collective-permute-start | bytes 49160 | tf_op jit(solution)/shard_map/ppermute | solution.py:446
  1.7 1.3 %collective-permute-start.3 = (s32[1,128]{1,0:T(1,128)}, s32[1,128]{1,0:T(1,128)S(1)}, u32[]{:S(2)}, u32[]{:S(2)}) collective-permute-start(s32[1,128]{1,0:T(1,128)} %bitcast.16), channel_id=1, source_target_pairs={{0,1},{1,0},{2,3},{3,2},{4,5},{5,4},{6,7},{7,6},{8,9},{9,8},{10,11... | collective-permute-start | bytes 1544 | tf_op jit(solution)/shard_map/ppermute | solution.py:446
  4.3 7.1 %collective-permute-start.5 = (bf16[64,1152]{1,0:T(8,128)(2,1)S(1)}, bf16[64,1152]{1,0:T(8,128)(2,1)S(1)}, u32[]{:S(2)}, u32[]{:S(2)}) collective-permute-start(bf16[64,1152]{1,0:T(8,128)(2,1)S(1)} %get-tuple-element.51), channel_id=1, source_target_pairs={{0,2},{1,3},{2,0},{3,1},{4,6},{5,7},{6,4},{7,5},{8,10},{9,11},{10,... | collective-permute-start | bytes 442376 | tf_op jit(solution)/shard_map/ppermute | solution.py:446
  7.2 1.4 %collective-permute-start.4 = (bf16[64,128]{1,0:T(8,128)(2,1)}, bf16[64,128]{1,0:T(8,128)(2,1)S(1)}, u32[]{:S(2)}, u32[]{:S(2)}) collective-permute-start(bf16[64,128]{1,0:T(8,128)(2,1)} %bitcast.18), channel_id=1, source_target_pairs={{0,1},{1,0},{2,3},{3,2},{4,5},{5,4},{6,7},{7,6},{8,9},{9,8},{10,11... | collective-permute-start | bytes 49160 | tf_op jit(solution)/shard_map/ppermute | solution.py:446
  11.6 5.4 %collective-permute-start.6 = (bf16[64,1152]{1,0:T(8,128)(2,1)S(1)}, bf16[64,1152]{1,0:T(8,128)(2,1)S(1)}, u32[]{:S(2)}, u32[]{:S(2)}) collective-permute-start(bf16[64,1152]{1,0:T(8,128)(2,1)S(1)} %get-tuple-element.55), channel_id=1, source_target_pairs={{0,4},{1,5},{2,6},{3,7},{4,0},{5,1},{6,2},{7,3},{8,12},{9,13},{10,... | collective-permute-start | bytes 442376 | tf_op jit(solution)/shard_map/ppermute | solution.py:446
  15.6 10.4 %copy-start = (f32[2048]{0:T(1024)S(1)}, f32[2048]{0:T(1024)}, u32[]{:S(2)}) copy-start(f32[2048]{0:T(1024)} %param.18) | copy-start | bytes 24580
  17.2 8.6 %collective-permute-start.7 = (bf16[64,1152]{1,0:T(8,128)(2,1)S(1)}, bf16[64,1152]{1,0:T(8,128)(2,1)S(1)}, u32[]{:S(2)}, u32[]{:S(2)}) collective-permute-start(bf16[64,1152]{1,0:T(8,128)(2,1)S(1)} %get-tuple-element.59), channel_id=1, source_target_pairs={{0,8},{1,9},{2,10},{3,11},{4,12},{5,13},{6,14},{7,15},{8,0},{9,1},... | collective-permute-start | bytes 442376 | tf_op jit(solution)/shard_map/ppermute | solution.py:446
  19.9 27.1 %copy-start.1 = (bf16[1024]{0:T(1024)(128)(2,1)S(1)}, bf16[1024]{0:T(1024)(128)(2,1)}, u32[]{:S(2)}) copy-start(bf16[1024]{0:T(1024)(128)(2,1)} %param.25) | copy-start | bytes 6148
  46.8 2.1 %collective-permute-start.8 = (bf16[128,1024]{1,0:T(8,128)(2,1)S(1)}, bf16[128,1024]{1,0:T(8,128)(2,1)S(1)}, u32[]{:S(2)}, u32[]{:S(2)}) collective-permute-start(bf16[128,1024]{1,0:T(8,128)(2,1)S(1)} %get-tuple-element.66), channel_id=1, source_target_pairs={{0,1},{1,0},{2,3},{3,2},{4,5},{5,4},{6,7},{7,6},{8,9},{9,8},{10,11... | collective-permute-start | bytes 786440 | tf_op jit(solution)/shard_map/ppermute | solution.py:446
